TPU v7x, 256 devices: a whole 4x4x8 slice. The times are simulated.
256 devices in a mesh: cells: 64 (over x, z, core), vecs: 4 (over y).
Axes of the slice: x: 4, y: 4, z: 8, core: 2. Of those that a mesh axis runs over, the one named last changes fastest.
Arguments:
- wave_block: float32 [64, 589824], P('vecs', 'cells'), may hold values from -6 to 6
- connectivity: int32 [125, 8192], P(None, 'cells'), may hold values from 0 to 10304, as said below
- send_list: int32 [69696], P('cells'), may hold values from 0 to 9215, as said below
- levels: int32 [8192], P('cells'), may hold values from 0 to 2
- live_cells: int32 [64], P('cells'), may hold values from 64 to 128, as said below
- potential: float32 [125, 8192], P(None, 'cells'), may hold values from -24 to 8
- mass_scale: float32 [589824], P('cells'), may hold values from 0.5 to 2
- center: float32 [], replicated, may hold values from 20 to 30
- halfwidth: float32 [], replicated, may hold values from 25 to 35
- earlier_vectors: bfloat16 [2048, 589824], P(None, ('cells', 'vecs')), may hold values from -0.0078125 to 0.0078125
Outputs:
- filtered: float32 [64, 589824], P(None, ('cells', 'vecs'))
- projections: float32 [2048, 64], P(('cells', 'vecs'))
Inputs may be any that keep to these rules, and one draw needn't show every extreme that they name: `connectivity`: column c names the slots of cell c's 125 nodes on its device, node (a,b,c) of the reference cube at row 25 a + 5 b + c. A device's cells form a structured block of 8 x 8 x 2 cells of degree 4 in Morton order, nodes numbered at random over the 9216 node slots; the face of the block toward the device before it lies in the ghost slots 9216 to 10304 in the order of that device's send_list, so that exactly 64 cells of each device name ghost slots. `send_list`: A device's 1089 entries are distinct node slots of its block's face toward the device after it. Cells 0 to live_cells - 1 of a device are in use, the rest of its slots are empty; some device uses all 128, some only 64.
All inputs are finite; a program needn't handle non-finite values.
Results may differ from a plain program's by a relative error of at most 0.0031.
Values may be sent and summed in bfloat16 or wider, within the bound.
No kernel may reach another device: no remote copies, remote signals or barrier semaphores. Data moves between devices by JAX's collectives and lax.ppermute only.
A program may use at most 128 MiB of HBM per device.

v0:
```python
import math

import jax
import jax.numpy as jnp
import numpy as np
from jax import lax
from jax.sharding import PartitionSpec as P


def passed_along(value, axis, steps):
    count = lax.axis_size(axis)
    leading, last = (max(0, -steps), min(count, count - steps))
    return lax.ppermute(value, axis, [(source, source + steps) for source in range(leading, last)])


def gll_tables():
    root_value = math.sqrt(3.0 / 7.0)
    points = np.array([-1.0, -root_value, 0.0, root_value, 1.0])
    weights = np.array([0.1, 49.0 / 90.0, 32.0 / 45.0, 49.0 / 90.0, 0.1])
    barycentric = np.ones(5)
    for node_index in range(5):
        for other_node in range(5):
            if other_node != node_index:
                barycentric[node_index] = barycentric[node_index] / (
                    points[node_index] - points[other_node]
                )
    derivative = np.zeros((5, 5))
    for row_index in range(5):
        for col_index in range(5):
            if row_index != col_index:
                derivative[row_index, col_index] = (
                    barycentric[col_index]
                    / barycentric[row_index]
                    / (points[row_index] - points[col_index])
                )
        derivative[row_index, row_index] = -np.sum(derivative[row_index])
    mass_one = np.zeros((5, 5))
    for node_index in range(5):
        mass_one[node_index, node_index] = weights[node_index]
    laplace_one = derivative.T @ mass_one @ derivative
    stiffness = (
        np.kron(np.kron(laplace_one, mass_one), mass_one)
        + np.kron(np.kron(mass_one, laplace_one), mass_one)
        + np.kron(np.kron(mass_one, mass_one), laplace_one)
    )
    quadrature = np.kron(np.kron(weights, weights), weights)
    return (stiffness.astype(np.float32), quadrature.astype(np.float32))


def per_device(
    wave_block,
    connectivity,
    send_list,
    levels,
    live_cells,
    potential,
    mass_scale,
    center,
    halfwidth,
    earlier_vectors,
):
    stiffness, quadrature = gll_tables()
    stiffness_low = jnp.asarray(stiffness).astype(jnp.bfloat16)
    quad_weights = jnp.asarray(quadrature).astype(jnp.float32)
    columns = wave_block.shape[0]
    owned_count = wave_block.shape[1]
    ghost_count = send_list.shape[0]
    cell_count = connectivity.shape[1]
    cell_size = jnp.exp2(-levels.astype(jnp.float32))
    in_use = (jnp.arange(cell_count, dtype=jnp.int32) < live_cells[0]).astype(jnp.float32)
    kinetic = cell_size / 4.0 * in_use
    volume = cell_size**3 / 8.0 * in_use
    coefficient = volume[None, :] * quad_weights[:, None] * potential

    def cell_sum(extended, cells_conn, kin_part, coeff_part):
        values = extended[:, cells_conn].astype(jnp.bfloat16)
        stiff_part = jnp.einsum(
            "jk,vkc->vjc", stiffness_low, values, preferred_element_type=jnp.float32
        )
        cell_terms = kin_part[None, None, :] * stiff_part + coeff_part[None] * values.astype(
            jnp.float32
        )
        return (
            jnp.zeros((columns, owned_count + ghost_count), jnp.float32)
            .at[:, cells_conn]
            .add(cell_terms)
        )

    def apply_operator(vectors):
        scaled = vectors * mass_scale[None, :]
        top_face = scaled[:, send_list]
        ghosts = passed_along(top_face.astype(jnp.bfloat16), "cells", 1).astype(top_face.dtype)
        extended = jnp.concatenate([scaled, ghosts], 1)
        slot_sums = cell_sum(extended, connectivity, kinetic, coefficient)
        returned = passed_along(
            slot_sums[:, owned_count:].astype(jnp.bfloat16), "cells", -1
        ).astype(jnp.float32)
        summed = slot_sums[:, :owned_count].at[:, send_list].add(returned)
        return summed * mass_scale[None, :]

    degree_one = (apply_operator(wave_block) - center * wave_block) / halfwidth
    degree_two = 2.0 * (apply_operator(degree_one) - center * degree_one) / halfwidth - wave_block
    rounded = degree_two.astype(jnp.bfloat16)
    quarter = lax.all_to_all(rounded, "vecs", split_axis=1, concat_axis=0, tiled=True)
    row_share = earlier_vectors.shape[0] // lax.axis_size(("cells", "vecs"))
    partial_sum = lax.dot_general(
        earlier_vectors, quarter, (((1,), (1,)), ((), ())), preferred_element_type=jnp.float32
    )
    projections = lax.psum(partial_sum, ("cells", "vecs"))
    filtered = quarter.astype(jnp.float32) - lax.dot_general(
        projections.astype(jnp.bfloat16),
        earlier_vectors,
        (((0,), (0,)), ((), ())),
        preferred_element_type=jnp.float32,
    )
    own_rows = lax.dynamic_slice_in_dim(
        projections, lax.axis_index(("cells", "vecs")) * row_share, row_share, 0
    )
    return (filtered, own_rows)


def solution(mesh):
    in_specs = (
        P("vecs", "cells"),
        P(None, "cells"),
        P("cells"),
        P("cells"),
        P("cells"),
        P(None, "cells"),
        P("cells"),
        P(),
        P(),
        P(None, ("cells", "vecs")),
    )
    out_specs = (P(None, ("cells", "vecs")), P(("cells", "vecs"), None))
    return jax.shard_map(
        per_device, mesh=mesh, in_specs=in_specs, out_specs=out_specs, check_vma=False
    )
```

profile of v0, /device:TPU:1, one launch (start us, length us, event | category | flops | bytes accessed | tf_op | source)
XLA Modules:
  0.0 647.3 jit_solution(2964414800948179650)
XLA Ops:
  7.2 0.7 compare_select_fusion.1
  7.9 1.1 broadcast_multiply_fusion.1
  9.0 1.1 copy.91
  10.2 2.9 gather_fusion
  13.2 4.9 collective-permute-start
  18.2 0.9 fusion.19
  19.7 0.7 compare_select_fusion.3
  20.3 0.9 multiply_multiply_fusion
  21.4 2.1 copy.93
  23.6 32.9 %gather_fusion.1 = bf16[16000,16]{1,0:T(8,128)(2,1)} fusion(bf16[16,10305]{0,1:T(8,128)(2,1)S(1)} %copy.93, s32[16384]{0:T(1024)S(1)} %pad_clamp_fusion), kind=kCustom, calls=%fused_computation.1 | custom fusion | bytes 1088000 | tf_op jit(solution)/shard_map/gather | solution.py:76
  56.5 3.7 copy.94
  60.2 0.3 reshape.88
  60.5 0.3 copy.95
  60.8 0.3 fusion.9
  61.1 7.5 %copy.110 = f32[125,128,16]{2,1,0:T(8,128)} copy(f32[125,128,16]{0,1,2:T(8,128)S(1)} %fusion.9) | data formatting | bytes 2048000 | tf_op jit(solution)/shard_map/add | solution.py:80
  68.6 90.6 %scatter_custom_fusion = f32[16,10305]{0,1:T(8,128)} fusion(s32[16000]{0:T(1024)S(1)} %fusion.19, f32[16000,16]{1,0:T(8,128)} %bitcast.60, f32[]{:T(128)} %constant.16.clone.1), kind=kCustom, calls=%fused_computation.11 | custom fusion | flops 256000 | bytes 660032 | tf_op jit(solution)/shard_map/scatter-add | solution.py:86
  159.3 1.1 slice.33
  160.4 1.9 collective-permute-start.1
  163.6 3.9 slice.26
  167.6 0.7 collective-permute-done.1
  168.3 13.8 %scatter_custom_fusion.1 = f32[16,9216]{0,1:T(8,128)} fusion(f32[16,9216]{0,1:T(8,128)} %slice.26, s32[1089]{0:T(1024)S(1)} %compare_select_fusion.1, bf16[16,1089]{0,1:T(8,128)(2,1)S(1)} %collective-permute-done.1), kind=kCustom, calls=%fused_computation.30 | custom fusion | flops 34848 | bytes 870400 | tf_op jit(solution)/shard_map/scatter-add | solution.py:98
  182.0 3.0 copy.99
  185.2 1.9 copy.100
  187.1 4.4 gather_fusion.2
  191.7 3.0 collective-permute-start.2
  194.7 1.0 collective-permute-done.2
  195.7 0.7 pad_maximum_fusion.1
  196.5 2.7 copy.102
  199.2 32.9 %gather_fusion.3 = bf16[16000,16]{1,0:T(8,128)(2,1)} fusion(bf16[16,10305]{0,1:T(8,128)(2,1)S(1)} %copy.102, s32[16384]{0:T(1024)S(1)} %pad_clamp_fusion), kind=kCustom, calls=%fused_computation.3 | custom fusion | bytes 1088000 | tf_op jit(solution)/shard_map/gather | solution.py:76
  232.1 3.7 copy.103
  235.8 0.3 reshape.89
  236.1 0.3 copy.104
  236.4 0.3 fusion.6
  236.8 7.5 %copy.111 = f32[125,128,16]{2,1,0:T(8,128)} copy(f32[125,128,16]{0,1,2:T(8,128)S(1)} %fusion.6) | data formatting | bytes 2048000 | tf_op jit(solution)/shard_map/add | solution.py:80
  244.3 90.6 %scatter_custom_fusion.2 = f32[16,10305]{0,1:T(8,128)} fusion(s32[16000]{0:T(1024)S(1)} %fusion.19, f32[16000,16]{1,0:T(8,128)} %bitcast.59, f32[]{:T(128)} %constant.16.clone.1), kind=kCustom, calls=%fused_computation.9 | custom fusion | flops 256000 | bytes 660032 | tf_op jit(solution)/shard_map/scatter-add | solution.py:86
  334.9 1.1 slice.32
  336.0 1.9 collective-permute-start.3
  337.9 3.9 slice.28
  341.9 2.6 collective-permute-done.3
  344.5 13.8 %scatter_custom_fusion.3 = f32[16,9216]{0,1:T(8,128)} fusion(f32[16,9216]{0,1:T(8,128)} %slice.28, s32[1089]{0:T(1024)S(1)} %compare_select_fusion.1, bf16[16,1089]{0,1:T(8,128)(2,1)S(1)} %collective-permute-done.3), kind=kCustom, calls=%fused_computation.28 | custom fusion | flops 34848 | bytes 870400 | tf_op jit(solution)/shard_map/scatter-add | solution.py:98
  358.3 3.0 copy.107
  361.3 0.2 subtract_convert_fusion
  361.6 9.7 %all_to_all.19 = bf16[16,4,2304]{2,0,1:T(8,128)(2,1)S(1)} all-to-all(bf16[16,4,2304]{2,0,1:T(8,128)(2,1)S(1)} %bitcast.63), channel_id=1, replica_groups=mesh['cells'=64,'vecs'=4] {'vecs'}, dimensions={1} | all-to-all | bytes 589824 | tf_op jit(solution)/shard_map/all_to_all | solution.py:104
  371.2 7.4 %convolution_bitcast_fusion = f32[2048,64]{0,1:T(8,128)} fusion(bf16[64,2304]{1,0:T(8,128)(2,1)S(1)} %bitcast.61, bf16[2048,2304]{1,0:T(8,128)(2,1)} %param.21), kind=kOutput, calls=%fused_computation.13 | convolution fusion | flops 603979776 | bytes 10256384 | tf_op jit(solution)/shard_map/dot_general | solution.py:106
  378.7 253.8 %all-reduce.2.cloned.1.call-done = f32[2048,64]{0,1:T(8,128)} async-done(((f32[2048,64]{0,1:T(8,128)}), f32[2048,64]{0,1:T(8,128)}) %all-reduce.2.cloned.1.call-update) | async-done | bytes 524304 | tf_op jit(solution)/shard_map/psum | solution.py:109
  632.5 0.8 constant_dynamic-slice_fusion
  633.3 0.7 copy.109
  634.0 6.4 convolution_subtract_fusion
  (21 shorter events, 0.7 us)
Async XLA Ops:
  7.2 625.3 %all-reduce.2.cloned.1.call-start = ((), (), s32[]{:S(2)}) async-start(), calls=%async_computation.1 | async-start | bytes 1048576 | tf_op jit(solution)/shard_map/psum | solution.py:109
  13.2 8.2 %collective-permute-start = (bf16[16,1089]{1,0:T(8,128)(2,1)S(1)}, bf16[16,1089]{1,0:T(8,128)(2,1)S(1)}, u32[]{:S(2)}, u32[]{:S(2)}) collective-permute-start(bf16[16,1089]{1,0:T(8,128)(2,1)S(1)} %bitcast.65), channel_id=1, source_target_pairs={{0,4},{4,8},{8,12},{12,16},{16,20},{20,24},{24,28},{28,32},{32,36}... | collective-permute-start | bytes 104552 | tf_op jit(solution)/shard_map/ppermute | solution.py:13
  23.5 37.2 %copy-start.4 = (bf16[125,125,1]{1,0,2:T(8,128)(2,1)S(1)}, bf16[125,125,1]{1,0,2:T(8,128)(2,1)}, u32[]{:S(2)}) copy-start(bf16[125,125,1]{1,0,2:T(8,128)(2,1)} %constant.46) | copy-start | bytes 93754
  160.4 7.9 %collective-permute-start.1 = (bf16[16,1089]{0,1:T(8,128)(2,1)S(1)}, bf16[16,1089]{0,1:T(8,128)(2,1)S(1)}, u32[]{:S(2)}, u32[]{:S(2)}) collective-permute-start(bf16[16,1089]{0,1:T(8,128)(2,1)S(1)} %slice.33), channel_id=1, source_target_pairs={{4,0},{8,4},{12,8},{16,12},{20,16},{24,20},{28,24},{32,28},{36,32}... | collective-permute-start | bytes 104552 | tf_op jit(solution)/shard_map/ppermute | solution.py:13
  167.5 17.5 %copy-start = (f32[16,9216]{1,0:T(8,128)S(1)}, f32[16,9216]{1,0:T(8,128)}, u32[]{:S(2)}) copy-start(f32[16,9216]{1,0:T(8,128)} %param.12) | copy-start | bytes 1769476
  167.5 17.5 %copy-start.3 = (f32[9216]{0:T(1024)S(1)}, f32[9216]{0:T(1024)}, u32[]{:S(2)}) copy-start(f32[9216]{0:T(1024)} %param.18) | copy-start | bytes 110596
  185.1 10.7 %copy-start.1 = (f32[16,9216]{1,0:T(8,128)}, f32[16,9216]{1,0:T(8,128)S(1)}, u32[]{:S(2)}) copy-start(f32[16,9216]{1,0:T(8,128)S(1)} %copy.99) | copy-start | bytes 1769476
  191.7 4.1 collective-permute-start.2
  336.0 8.5 %collective-permute-start.3 = (bf16[16,1089]{0,1:T(8,128)(2,1)S(1)}, bf16[16,1089]{0,1:T(8,128)(2,1)S(1)}, u32[]{:S(2)}, u32[]{:S(2)}) collective-permute-start(bf16[16,1089]{0,1:T(8,128)(2,1)S(1)} %slice.32), channel_id=1, source_target_pairs={{4,0},{8,4},{12,8},{16,12},{20,16},{24,20},{28,24},{32,28},{36,32}... | collective-permute-start | bytes 104552 | tf_op jit(solution)/shard_map/ppermute | solution.py:13
  341.9 19.4 %copy-start.2 = (f32[16,9216]{1,0:T(8,128)S(1)}, f32[16,9216]{1,0:T(8,128)}, u32[]{:S(2)}) copy-start(f32[16,9216]{1,0:T(8,128)} %copy-done.1) | copy-start | bytes 1769476
Sparse Core Ops, SparseCore 0:
  378.8 253.6 all-reduce.1
where the time goes:
time: 649 us; the launch traced here: 647 us
  waiting for transfers between devices  258 us (40%)
  other arithmetic  214 us (33%)
  local copies, waits for them, and re-layouts  123 us (19%)
  between operations  16.2 us (2%)
  matrix products  14.4 us (2%)
  starting transfers between devices  11.8 us (2%)
  blocking collectives  9.69 us (1%)
    psum x1, waiting for transfers between devices, per_device(): projections = lax.psum(partial_sum, ('cells', 'vecs'))  254 us
    scatter-add x2, other arithmetic, cell_sum(): return jnp.zeros((columns, owned_count + ghost_count), jnp.float32).at[:,...  181 us
    gather x4, local copies, waits for them, and re-layouts, cell_sum(): values = extended[:, cells_conn].astype(jnp.bfloat16)  73.2 us
    scatter-add x2, other arithmetic, apply_operator(): summed = slot_sums[:, :owned_count].at[:, send_list].add(returned)  27.5 us
    add x2, local copies, waits for them, and re-layouts, cell_sum(): kin_part[None, None, :] * stiff_part  15.1 us
  transfers between devices with their start and end apart: 5, of which 4 were waited for; matrix products, arithmetic and copies ran while one was open for 2% of the time, Pallas kernels for 0%

commit v1 on v0

v1 whole, which is shorter than its diff:
```python
import math

import jax
import jax.numpy as jnp
import numpy as np
from jax import lax
from jax.experimental import pallas as pl
from jax.experimental.pallas import tpu as pltpu
from jax.sharding import PartitionSpec as P

F32, BF16, I32 = jnp.float32, jnp.bfloat16, jnp.int32
AXES = ("cells", "vecs")
LANES = 128
VMEM_LIMIT = 48 * 2**20


def gll_tables():
    root_value = math.sqrt(3.0 / 7.0)
    points = np.array([-1.0, -root_value, 0.0, root_value, 1.0])
    weights = np.array([0.1, 49.0 / 90.0, 32.0 / 45.0, 49.0 / 90.0, 0.1])
    barycentric = np.ones(5)
    for node_index in range(5):
        for other_node in range(5):
            if other_node != node_index:
                barycentric[node_index] = barycentric[node_index] / (
                    points[node_index] - points[other_node]
                )
    derivative = np.zeros((5, 5))
    for row_index in range(5):
        for col_index in range(5):
            if row_index != col_index:
                derivative[row_index, col_index] = (
                    barycentric[col_index]
                    / barycentric[row_index]
                    / (points[row_index] - points[col_index])
                )
        derivative[row_index, row_index] = -np.sum(derivative[row_index])
    mass_one = np.zeros((5, 5))
    for node_index in range(5):
        mass_one[node_index, node_index] = weights[node_index]
    laplace_one = derivative.T @ mass_one @ derivative
    stiffness = (
        np.kron(np.kron(laplace_one, mass_one), mass_one)
        + np.kron(np.kron(mass_one, laplace_one), mass_one)
        + np.kron(np.kron(mass_one, mass_one), laplace_one)
    )
    quadrature = np.kron(np.kron(weights, weights), weights)
    return (stiffness.astype(np.float32), quadrature.astype(np.float32))


STIFFNESS, QUADRATURE = gll_tables()
STIFFNESS = STIFFNESS.astype(jnp.bfloat16).astype(np.float32)


def node(a, b, c):
    return 25 * a + 5 * b + c


def lane_index(rows):
    return lax.broadcasted_iota(I32, (rows, LANES), 1)


def axis_bits(lane, axis):
    return [(lane >> bit) & 1 for bit in ((0, 3, 5), (1, 4, 6))[axis]]


def axis_place(lane, axis):
    low, mid, high = axis_bits(lane, axis)
    return low + 2 * mid + 4 * high


def below_of(lane, axis):
    low, mid, high = axis_bits(lane, axis)
    scale = 1 + axis
    step = jnp.where(low == 1, 1, jnp.where(mid == 1, 7, 23)) * scale
    first = axis_place(lane, axis) == 0
    return jnp.where(first, lane, lane - step), jnp.logical_not(first)


def above_of(lane, axis):
    low, mid, high = axis_bits(lane, axis)
    scale = 1 + axis
    step = jnp.where(low == 0, 1, jnp.where(mid == 0, 7, 23)) * scale
    last = axis_place(lane, axis) == 7
    return jnp.where(last, lane, lane + step), jnp.logical_not(last)


def pick(values, index):
    return jnp.take_along_axis(values, index, axis=1)


def up_layer(values):
    return pltpu.roll(values, 4, 1)


def down_layer(values):
    return pltpu.roll(values, LANES - 4, 1)


def row_groups(values, group):
    return values.shape[0] // group


def split_low(values):
    high = values.astype(BF16)
    return high, (values - high.astype(F32)).astype(BF16)


def gather_kernel(vectors, conn_ref, wave_ref, mass_ref, wave_out, mass_out, face_out, table):
    groups = wave_ref.shape[1] // 256
    rows = vectors * groups
    high, low = split_low(wave_ref[...])
    for h in range(groups):
        table[vectors * h : vectors * (h + 1), 0:256] = high[:, 256 * h : 256 * (h + 1)]
        table[vectors * h : vectors * (h + 1), 256:512] = low[:, 256 * h : 256 * (h + 1)]
    mass_high, mass_low = split_low(mass_ref[...])
    table[rows : rows + groups, 0:256] = mass_high
    table[rows : rows + groups, 256:512] = mass_low
    width = 4 * LANES
    place = lax.broadcasted_iota(I32, (256, width), 0).astype(F32).astype(BF16)
    group_row = lax.broadcasted_iota(I32, (groups, width), 0)

    def one(ab, carry):
        slots = jnp.concatenate([conn_ref[pl.ds(5 * ab + c, 1), :] for c in range(1, 5)], 1)
        within = jnp.broadcast_to((slots & 255).astype(F32).astype(BF16), (256, width))
        chosen = jnp.where(place == within, BF16(1), BF16(0))
        found = jnp.dot(
            table[...], jnp.concatenate([chosen, chosen], 0), preferred_element_type=F32
        )
        group = slots >> 8
        wide = jnp.broadcast_to(group, (vectors, width))
        total = jnp.zeros((vectors, width), F32)
        for h in range(groups):
            total = jnp.where(wide == h, found[vectors * h : vectors * (h + 1)], total)
        mass = jnp.sum(
            jnp.where(
                group_row == jnp.broadcast_to(group, (groups, width)),
                found[rows : rows + groups],
                0.0,
            ),
            0,
            keepdims=True,
        )
        for c in range(1, 5):
            wave_out[5 * ab + c] = total[:, LANES * (c - 1) : LANES * c]
            mass_out[pl.ds(5 * ab + c, 1), :] = mass[:, LANES * (c - 1) : LANES * c]
        return carry

    lax.fori_loop(0, 25, one, 0, unroll=5)
    upper = (lane_index(vectors) >> 2) & 1 == 1
    upper_one = (lane_index(1) >> 2) & 1 == 1
    for i in range(13):
        first = wave_out[5 * (2 * i) + 4]
        first_mass = mass_out[5 * (2 * i) + 4 : 5 * (2 * i) + 5, :]
        second, second_mass = first, first_mass
        if i < 12:
            second = wave_out[5 * (2 * i + 1) + 4]
            second_mass = mass_out[5 * (2 * i + 1) + 4 : 5 * (2 * i + 1) + 5, :]
        face_out[i, 0:vectors, :] = jnp.where(upper, first, down_layer(second))
        packed = jnp.where(upper_one, first_mass, down_layer(second_mass))
        face_out[i, vectors : vectors + 8, :] = jnp.broadcast_to(packed, (8, LANES))


def apply_cells(values, terms, potential_ref, levels_ref, live_ref, vectors):
    lane = lane_index(1)
    size = jnp.exp2(-levels_ref[...].astype(F32))
    in_use = jnp.where(lane < live_ref[0], 1.0, 0.0).astype(F32)
    kinetic_row = size / 4.0 * in_use
    volume_row = size * size * size / 8.0 * in_use
    kinetic = jnp.broadcast_to(kinetic_row, (8, LANES))

    def one(t, carry):
        part = pl.ds(pl.multiple_of(8 * t, 8), 8)
        for j in range(125):
            total = None
            for k in np.flatnonzero(STIFFNESS[j]):
                term = values[int(k), part, :] * float(STIFFNESS[j, k])
                total = term if total is None else total + term
            weight = volume_row * float(QUADRATURE[j]) * potential_ref[j : j + 1, :]
            weight = jnp.broadcast_to(weight, (8, LANES))
            terms[j, part, :] = kinetic * total + weight * values[j, part, :]
        return carry

    lax.fori_loop(0, vectors // 8, one, 0)


def join_cells(terms, vectors):
    lane = lane_index(8)
    upper = (lane >> 2) & 1 == 1

    def one(t, carry):
        part = pl.ds(pl.multiple_of(8 * t, 8), 8)
        for axis in range(2):
            before, has_before = below_of(lane, axis)
            after, has_after = above_of(lane, axis)
            for other in range(5):
                for c in range(5):
                    start = node(0, other, c) if axis == 0 else node(other, 0, c)
                    end = node(4, other, c) if axis == 0 else node(other, 4, c)
                    first, last = terms[start, part, :], terms[end, part, :]
                    joined = first + jnp.where(has_before, pick(last, before), 0.0)
                    terms[start, part, :] = joined
                    terms[end, part, :] = jnp.where(has_after, pick(joined, after), last)
        for ab in range(25):
            first, last = terms[5 * ab, part, :], terms[5 * ab + 4, part, :]
            joined = first + jnp.where(upper, up_layer(last), 0.0)
            terms[5 * ab, part, :] = joined
            terms[5 * ab + 4, part, :] = jnp.where(upper, last, down_layer(joined))
        return carry

    lax.fori_loop(0, vectors // 8, one, 0)


def pack_lower(terms, face_out, vectors):
    upper = (lane_index(vectors) >> 2) & 1 == 1
    for i in range(13):
        first = terms[5 * (2 * i)]
        second = terms[5 * (2 * i + 1)] if i < 12 else first
        face_out[i] = jnp.where(upper, up_layer(second), first).astype(BF16)


def pack_upper(terms, face_out, vectors):
    upper = (lane_index(vectors) >> 2) & 1 == 1
    for i in range(13):
        first = terms[5 * (2 * i) + 4]
        second = terms[5 * (2 * i + 1) + 4] if i < 12 else first
        face_out[i] = jnp.where(upper, first, down_layer(second)).astype(BF16)


def from_below(packed, ab):
    return packed if ab % 2 == 1 else down_layer(packed)


def from_above(packed, ab):
    return packed if ab % 2 == 1 else up_layer(packed)


def first_kernel(
    vectors, wave_ref, mass_ref, ghost_ref, potential_ref, levels_ref, live_ref,
    terms, low_wave, low_mass, face_down, face_up, values,
):
    upper = (lane_index(vectors) >> 2) & 1 == 1
    upper_one = (lane_index(1) >> 2) & 1 == 1
    for ab in range(25):
        packed = ghost_ref[ab // 2]
        wave = jnp.where(
            upper, up_layer(wave_ref[5 * ab + 4]), from_below(packed[0:vectors], ab)
        )
        mass = jnp.where(
            upper_one,
            up_layer(mass_ref[5 * ab + 4 : 5 * ab + 5, :]),
            from_below(packed[vectors : vectors + 1], ab),
        )
        low_wave[ab] = wave
        low_mass[ab : ab + 1, :] = mass
        values[5 * ab] = (wave * mass).astype(BF16).astype(F32)
        for c in range(1, 5):
            j = 5 * ab + c
            values[j] = (wave_ref[j] * mass_ref[j : j + 1, :]).astype(BF16).astype(F32)
    apply_cells(values, terms, potential_ref, levels_ref, live_ref, vectors)
    join_cells(terms, vectors)
    pack_lower(terms, face_down, vectors)
    pack_upper(terms, face_up, vectors)


def second_kernel(
    vectors, sums_ref, wave_ref, mass_ref, low_wave, low_mass, above_ref, below_ref,
    potential_ref, levels_ref, live_ref, scalars_ref, result, face_down, values, terms,
):
    upper = (lane_index(vectors) >> 2) & 1 == 1
    center, inverse = scalars_ref[0], scalars_ref[1]
    for ab in range(25):
        for c in range(5):
            j = 5 * ab + c
            total = sums_ref[j]
            if c == 0:
                below = from_below(below_ref[ab // 2].astype(F32), ab)
                total = total + jnp.where(upper, 0.0, below)
                wave, mass = low_wave[ab], low_mass[ab : ab + 1, :]
            else:
                wave, mass = wave_ref[j], mass_ref[j : j + 1, :]
            if c == 4:
                above = from_above(above_ref[ab // 2].astype(F32), ab)
                total = total + jnp.where(upper, above, 0.0)
            one = (mass * total - center * wave) * inverse
            values[j] = (one * mass).astype(BF16).astype(F32)
            result[j] = -2.0 * center * inverse * one - wave
    apply_cells(values, terms, potential_ref, levels_ref, live_ref, vectors)
    join_cells(terms, vectors)
    pack_lower(terms, face_down, vectors)
    for ab in range(25):
        for c in range(1, 5):
            j = 5 * ab + c
            result[j] = result[j] + (2.0 * inverse) * mass_ref[j : j + 1, :] * terms[j]


def scatter_kernel(
    vectors, conn_ref, result_ref, mass_ref, above_ref, wave_ref, scalars_ref, out_ref, total
):
    groups = wave_ref.shape[1] // 256
    rows = vectors * groups
    center, inverse = scalars_ref[0], scalars_ref[1]
    width = 4 * LANES
    place = lax.broadcasted_iota(I32, (256, width), 0).astype(F32).astype(BF16)
    group_row = lax.broadcasted_iota(I32, (groups, width), 0)
    lane = lane_index(1)
    last_x, last_y = axis_place(lane, 0) == 7, axis_place(lane, 1) == 7
    upper = (lane_index(vectors) >> 2) & 1 == 1
    total[...] = jnp.zeros_like(total)
    for ab in range(25):
        keep = None
        if ab // 5 == 4:
            keep = last_x
        if ab % 5 == 4:
            keep = last_y if keep is None else jnp.logical_and(keep, last_y)
        pieces, slots = [], []
        for c in range(1, 5):
            j = 5 * ab + c
            value = result_ref[j]
            if c == 4:
                above = from_above(above_ref[ab // 2].astype(F32), ab)
                share = (2.0 * inverse) * mass_ref[j : j + 1, :] * above
                value = value + jnp.where(upper, share, 0.0)
            pieces.append(value.astype(BF16))
            slot = conn_ref[j : j + 1, :]
            slots.append(slot if keep is None else jnp.where(keep, slot, 65535))
        value = jnp.concatenate(pieces, 1)
        slot = jnp.concatenate(slots, 1)
        within = jnp.broadcast_to((slot & 255).astype(F32).astype(BF16), (256, width))
        chosen = jnp.where(place == within, BF16(1), BF16(0))
        group = slot >> 8
        wide = jnp.broadcast_to(group.astype(F32).astype(BF16), (vectors, width))
        spread = [jnp.where(wide == BF16(h), value, BF16(0)) for h in range(groups)]
        held = jnp.where(group_row == jnp.broadcast_to(group, (groups, width)), 1.0, 0.0)
        spread.append(jnp.concatenate([held, jnp.zeros((48 - groups, width), F32)], 0).astype(BF16))
        total[...] += lax.dot_general(
            jnp.concatenate(spread, 0),
            chosen,
            (((1,), (1,)), ((), ())),
            preferred_element_type=F32,
        )
    quarter = groups // out_ref.shape[0]
    for h in range(groups):
        wave = wave_ref[:, 256 * h : 256 * (h + 1)]
        one = -center * wave * inverse
        alone = -2.0 * center * one * inverse - wave
        used = total[rows + h : rows + h + 1, :] > 0.5
        value = jnp.where(used, total[vectors * h : vectors * (h + 1), :], alone)
        at = h % quarter
        out_ref[h // quarter, :, 256 * at : 256 * (at + 1)] = value.astype(BF16)


VMEM_SPEC = pl.BlockSpec(memory_space=pltpu.VMEM)
SMEM_SPEC = pl.BlockSpec(memory_space=pltpu.SMEM)


def call(kernel, name, out_shape, specs, scratch, *operands):
    return pl.pallas_call(
        kernel,
        out_shape=out_shape,
        in_specs=specs,
        out_specs=jax.tree.map(lambda _: VMEM_SPEC, out_shape),
        scratch_shapes=scratch,
        compiler_params=pltpu.CompilerParams(vmem_limit_bytes=VMEM_LIMIT),
        name=name,
    )(*operands)


def passed_along(value, axis, steps):
    count = lax.axis_size(axis)
    leading, last = (max(0, -steps), min(count, count - steps))
    return lax.ppermute(value, axis, [(source, source + steps) for source in range(leading, last)])


def per_device(
    wave_block, connectivity, send_list, levels, live_cells, potential, mass_scale,
    center, halfwidth, earlier_vectors,
):
    vectors, owned = wave_block.shape
    groups = owned // 256
    table_rows = vectors * groups + 48
    scalars = jnp.stack([center, 1.0 / halfwidth])
    level_row = levels.reshape(1, LANES)
    shape = jax.ShapeDtypeStruct
    full = (125, vectors, LANES)
    wave, mass, face = call(
        lambda *refs: gather_kernel(vectors, *refs),
        "gather_nodes",
        (shape(full, F32), shape((125, LANES), F32), shape((13, vectors + 8, LANES), F32)),
        [VMEM_SPEC] * 3,
        [pltpu.VMEM((table_rows, 512), BF16)],
        connectivity, wave_block, mass_scale.reshape(groups, 256),
    )
    ghost = passed_along(face, "cells", 1)
    packed = shape((13, vectors, LANES), BF16)
    sums, low_wave, low_mass, face_down, face_up = call(
        lambda *refs: first_kernel(vectors, *refs),
        "first_operator",
        (shape(full, F32), shape((25, vectors, LANES), F32), shape((25, LANES), F32), packed, packed),
        [VMEM_SPEC] * 5 + [SMEM_SPEC],
        [pltpu.VMEM(full, F32)],
        wave, mass, ghost, potential, level_row, live_cells,
    )
    above = passed_along(face_down, "cells", -1)
    below = passed_along(face_up, "cells", 1)
    result, face_down = call(
        lambda *refs: second_kernel(vectors, *refs),
        "second_operator",
        (shape(full, F32), packed),
        [VMEM_SPEC] * 9 + [SMEM_SPEC] * 2,
        [pltpu.VMEM(full, F32), pltpu.VMEM(full, F32)],
        sums, wave, mass, low_wave, low_mass, above, below, potential, level_row, live_cells, scalars,
    )
    above = passed_along(face_down, "cells", -1)
    parts = lax.axis_size("vecs")
    rounded = call(
        lambda *refs: scatter_kernel(vectors, *refs),
        "scatter_nodes",
        shape((parts, vectors, owned // parts), BF16),
        [VMEM_SPEC] * 5 + [SMEM_SPEC],
        [pltpu.VMEM((table_rows, 256), F32)],
        connectivity, result, mass, above, wave_block, scalars,
    )
    quarter = lax.all_to_all(rounded, "vecs", split_axis=0, concat_axis=0, tiled=True)
    quarter = quarter.reshape(parts * vectors, owned // parts)
    devices = lax.axis_size(AXES)
    total_vectors = parts * vectors
    row_share = earlier_vectors.shape[0] // devices
    partial_sum = lax.dot_general(
        earlier_vectors, quarter, (((1,), (1,)), ((), ())), preferred_element_type=F32
    )
    half = row_share // 2
    partial_sum = partial_sum.reshape(devices, 2, half, total_vectors).transpose(0, 2, 1, 3)
    partial_sum = partial_sum.reshape(devices * half, 2 * total_vectors)
    shares = lax.all_to_all(partial_sum, AXES, split_axis=0, concat_axis=0, tiled=True)
    own = jnp.sum(shares.reshape(devices, half, 2 * total_vectors), 0)
    own_rows = own.reshape(half, 2, total_vectors).transpose(1, 0, 2).reshape(row_share, total_vectors)
    low = jnp.broadcast_to(own.astype(BF16)[None], (devices, half, 2 * total_vectors))
    low = lax.all_to_all(low, AXES, split_axis=0, concat_axis=0, tiled=True)
    low = low.reshape(devices, half, 2, total_vectors).transpose(0, 2, 1, 3)
    low = low.reshape(devices * row_share, total_vectors)
    filtered = quarter.astype(F32) - lax.dot_general(
        low, earlier_vectors, (((0,), (0,)), ((), ())), preferred_element_type=F32
    )
    return (filtered, own_rows)


def solution(mesh):
    in_specs = (
        P("vecs", "cells"),
        P(None, "cells"),
        P("cells"),
        P("cells"),
        P("cells"),
        P(None, "cells"),
        P("cells"),
        P(),
        P(),
        P(None, AXES),
    )
    out_specs = (P(None, AXES), P(AXES, None))
    return jax.shard_map(
        per_device, mesh=mesh, in_specs=in_specs, out_specs=out_specs, check_vma=False
    )
```

time: 649 us -> 131 us (0.20)
  waiting for transfers between devices: 258 us -> 20.6 us
  other arithmetic: 214 us -> 0.36 us
  local copies, waits for them, and re-layouts: 123 us -> 9.07 us
  blocking collectives: 9.69 us -> 45.2 us
  Pallas kernels: 0 us -> 20.8 us
  between operations: 16.2 us -> 2.75 us
  starting transfers between devices: 11.8 us -> 19.1 us
    psum x1 -> x0, waiting for transfers between devices: 254 us -> none  [per_device(): projections = lax.psum(partial_sum, ('cells', 'vecs'))]
    scatter-add x4 -> x0, other arithmetic: 209 us -> none  [the longest x2 181 us: cell_sum(): return jnp.zeros((columns, owned_count + ghost_count), jnp.float32).at[:,...]
    gather x8 -> x0, local copies, waits for them, and re-layouts: 80.9 us -> none  [the longest x4 73.2 us: cell_sum(): values = extended[:, cells_conn].astype(jnp.bfloat16)]
    all_to_all x1 -> x2, blocking collectives: 9.69 us -> 45.2 us  [the longest x1 35.5 us: per_device(): lax.all_to_all(partial_sum, AXES, split_axis=0, concat_axis=0, tiled=True)]
    pallas_call x0 -> x4, Pallas kernels: none -> 20.8 us  [call(): pl.pallas_call(kernel, out_shape=out_shape, in_specs=specs, out_specs=jax...]
    all_to_all x0 -> x1, waiting for transfers between devices: none -> 15.2 us  [per_device(): low = lax.all_to_all(low, AXES, split_axis=0, concat_axis=0, tiled=True)]
    add x2 -> x0, local copies, waits for them, and re-layouts: 15.1 us -> none  [cell_sum(): kin_part[None, None, :] * stiff_part]
    slice x4 -> x0, local copies, waits for them, and re-layouts: 10.1 us -> none  [the longest x2 7.9 us: apply_operator(): summed = slot_sums[:, :owned_count].at[:, send_list].add(returned)]
  transfers between devices with their start and end apart: 5 -> 5, of which waited for: 4 -> 4; matrix products, arithmetic and copies ran while one was open for 2% -> 1% of each run, Pallas kernels for 0% -> 0%
where the time goes in v1:
time: 131 us
  blocking collectives  45.2 us (35%)
  Pallas kernels  20.8 us (16%)
  waiting for transfers between devices  20.6 us (16%)
  starting transfers between devices  19.1 us (15%)
  matrix products  12.9 us (10%)
  local copies, waits for them, and re-layouts  9.07 us (7%)
  between operations  2.75 us (2%)
    all_to_all x1, blocking collectives, per_device(): lax.all_to_all(partial_sum, AXES, split_axis=0, concat_axis=0, tiled=True)  35.5 us
    pallas_call x4, Pallas kernels, call(): pl.pallas_call(kernel, out_shape=out_shape, in_specs=specs, out_specs=jax...  20.8 us
    all_to_all x1, waiting for transfers between devices, per_device(): low = lax.all_to_all(low, AXES, split_axis=0, concat_axis=0, tiled=True)  15.2 us
    ppermute x4, starting transfers between devices, passed_along(): lax.ppermute(value, axis, [(source, source + steps) for source in range(l...  13.2 us
    all_to_all x1, blocking collectives, per_device(): lax.all_to_all(rounded, 'vecs', split_axis=0, concat_axis=0, tiled=True)  9.69 us
    dot_general x1, matrix products, per_device(): lax.dot_general(earlier_vectors, quarter, (((1,), (1,)), ((), ())), prefe...  6.61 us
    dot_general x1, matrix products, per_device(): lax.dot_general(low, earlier_vectors, (((0,), (0,)), ((), ())), preferred...  6.28 us
    all_to_all x1, starting transfers between devices, per_device(): low = lax.all_to_all(low, AXES, split_axis=0, concat_axis=0, tiled=True)  5.91 us
  transfers between devices with their start and end apart: 5, of which 4 were waited for; matrix products, arithmetic and copies ran while one was open for 1% of the time, Pallas kernels for 0%

profile of v1, /device:TPU:1, one launch (start us, length us, event | category | flops | bytes accessed | tf_op | source)
XLA Modules:
  0.0 130.7 jit_solution(17696164969646593368)
XLA Ops:
  0.6 0.8 reshape.37.refs_2_
  1.4 0.0 copy-start
  1.4 1.1 copy-done
  2.5 0.0 copy-start.3
  2.5 0.8 copy-done.3
  3.3 9.4 %gather_nodes.1 = (f32[125,16,128]{2,1,0:T(8,128)S(1)}, f32[125,128]{1,0:T(8,128)S(1)}, f32[13,24,128]{2,1,0:T(8,128)S(1)}) custom-call(s32[125,128]{1,0:T(8,128)S(1)} %copy-done.3, f32[16,9216]{1,0:T(8,128)S(1)} %copy-done, f32[36,256]{1,0:T(8,128)S(1)} %reshape.37.refs_2_), custom_call_target="tpu_custom_call" | custom-call | tf_op jit(solution)/shard_map/gather_nodes/pallas_call | solution.py:358
  12.7 4.9 %collective-permute-start = (f32[13,24,128]{2,1,0:T(8,128)S(1)}, f32[13,24,128]{2,1,0:T(8,128)S(1)}, u32[]{:S(2)}, u32[]{:S(2)}) collective-permute-start(f32[13,24,128]{2,1,0:T(8,128)S(1)} %get-tuple-element.14), channel_id=1, source_target_pairs={{0,4},{4,8},{8,12},{12,16},{16,20},{20,24},{24,28},{28,32},{32,36}... | collective-permute-start | bytes 479240 | tf_op jit(solution)/shard_map/ppermute | solution.py:372
  19.7 0.2 collective-permute-done.refs_2_
  19.9 0.0 copy-start.2
  19.9 0.8 copy-done.2
  20.7 0.0 copy-start.5
  20.7 0.7 copy-done.5
  21.4 2.9 %first_operator.1 = (f32[125,16,128]{2,1,0:T(8,128)S(1)}, f32[25,16,128]{2,1,0:T(8,128)S(1)}, f32[25,128]{1,0:T(8,128)S(1)}, bf16[13,16,128]{2,1,0:T(8,128)(2,1)S(1)}, bf16[13,16,128]{2,1,0:T(8,128)(2,1)S(1)}) custom-call(f32[125,16,128]{2,1,0:T(8,128)S(1)} %get-tuple-element.12.refs_0_.refs_1_, f32[125,128]{1,0:T(8,128)S(1)} %get-tuple-element.13.refs_1_.refs_2_, ...), custom_call_target="tpu_custom_call" | custom-call | tf_op jit(solution)/shard_map/first_operator/pallas_call | solution.py:358
  24.2 1.9 %collective-permute-start.1 = (bf16[13,16,128]{2,1,0:T(8,128)(2,1)S(1)}, bf16[13,16,128]{2,1,0:T(8,128)(2,1)S(1)}, u32[]{:S(2)}, u32[]{:S(2)}) collective-permute-start(bf16[13,16,128]{2,1,0:T(8,128)(2,1)S(1)} %get-tuple-element.18), channel_id=1, source_target_pairs={{4,0},{8,4},{12,8},{16,12},{20,16},{24,20},{28,24},{32,28},{36,32}... | collective-permute-start | bytes 159752 | tf_op jit(solution)/shard_map/ppermute | solution.py:372
  26.2 4.4 %collective-permute-start.2 = (bf16[13,16,128]{2,1,0:T(8,128)(2,1)S(1)}, bf16[13,16,128]{2,1,0:T(8,128)(2,1)S(1)}, u32[]{:S(2)}, u32[]{:S(2)}) collective-permute-start(bf16[13,16,128]{2,1,0:T(8,128)(2,1)S(1)} %get-tuple-element.19), channel_id=1, source_target_pairs={{0,4},{4,8},{8,12},{12,16},{16,20},{20,24},{24,28},{28,32},{32,36}... | collective-permute-start | bytes 159752 | tf_op jit(solution)/shard_map/ppermute | solution.py:372
  30.6 0.1 pad_maximum_fusion.refs_10_.refs_5_
  30.6 0.0 collective-permute-done.1.refs_5_
  30.6 1.1 collective-permute-done.2.refs_6_
  31.8 3.6 %second_operator.1 = (f32[125,16,128]{2,1,0:T(8,128)S(1)}, bf16[13,16,128]{2,1,0:T(8,128)(2,1)S(1)}) custom-call(f32[125,16,128]{2,1,0:T(8,128)S(1)} %get-tuple-element.15.refs_0_, f32[125,16,128]{2,1,0:T(8,128)S(1)} %get-tuple-element.12.refs_0_.refs_1_, f32[125,128]{1,0:T(8,128)S(1)} %get-tuple-element.13.refs_1_.refs_2_, ...), custom_call_target="tpu_custom_call" | custom-call | tf_op jit(solution)/shard_map/second_operator/pallas_call | solution.py:358
  35.3 1.9 %collective-permute-start.3 = (bf16[13,16,128]{2,1,0:T(8,128)(2,1)S(1)}, bf16[13,16,128]{2,1,0:T(8,128)(2,1)S(1)}, u32[]{:S(2)}, u32[]{:S(2)}) collective-permute-start(bf16[13,16,128]{2,1,0:T(8,128)(2,1)S(1)} %get-tuple-element.21), channel_id=1, source_target_pairs={{4,0},{8,4},{12,8},{16,12},{20,16},{24,20},{28,24},{32,28},{36,32}... | collective-permute-start | bytes 159752 | tf_op jit(solution)/shard_map/ppermute | solution.py:372
  37.3 4.1 %collective-permute-done.3.refs_3_ = bf16[13,16,128]{2,1,0:T(8,128)(2,1)S(1)} collective-permute-done((bf16[13,16,128]{2,1,0:T(8,128)(2,1)S(1)}, bf16[13,16,128]{2,1,0:T(8,128)(2,1)S(1)}, u32[]{:S(2)}, u32[]{:S(2)}) %collective-permute-start.3) | collective-permute-done | bytes 53280 | tf_op jit(solution)/shard_map/ppermute | solution.py:372
  41.4 0.0 copy-start.1
  41.4 1.1 copy-done.1
  42.5 0.0 copy-start.4
  42.5 0.8 copy-done.4
  43.3 5.0 %scatter_nodes.1 = bf16[4,16,2304]{2,1,0:T(8,128)(2,1)S(1)} custom-call(s32[125,128]{1,0:T(8,128)S(1)} %copy-done.4, f32[125,16,128]{2,1,0:T(8,128)S(1)} %get-tuple-element.20.refs_1_, f32[125,128]{1,0:T(8,128)S(1)} %get-tuple-element.13.refs_1_.refs_2_, bf16[13,16,128]{2,1,0:T(8,128)(2,1)S(1)} %collective-permute-done.3.refs_3_, f32[16,9216]{1,0:T(8,128)S(1)} %copy-done.1, ...), custom_call_target="tpu_custom_call" | custom-call | tf_op jit(solution)/shard_map/scatter_nodes/pallas_call | solution.py:358
  48.3 9.7 %all_to_all.19 = bf16[4,16,2304]{2,1,0:T(8,128)(2,1)S(1)} all-to-all(bf16[4,16,2304]{2,1,0:T(8,128)(2,1)S(1)} %scatter_nodes.1), channel_id=1, replica_groups=mesh['cells'=64,'vecs'=4] {'vecs'}, dimensions={0} | all-to-all | bytes 589824 | tf_op jit(solution)/shard_map/all_to_all | solution.py:424
  58.0 6.6 %convolution_bitcast_fusion = f32[2048,64]{0,1:T(8,128)S(1)} fusion(bf16[64,2304]{1,0:T(8,128)(2,1)S(1)} %bitcast.26, bf16[2048,2304]{1,0:T(8,128)(2,1)} %param.18), kind=kOutput, calls=%fused_computation | convolution fusion | flops 603979776 | bytes 10256384 | tf_op jit(solution)/shard_map/dot_general | solution.py:429
  64.6 0.3 copy.18
  64.9 0.5 copy.19
  65.4 0.2 copy.20
  65.7 35.5 %all_to_all.20 = f32[256,4,128]{2,1,0:T(4,128)S(1)} all-to-all(f32[256,4,128]{2,1,0:T(4,128)S(1)} %copy.20), channel_id=1, replica_groups=mesh['cells'=64,'vecs'=4] {'cells','vecs'}, dimensions={0} | all-to-all | bytes 1048576 | tf_op jit(solution)/shard_map/all_to_all | solution.py:435
  101.1 0.3 reduce_sum.9
  101.4 0.8 broadcast_in_dim.2
  102.2 5.9 %all-to-all-start.2 = ((bf16[256,4,128]{2,1,0:T(4,128)(2,1)}), bf16[256,4,128]{2,1,0:T(4,128)(2,1)S(1)}, u32[]{:S(2)}, u32[]{:S(2)}) async-start(bf16[256,4,128]{2,1,0:T(4,128)(2,1)} %broadcast_in_dim.2), calls=%async_computation.2 | async-start | bytes 524288 | tf_op jit(solution)/shard_map/all_to_all | solution.py:439
  108.1 0.1 reshape.43
  108.2 0.6 copy.23
  108.8 15.2 %all-to-all-done.2 = bf16[256,4,128]{2,1,0:T(4,128)(2,1)S(1)} async-done(((bf16[256,4,128]{2,1,0:T(4,128)(2,1)}), bf16[256,4,128]{2,1,0:T(4,128)(2,1)S(1)}, u32[]{:S(2)}, u32[]{:S(2)}) %all-to-all-start.2) | async-done | bytes 262176 | tf_op jit(solution)/shard_map/all_to_all | solution.py:439
  124.0 0.2 copy.21
  124.1 0.3 copy.22
  124.5 6.3 %convert_subtract_fusion = f32[64,2304]{1,0:T(8,128)} fusion(bf16[4,16,2304]{2,1,0:T(8,128)(2,1)S(1)} %all_to_all.19, bf16[2048,64]{1,0:T(8,128)(2,1)S(1)} %bitcast.25, bf16[2048,2304]{1,0:T(8,128)(2,1)} %param.18), kind=kOutput, calls=%fused_computation.1 | convolution fusion | flops 604274688 | bytes 10584064 | tf_op jit(solution)/shard_map/dot_general | solution.py:442
  (1 shorter events, 0.0 us)
Async XLA Ops:
  1.4 1.1 copy-start
  2.5 0.8 copy-start.3
  12.7 7.1 %collective-permute-start = (f32[13,24,128]{2,1,0:T(8,128)S(1)}, f32[13,24,128]{2,1,0:T(8,128)S(1)}, u32[]{:S(2)}, u32[]{:S(2)}) collective-permute-start(f32[13,24,128]{2,1,0:T(8,128)S(1)} %get-tuple-element.14), channel_id=1, source_target_pairs={{0,4},{4,8},{8,12},{12,16},{16,20},{20,24},{24,28},{28,32},{32,36}... | collective-permute-start | bytes 479240 | tf_op jit(solution)/shard_map/ppermute | solution.py:372
  19.9 0.8 copy-start.2
  20.7 0.7 copy-start.5
  24.2 6.4 %collective-permute-start.1 = (bf16[13,16,128]{2,1,0:T(8,128)(2,1)S(1)}, bf16[13,16,128]{2,1,0:T(8,128)(2,1)S(1)}, u32[]{:S(2)}, u32[]{:S(2)}) collective-permute-start(bf16[13,16,128]{2,1,0:T(8,128)(2,1)S(1)} %get-tuple-element.18), channel_id=1, source_target_pairs={{4,0},{8,4},{12,8},{16,12},{20,16},{24,20},{28,24},{32,28},{36,32}... | collective-permute-start | bytes 159752 | tf_op jit(solution)/shard_map/ppermute | solution.py:372
  26.2 5.6 %collective-permute-start.2 = (bf16[13,16,128]{2,1,0:T(8,128)(2,1)S(1)}, bf16[13,16,128]{2,1,0:T(8,128)(2,1)S(1)}, u32[]{:S(2)}, u32[]{:S(2)}) collective-permute-start(bf16[13,16,128]{2,1,0:T(8,128)(2,1)S(1)} %get-tuple-element.19), channel_id=1, source_target_pairs={{0,4},{4,8},{8,12},{12,16},{16,20},{20,24},{24,28},{28,32},{32,36}... | collective-permute-start | bytes 159752 | tf_op jit(solution)/shard_map/ppermute | solution.py:372
  35.3 6.1 %collective-permute-start.3 = (bf16[13,16,128]{2,1,0:T(8,128)(2,1)S(1)}, bf16[13,16,128]{2,1,0:T(8,128)(2,1)S(1)}, u32[]{:S(2)}, u32[]{:S(2)}) collective-permute-start(bf16[13,16,128]{2,1,0:T(8,128)(2,1)S(1)} %get-tuple-element.21), channel_id=1, source_target_pairs={{4,0},{8,4},{12,8},{16,12},{20,16},{24,20},{28,24},{32,28},{36,32}... | collective-permute-start | bytes 159752 | tf_op jit(solution)/shard_map/ppermute | solution.py:372
  41.4 1.1 copy-start.1
  42.5 0.8 copy-start.4
  102.2 21.8 %all-to-all-start.2 = ((bf16[256,4,128]{2,1,0:T(4,128)(2,1)}), bf16[256,4,128]{2,1,0:T(4,128)(2,1)S(1)}, u32[]{:S(2)}, u32[]{:S(2)}) async-start(bf16[256,4,128]{2,1,0:T(4,128)(2,1)} %broadcast_in_dim.2), calls=%async_computation.2 | async-start | bytes 524288 | tf_op jit(solution)/shard_map/all_to_all | solution.py:439

commit v2 on v0

v2 whole, which is shorter than its diff:
```python
import math

import jax
import jax.numpy as jnp
import numpy as np
from jax import lax
from jax.experimental import pallas as pl
from jax.experimental.pallas import tpu as pltpu
from jax.sharding import PartitionSpec as P

F32, BF16, I32 = jnp.float32, jnp.bfloat16, jnp.int32
AXES = ("cells", "vecs")
LANES = 128
VMEM_LIMIT = 20 * 2**20


def gll_tables():
    root_value = math.sqrt(3.0 / 7.0)
    points = np.array([-1.0, -root_value, 0.0, root_value, 1.0])
    weights = np.array([0.1, 49.0 / 90.0, 32.0 / 45.0, 49.0 / 90.0, 0.1])
    barycentric = np.ones(5)
    for node_index in range(5):
        for other_node in range(5):
            if other_node != node_index:
                barycentric[node_index] = barycentric[node_index] / (
                    points[node_index] - points[other_node]
                )
    derivative = np.zeros((5, 5))
    for row_index in range(5):
        for col_index in range(5):
            if row_index != col_index:
                derivative[row_index, col_index] = (
                    barycentric[col_index]
                    / barycentric[row_index]
                    / (points[row_index] - points[col_index])
                )
        derivative[row_index, row_index] = -np.sum(derivative[row_index])
    mass_one = np.zeros((5, 5))
    for node_index in range(5):
        mass_one[node_index, node_index] = weights[node_index]
    laplace_one = derivative.T @ mass_one @ derivative
    stiffness = (
        np.kron(np.kron(laplace_one, mass_one), mass_one)
        + np.kron(np.kron(mass_one, laplace_one), mass_one)
        + np.kron(np.kron(mass_one, mass_one), laplace_one)
    )
    quadrature = np.kron(np.kron(weights, weights), weights)
    return (stiffness.astype(np.float32), quadrature.astype(np.float32))


STIFFNESS, QUADRATURE = gll_tables()
STIFFNESS = STIFFNESS.astype(jnp.bfloat16).astype(np.float32)


def node(a, b, c):
    return 25 * a + 5 * b + c


def lane_index(rows):
    return lax.broadcasted_iota(I32, (rows, LANES), 1)


def axis_bits(lane, axis):
    return [(lane >> bit) & 1 for bit in ((0, 3, 5), (1, 4, 6))[axis]]


def axis_place(lane, axis):
    low, mid, high = axis_bits(lane, axis)
    return low + 2 * mid + 4 * high


def below_of(lane, axis):
    low, mid, high = axis_bits(lane, axis)
    scale = 1 + axis
    step = jnp.where(low == 1, 1, jnp.where(mid == 1, 7, 23)) * scale
    first = axis_place(lane, axis) == 0
    return jnp.where(first, lane, lane - step), jnp.logical_not(first)


def above_of(lane, axis):
    low, mid, high = axis_bits(lane, axis)
    scale = 1 + axis
    step = jnp.where(low == 0, 1, jnp.where(mid == 0, 7, 23)) * scale
    last = axis_place(lane, axis) == 7
    return jnp.where(last, lane, lane + step), jnp.logical_not(last)


def pick(values, index):
    return jnp.take_along_axis(values, index, axis=1)


def up_layer(values):
    return pltpu.roll(values, 4, 1)


def down_layer(values):
    return pltpu.roll(values, LANES - 4, 1)


def split_low(values):
    high = values.astype(BF16)
    return high, (values - high.astype(F32)).astype(BF16)


class Nodes:
    def __init__(self, low, mid, top):
        self.low, self.mid, self.top = low, mid, top

    def at(self, j):
        ab, c = divmod(j, 5)
        if c == 0:
            return self.low, ab
        if c == 4:
            return self.top, ab
        return self.mid, 3 * ab + c - 1

    def load(self, j, part=slice(None)):
        ref, row = self.at(j)
        return ref[row, part, :]

    def store(self, j, value, part=slice(None)):
        ref, row = self.at(j)
        ref[row, part, :] = value

    def line(self, j):
        ref, row = self.at(j)
        return ref[row : row + 1, :]

    def store_line(self, j, value):
        ref, row = self.at(j)
        ref[row : row + 1, :] = value


ALL_ROWS = list(range(125))
MID_ROWS = [j for j in ALL_ROWS if j % 5 in (1, 2, 3)]
LOW_ROWS = [j for j in ALL_ROWS if j % 5 == 0]
TOP_ROWS = [j for j in ALL_ROWS if j % 5 == 4]


def upper_lanes(rows):
    return (lane_index(rows) >> 2) & 1 == 1


def one_hot(slots, width):
    place = lax.broadcasted_iota(I32, (256, width), 0).astype(F32).astype(BF16)
    within = jnp.broadcast_to((slots & 255).astype(F32).astype(BF16), (256, width))
    return jnp.where(place == within, BF16(1), BF16(0))


def gather_rows(vectors, groups, rows, conn, table, wave, mass):
    base = vectors * groups
    start = 0
    while start < len(rows):
        count = 5 if len(rows) - start == 5 else min(4, len(rows) - start)
        width = count * LANES
        chunk = rows[start : start + count]
        slots = jnp.concatenate([conn[j : j + 1, :] for j in chunk], 1)
        chosen = one_hot(slots, width)
        found = jnp.dot(
            table[...], jnp.concatenate([chosen, chosen], 0), preferred_element_type=F32
        )
        group = slots >> 8
        wide = jnp.broadcast_to(group, (vectors, width))
        total = jnp.zeros((vectors, width), F32)
        for h in range(groups):
            total = jnp.where(wide == h, found[vectors * h : vectors * (h + 1)], total)
        group_row = lax.broadcasted_iota(I32, (groups, width), 0)
        mine = group_row == jnp.broadcast_to(group, (groups, width))
        line = jnp.sum(jnp.where(mine, found[base : base + groups], 0.0), 0, keepdims=True)
        for i in range(count):
            wave[start + i] = total[:, LANES * i : LANES * (i + 1)]
            mass[start + i : start + i + 1, :] = line[:, LANES * i : LANES * (i + 1)]
        start += count


def gather_face_kernel(
    vectors, conn_hbm, wave_hbm, mass_hbm, table, conn, wave_top, mass_top, face_out,
    wave_in, mass_in, sems,
):
    copies = [
        pltpu.make_async_copy(wave_hbm, wave_in, sems.at[0]),
        pltpu.make_async_copy(mass_hbm, mass_in, sems.at[1]),
        pltpu.make_async_copy(conn_hbm, conn, sems.at[2]),
    ]
    for copy in copies:
        copy.start()
    for copy in copies:
        copy.wait()
    groups = wave_in.shape[1] // 256
    base = vectors * groups
    high, low = split_low(wave_in[...])
    for h in range(groups):
        table[vectors * h : vectors * (h + 1), 0:256] = high[:, 256 * h : 256 * (h + 1)]
        table[vectors * h : vectors * (h + 1), 256:512] = low[:, 256 * h : 256 * (h + 1)]
    for half in range(2):
        high, low = split_low(mass_in[pl.ds(half, groups, stride=2), :])
        spare = jnp.zeros((table.shape[0] - base - groups, LANES), F32)
        columns = slice(LANES * half, LANES * (half + 1))
        table[base:, columns] = jnp.concatenate([high.astype(F32), spare], 0).astype(BF16)
        columns = slice(256 + LANES * half, 256 + LANES * (half + 1))
        table[base:, columns] = jnp.concatenate([low.astype(F32), spare], 0).astype(BF16)
    gather_rows(vectors, groups, TOP_ROWS, conn, table, wave_top, mass_top)
    upper, upper_one = upper_lanes(vectors), upper_lanes(1)
    for i in range(13):
        second = min(2 * i + 1, 24)
        face_out[i, 0:vectors, :] = jnp.where(upper, wave_top[2 * i], down_layer(wave_top[second]))
        packed = jnp.where(
            upper_one,
            mass_top[2 * i : 2 * i + 1, :],
            down_layer(mass_top[second : second + 1, :]),
        )
        face_out[i, vectors : vectors + 8, :] = jnp.broadcast_to(packed, (8, LANES))


def gather_rest_kernel(
    vectors, groups, table, conn, potential_hbm, levels_hbm, live_ref,
    wave_mid, mass_mid, kinetic, coefficient, levels_in, sems,
):
    copies = [
        pltpu.make_async_copy(potential_hbm, coefficient, sems.at[0]),
        pltpu.make_async_copy(levels_hbm, levels_in, sems.at[1]),
    ]
    for copy in copies:
        copy.start()
    gather_rows(vectors, groups, MID_ROWS, conn, table, wave_mid, mass_mid)
    copies[0].wait()
    copies[1].wait()
    size = jnp.exp2(-levels_in[...].astype(F32))
    in_use = jnp.where(lane_index(1) < live_ref[0], 1.0, 0.0).astype(F32)
    kinetic[...] = jnp.broadcast_to(size / 4.0 * in_use, (8, LANES))
    volume = size * size * size / 8.0 * in_use
    for j in ALL_ROWS:
        line = volume * float(QUADRATURE[j]) * coefficient[j : j + 1, :]
        coefficient[j : j + 1, :] = line


def apply_cells(values, terms, kinetic, coefficient, rows, vectors):
    def one(t, carry):
        part = pl.ds(pl.multiple_of(8 * t, 8), 8)
        for j in rows:
            total = None
            for k in np.flatnonzero(STIFFNESS[j]):
                term = values[int(k), part, :] * float(STIFFNESS[j, k])
                total = term if total is None else total + term
            weight = jnp.broadcast_to(coefficient[j : j + 1, :], (8, LANES))
            terms.store(j, kinetic[...] * total + weight * values[j, part, :], part)
        return carry

    lax.fori_loop(0, vectors // 8, one, 0)


def join_layer(terms, layers, vectors):
    lane = lane_index(8)
    moves = [below_of(lane, axis) + above_of(lane, axis) for axis in range(2)]

    def one(t, carry):
        part = pl.ds(pl.multiple_of(8 * t, 8), 8)
        for axis in range(2):
            before, has_before, after, has_after = moves[axis]
            for other in range(5):
                for c in layers:
                    start = node(0, other, c) if axis == 0 else node(other, 0, c)
                    end = node(4, other, c) if axis == 0 else node(other, 4, c)
                    first, last = terms.load(start, part), terms.load(end, part)
                    joined = first + jnp.where(has_before, pick(last, before), 0.0)
                    terms.store(start, joined, part)
                    terms.store(end, jnp.where(has_after, pick(joined, after), last), part)
        return carry

    lax.fori_loop(0, vectors // 8, one, 0)


def pack_lower(low, face_out, vectors):
    upper = upper_lanes(vectors)
    for i in range(13):
        second = min(2 * i + 1, 24)
        face_out[i] = jnp.where(upper, up_layer(low[second]), low[2 * i]).astype(BF16)


def pack_upper(top, face_out, vectors):
    upper = upper_lanes(vectors)
    for i in range(13):
        second = min(2 * i + 1, 24)
        face_out[i] = jnp.where(upper, top[2 * i], down_layer(top[second])).astype(BF16)


def from_below(packed, ab):
    return packed if ab % 2 == 1 else down_layer(packed)


def from_above(packed, ab):
    return packed if ab % 2 == 1 else up_layer(packed)


def first_faces_kernel(
    vectors, wave_mid, wave_top, mass_mid, mass_top, ghost, kinetic, coefficient,
    values, wave_low, mass_low, low, top, face_down, face_up,
):
    upper, upper_one = upper_lanes(vectors), upper_lanes(1)
    for ab in range(25):
        packed = ghost[ab // 2]
        wave_low[ab] = jnp.where(upper, up_layer(wave_top[ab]), from_below(packed[0:vectors], ab))
        mass_low[ab : ab + 1, :] = jnp.where(
            upper_one,
            up_layer(mass_top[ab : ab + 1, :]),
            from_below(packed[vectors : vectors + 1], ab),
        )
    wave, mass = Nodes(wave_low, wave_mid, wave_top), Nodes(mass_low, mass_mid, mass_top)
    for j in ALL_ROWS:
        values[j] = (wave.load(j) * mass.line(j)).astype(BF16).astype(F32)
    terms = Nodes(low, None, top)
    apply_cells(values, terms, kinetic, coefficient, LOW_ROWS + TOP_ROWS, vectors)
    join_layer(terms, (0, 4), vectors)
    pack_lower(low, face_down, vectors)
    pack_upper(top, face_up, vectors)


def rest_kernel(vectors, values, kinetic, coefficient, mid):
    terms = Nodes(None, mid, None)
    apply_cells(values, terms, kinetic, coefficient, MID_ROWS, vectors)
    join_layer(terms, (1, 2, 3), vectors)


def second_faces_kernel(
    vectors, low, mid, top, wave_low, wave_mid, wave_top, mass_low, mass_mid, mass_top,
    above, below, kinetic, coefficient, center_ref, halfwidth_ref,
    values, base_mid, base_top, low_out, face_down,
):
    upper = upper_lanes(vectors)
    center = center_ref[0]
    inverse = 1.0 / jnp.full((1, LANES), halfwidth_ref[0], F32)
    again = (-2.0 * center) * inverse
    sums = Nodes(low, mid, top)
    wave, mass = Nodes(wave_low, wave_mid, wave_top), Nodes(mass_low, mass_mid, mass_top)
    base = Nodes(None, base_mid, base_top)

    def degree_one(j, total):
        one = (mass.line(j) * total - center * wave.load(j)) * inverse
        values[j] = (one * mass.line(j)).astype(BF16).astype(F32)
        if j % 5 > 0:
            base.store(j, again * one - wave.load(j))

    for ab in range(25):
        first, last = low[ab], top[ab]
        shared = first + up_layer(last)
        incoming = from_below(below[ab // 2].astype(F32), ab)
        degree_one(5 * ab, jnp.where(upper, shared, first + incoming))
        incoming = from_above(above[ab // 2].astype(F32), ab)
        degree_one(5 * ab + 4, jnp.where(upper, last + incoming, down_layer(shared)))
        for c in range(1, 4):
            degree_one(5 * ab + c, mid[3 * ab + c - 1])
    terms = Nodes(low_out, None, None)
    apply_cells(values, terms, kinetic, coefficient, LOW_ROWS, vectors)
    join_layer(terms, (0,), vectors)
    pack_lower(low_out, face_down, vectors)


def kept_lanes(ab):
    lane = lane_index(1)
    keep = None
    if ab // 5 == 4:
        keep = axis_place(lane, 0) == 7
    if ab % 5 == 4:
        last = axis_place(lane, 1) == 7
        keep = last if keep is None else jnp.logical_and(keep, last)
    return keep


def scatter_rows(vectors, groups, rows, conn, value_of, total):
    start = 0
    while start < len(rows):
        count = 5 if len(rows) - start == 5 else min(4, len(rows) - start)
        width = count * LANES
        pieces, slots = [], []
        for j in rows[start : start + count]:
            keep, slot = kept_lanes(j // 5), conn[j : j + 1, :]
            slots.append(slot if keep is None else jnp.where(keep, slot, 65535))
            pieces.append(value_of(j).astype(BF16))
        value, slot = jnp.concatenate(pieces, 1), jnp.concatenate(slots, 1)
        group = slot >> 8
        wide = jnp.broadcast_to(group.astype(F32).astype(BF16), (vectors, width))
        spread = [jnp.where(wide == BF16(h), value, BF16(0)) for h in range(groups)]
        spare = total.shape[0] - vectors * groups
        group_row = lax.broadcasted_iota(I32, (spare, width), 0)
        held = jnp.where(group_row == jnp.broadcast_to(group, (spare, width)), 1.0, 0.0)
        spread.append(held.astype(BF16))
        moved = lax.dot_general(
            jnp.concatenate(spread, 0),
            one_hot(slot, width),
            (((1,), (1,)), ((), ())),
            preferred_element_type=F32,
        )
        if start == 0:
            total[...] = moved
        else:
            total[...] += moved
        start += count


def second_rest_kernel(
    vectors, values, kinetic, coefficient, low, mass_mid, mass_top, base_mid, base_top, conn,
    wave_hbm, center_ref, halfwidth_ref, total, done_top, alone, mid, top, wave_in, sems,
):
    copy = pltpu.make_async_copy(wave_hbm, wave_in, sems.at[0])
    copy.start()
    groups = wave_in.shape[1] // 256
    center = center_ref[0]
    inverse = 1.0 / jnp.full((1, LANES), halfwidth_ref[0], F32)
    terms = Nodes(None, mid, top)
    apply_cells(values, terms, kinetic, coefficient, MID_ROWS + TOP_ROWS, vectors)
    join_layer(terms, (1, 2, 3, 4), vectors)
    upper = upper_lanes(vectors)
    for ab in range(25):
        last = top[ab]
        joined = jnp.where(upper, last, down_layer(low[ab]) + last)
        line = (2.0 * inverse) * mass_top[ab : ab + 1, :]
        done_top[ab] = base_top[ab] + line * joined

    def value_of(j):
        row = 3 * (j // 5) + j % 5 - 1
        return base_mid[row] + (2.0 * inverse) * mass_mid[row : row + 1, :] * mid[row]

    scatter_rows(vectors, groups, MID_ROWS, conn, value_of, total)
    copy.wait()
    wide_inverse = jnp.concatenate([inverse, inverse], 1)
    for h in range(groups):
        wave = wave_in[:, 256 * h : 256 * (h + 1)]
        one = -center * wave * wide_inverse
        alone[:, 256 * h : 256 * (h + 1)] = (
            (-2.0 * center) * wide_inverse * one - wave
        ).astype(BF16)


def scatter_top_kernel(
    vectors, conn, before, done_top, mass_top, above, alone, halfwidth_ref, out_ref, total
):
    groups = alone.shape[1] // 256
    base = vectors * groups
    upper = upper_lanes(vectors)
    inverse = 1.0 / jnp.full((1, LANES), halfwidth_ref[0], F32)

    def value_of(j):
        ab = j // 5
        incoming = from_above(above[ab // 2].astype(F32), ab)
        share = (2.0 * inverse) * mass_top[ab : ab + 1, :] * incoming
        return done_top[ab] + jnp.where(upper, share, 0.0)

    scatter_rows(vectors, groups, TOP_ROWS, conn, value_of, total)
    quarter = groups // out_ref.shape[0]
    for h in range(groups):
        rows = slice(vectors * h, vectors * (h + 1))
        count = total[base + h : base + h + 1, :] + before[base + h : base + h + 1, :]
        value = total[rows, :] + before[rows, :]
        own = alone[:, 256 * h : 256 * (h + 1)].astype(F32)
        at = h % quarter
        out_ref[h // quarter, :, 256 * at : 256 * (at + 1)] = jnp.where(
            count > 0.5, value, own
        ).astype(BF16)


def stream_rows(earlier_hbm, earlier, sems):
    count = sems.shape[0]
    size = earlier.shape[0] // count
    copies = []
    for i in range(count):
        rows = slice(size * i, size * (i + 1))
        copy = pltpu.make_async_copy(earlier_hbm.at[rows, :], earlier.at[rows, :], sems.at[i])
        copy.start()
        copies.append((rows, copy))
    return copies


def project_kernel(
    cores, parts, share, earlier_hbm, quarter, core_ref, keep, send, earlier, sems
):
    half = share // 2
    for i, (rows, copy) in enumerate(stream_rows(earlier_hbm, earlier, sems)):
        copy.wait()
        product = lax.dot_general(
            earlier[rows, :], quarter[...], (((1,), (1,)), ((), ())), preferred_element_type=F32
        )
        chunk = product.shape[0] // (cores * parts * share)
        lines = chunk * parts * half
        place = slice(lines * i, lines * (i + 1))
        product = product.reshape(chunk, cores, parts, share, product.shape[-1])
        for core in range(cores):
            mine = product[:, core].reshape(chunk * parts, share, product.shape[-1])
            mine = jnp.concatenate([mine[:, :half], mine[:, half:]], 2)
            mine = mine.reshape(lines, mine.shape[-1])

            @pl.when(core_ref[0] == core)
            def _():
                keep[place, :] = mine

            @pl.when(core_ref[0] != core)
            def _():
                send[place, :] = mine


def filter_kernel(
    cores, parts, share, mine, theirs, earlier_hbm, quarter, core_ref, out_ref, low, earlier, sems
):
    copies = stream_rows(earlier_hbm, earlier, sems)
    half = share // 2
    columns = mine.shape[-1] // 2
    block = parts * share

    def unpack(ref, core):
        value = ref[...].astype(F32)
        value = jnp.concatenate([value[:, :, :columns], value[:, :, columns:]], 1)
        value = value.reshape(value.shape[0] // parts, block, columns)
        for i in range(value.shape[0]):
            at = (cores * i + core) * block
            low[at : at + block, :] = value[i].astype(BF16)

    for core in range(cores):

        @pl.when(core_ref[0] == core)
        def _():
            unpack(mine, core)
            unpack(theirs, 1 - core)

    out_ref[...] = quarter[...].astype(F32)
    for rows, copy in copies:
        copy.wait()
        out_ref[...] -= lax.dot_general(
            low[rows, :], earlier[rows, :], (((0,), (0,)), ((), ())), preferred_element_type=F32
        )


VMEM_SPEC = pl.BlockSpec(memory_space=pltpu.VMEM)
SMEM_SPEC = pl.BlockSpec(memory_space=pltpu.SMEM)
HBM_SPEC = pl.BlockSpec(memory_space=pltpu.HBM)


def call(kernel, name, out_shape, specs, scratch, *operands):
    return pl.pallas_call(
        kernel,
        out_shape=out_shape,
        in_specs=[{"v": VMEM_SPEC, "s": SMEM_SPEC, "h": HBM_SPEC}[letter] for letter in specs],
        out_specs=jax.tree.map(lambda _: VMEM_SPEC, out_shape),
        scratch_shapes=scratch,
        compiler_params=pltpu.CompilerParams(vmem_limit_bytes=VMEM_LIMIT),
        name=name,
    )(*[
        pltpu.with_memory_space_constraint(operand, pltpu.HBM) if letter == "h" else operand
        for letter, operand in zip(specs, operands)
    ])


def passed_along(value, axis, steps):
    count = lax.axis_size(axis)
    leading, last = (max(0, -steps), min(count, count - steps))
    return lax.ppermute(value, axis, [(source, source + steps) for source in range(leading, last)])


def per_device(
    wave_block, connectivity, send_list, levels, live_cells, potential, mass_scale,
    center, halfwidth, earlier_vectors,
):
    vectors, owned = wave_block.shape
    groups = owned // 256
    table_rows = vectors * groups + 48
    cells, parts = lax.axis_size("cells"), lax.axis_size("vecs")
    devices, cores = cells * parts, 2
    center, halfwidth = center.reshape(1), halfwidth.reshape(1)

    def shape(*sizes, kind=F32):
        return jax.ShapeDtypeStruct(sizes, kind)

    def rows(count):
        return shape(count, vectors, LANES)

    def lines(count):
        return shape(count, LANES)

    packed = shape(13, vectors, LANES, kind=BF16)
    scratch_rows = lambda count: pltpu.VMEM((count, vectors, LANES), F32)
    wave_scratch = pltpu.VMEM((vectors, owned), F32)

    table, conn, wave_top, mass_top, face = call(
        lambda *refs: gather_face_kernel(vectors, *refs),
        "gather_face",
        (
            shape(table_rows, 512, kind=BF16), shape(125, LANES, kind=I32), rows(25), lines(25),
            shape(13, vectors + 8, LANES),
        ),
        "hhh",
        [wave_scratch, pltpu.VMEM((owned // LANES, LANES), F32), pltpu.SemaphoreType.DMA((3,))],
        connectivity, wave_block, mass_scale.reshape(owned // LANES, LANES),
    )
    ghost = passed_along(face, "cells", 1)
    wave_mid, mass_mid, kinetic, coefficient = call(
        lambda *refs: gather_rest_kernel(vectors, groups, *refs),
        "gather_rest",
        (rows(75), lines(75), lines(8), lines(125)),
        "vvhhs",
        [pltpu.VMEM((1, LANES), I32), pltpu.SemaphoreType.DMA((2,))],
        table, conn, potential, levels.reshape(1, LANES), live_cells,
    )
    values, wave_low, mass_low, low, top, face_down, face_up = call(
        lambda *refs: first_faces_kernel(vectors, *refs),
        "first_faces",
        (rows(125), rows(25), lines(25), rows(25), rows(25), packed, packed),
        "vvvvvvv",
        [],
        wave_mid, wave_top, mass_mid, mass_top, ghost, kinetic, coefficient,
    )
    above = passed_along(face_down, "cells", -1)
    below = passed_along(face_up, "cells", 1)
    mid = call(
        lambda *refs: rest_kernel(vectors, *refs), "first_rest", rows(75), "vvv", [],
        values, kinetic, coefficient,
    )
    values, base_mid, base_top, low, face_down = call(
        lambda *refs: second_faces_kernel(vectors, *refs),
        "second_faces",
        (rows(125), rows(75), rows(25), rows(25), packed),
        "v" * 13 + "ss",
        [],
        low, mid, top, wave_low, wave_mid, wave_top, mass_low, mass_mid, mass_top,
        above, below, kinetic, coefficient, center, halfwidth,
    )
    above = passed_along(face_down, "cells", -1)
    before, done_top, alone = call(
        lambda *refs: second_rest_kernel(vectors, *refs),
        "second_rest",
        (shape(table_rows, 256), rows(25), shape(vectors, owned, kind=BF16)),
        "v" * 9 + "hss",
        [scratch_rows(75), scratch_rows(25), wave_scratch, pltpu.SemaphoreType.DMA((1,))],
        values, kinetic, coefficient, low, mass_mid, mass_top, base_mid, base_top, conn,
        wave_block, center, halfwidth,
    )
    rounded = call(
        lambda *refs: scatter_top_kernel(vectors, *refs),
        "scatter_top",
        shape(parts, vectors, owned // parts, kind=BF16),
        "vvvvvvs",
        [pltpu.VMEM((table_rows, 256), F32)],
        conn, before, done_top, mass_top, above, alone, halfwidth,
    )
    quarter = lax.all_to_all(rounded, "vecs", split_axis=0, concat_axis=0, tiled=True)
    quarter = quarter.reshape(parts * vectors, owned // parts)
    total_vectors = parts * vectors
    share = earlier_vectors.shape[0] // devices
    half, peers = share // 2, devices // cores
    core = (lax.axis_index("cells") % cores).astype(I32).reshape(1)
    pair = [(i, i ^ 1) for i in range(cells)]
    same_core = [
        [(cores * block + k) * parts + part for block in range(cells // cores) for part in range(parts)]
        for k in range(cores)
    ]
    sent = shape(peers * half, 2 * total_vectors)
    blocks = math.gcd(8, peers // parts)
    earlier_scratch = [
        pltpu.VMEM(earlier_vectors.shape, BF16), pltpu.SemaphoreType.DMA((blocks,))
    ]
    keep, send = call(
        lambda *refs: project_kernel(cores, parts, share, *refs),
        "project", (sent, sent), "hvs", earlier_scratch, earlier_vectors, quarter, core,
    )
    shares = (keep + lax.ppermute(send, "cells", pair)).reshape(peers, half, 2 * total_vectors)
    shares = lax.all_to_all(
        shares, AXES, split_axis=0, concat_axis=0, tiled=True, axis_index_groups=same_core
    )
    own = jnp.sum(shares, 0)
    own_rows = own.reshape(half, 2, total_vectors).transpose(1, 0, 2).reshape(share, total_vectors)
    mine = jnp.broadcast_to(own.astype(BF16)[None], (peers, half, 2 * total_vectors))
    mine = lax.all_to_all(
        mine, AXES, split_axis=0, concat_axis=0, tiled=True, axis_index_groups=same_core
    )
    theirs = lax.ppermute(mine, "cells", pair)
    filtered = call(
        lambda *refs: filter_kernel(cores, parts, share, *refs),
        "filter",
        shape(total_vectors, owned // parts),
        "vvhvs",
        [pltpu.VMEM((devices * share, total_vectors), BF16)] + earlier_scratch,
        mine, theirs, earlier_vectors, quarter, core,
    )
    return (filtered, own_rows)


def solution(mesh):
    in_specs = (
        P("vecs", "cells"),
        P(None, "cells"),
        P("cells"),
        P("cells"),
        P("cells"),
        P(None, "cells"),
        P("cells"),
        P(),
        P(),
        P(None, AXES),
    )
    out_specs = (P(None, AXES), P(AXES, None))
    return jax.shard_map(
        per_device, mesh=mesh, in_specs=in_specs, out_specs=out_specs, check_vma=False
    )
```

time: 649 us -> 114 us (0.18)
  waiting for transfers between devices: 258 us -> 8.01 us
  other arithmetic: 214 us -> 0.18 us
  local copies, waits for them, and re-layouts: 123 us -> 0.72 us
  blocking collectives: 9.69 us -> 47.4 us
  Pallas kernels: 0 us -> 34.3 us
  matrix products: 14.4 us -> 0 us
  between operations: 16.2 us -> 2.85 us
  starting transfers between devices: 11.8 us -> 19.9 us
    psum x1 -> x0, waiting for transfers between devices: 254 us -> none  [per_device(): projections = lax.psum(partial_sum, ('cells', 'vecs'))]
    scatter-add x4 -> x0, other arithmetic: 209 us -> none  [the longest x2 181 us: cell_sum(): return jnp.zeros((columns, owned_count + ghost_count), jnp.float32).at[:,...]
    gather x8 -> x0, local copies, waits for them, and re-layouts: 80.9 us -> none  [the longest x4 73.2 us: cell_sum(): values = extended[:, cells_conn].astype(jnp.bfloat16)]
    all_to_all x1 -> x2, blocking collectives: 9.69 us -> 47.4 us  [the longest x1 29.6 us: per_device(): lax.all_to_all(shares, AXES, split_axis=0, concat_axis=0, tiled=True, axi...]
    pallas_call x0 -> x9, Pallas kernels: none -> 34.3 us  [call(): pl.pallas_call(kernel, out_shape=out_shape, in_specs=[{'v': VMEM_SPEC, 's...]
    add x2 -> x0, local copies, waits for them, and re-layouts: 15.1 us -> none  [cell_sum(): kin_part[None, None, :] * stiff_part]
    dot_general x4 -> x0, matrix products: 14.4 us -> none  [the longest x1 7.41 us: per_device(): lax.dot_general(earlier_vectors, quarter, (((1,), (1,)), ((), ())), prefe...]
    slice x4 -> x0, local copies, waits for them, and re-layouts: 10.1 us -> none  [the longest x2 7.9 us: apply_operator(): summed = slot_sums[:, :owned_count].at[:, send_list].add(returned)]
  transfers between devices with their start and end apart: 5 -> 7, of which waited for: 4 -> 3; matrix products, arithmetic and copies ran while one was open for 2% -> 1% of each run, Pallas kernels for 0% -> 11%
where the time goes in v2:
time: 114 us; the launch traced here: 113 us
  blocking collectives  47.4 us (42%)
  Pallas kernels  34.3 us (30%)
  starting transfers between devices  19.9 us (17%)
  waiting for transfers between devices  8.01 us (7%)
  between operations  2.85 us (2%)
    pallas_call x9, Pallas kernels, call(): pl.pallas_call(kernel, out_shape=out_shape, in_specs=[{'v': VMEM_SPEC, 's...  34.3 us
    all_to_all x1, blocking collectives, per_device(): lax.all_to_all(shares, AXES, split_axis=0, concat_axis=0, tiled=True, axi...  29.6 us
    all_to_all x1, blocking collectives, per_device(): lax.all_to_all(mine, AXES, split_axis=0, concat_axis=0, tiled=True, axis_...  17.8 us
    ppermute x4, starting transfers between devices, passed_along(): lax.ppermute(value, axis, [(source, source + steps) for source in range(l...  12.6 us
    all_to_all x1, waiting for transfers between devices, per_device(): lax.all_to_all(rounded, 'vecs', split_axis=0, concat_axis=0, tiled=True)  6.17 us
    all_to_all x1, starting transfers between devices, per_device(): lax.all_to_all(rounded, 'vecs', split_axis=0, concat_axis=0, tiled=True)  4.19 us
    ppermute x1, starting transfers between devices, per_device(): theirs = lax.ppermute(mine, 'cells', pair)  3.01 us
  transfers between devices with their start and end apart: 7, of which 3 were waited for; matrix products, arithmetic and copies ran while one was open for 1% of the time, Pallas kernels for 11%

profile of v2, /device:TPU:1, one launch (start us, length us, event | category | flops | bytes accessed | tf_op | source)
XLA Modules:
  0.0 113.3 jit_solution(5392377685727713851)
XLA Ops:
  0.6 3.5 %gather_face.1 = (bf16[624,512]{1,0:T(8,128)(2,1)S(1)}, s32[125,128]{1,0:T(8,128)S(1)}, f32[25,16,128]{2,1,0:T(8,128)S(1)}, f32[25,128]{1,0:T(8,128)S(1)}, f32[13,24,128]{2,1,0:T(8,128)S(1)}) custom-call(s32[125,128]{1,0:T(8,128)} %refs_0_.2, f32[16,9216]{1,0:T(8,128)} %refs_9_.1, f32[72,128]{1,0:T(8,128)} %bitcast.18), custom_call_target="tpu_custom_call" | custom-call | tf_op jit(solution)/shard_map/gather_face/pallas_call | solution.py:537
  4.2 4.9 %collective-permute-start = (f32[13,24,128]{2,1,0:T(8,128)S(1)}, f32[13,24,128]{2,1,0:T(8,128)S(1)}, u32[]{:S(2)}, u32[]{:S(2)}) collective-permute-start(f32[13,24,128]{2,1,0:T(8,128)S(1)} %get-tuple-element.34), channel_id=1, source_target_pairs={{0,4},{4,8},{8,12},{12,16},{16,20},{20,24},{24,28},{28,32},{32,36}... | collective-permute-start | bytes 479240 | tf_op jit(solution)/shard_map/ppermute | solution.py:554
  9.8 6.6 %gather_rest.1 = (f32[75,16,128]{2,1,0:T(8,128)S(1)}, f32[75,128]{1,0:T(8,128)S(1)}, f32[8,128]{1,0:T(8,128)S(1)}, f32[125,128]{1,0:T(8,128)S(1)}) custom-call(bf16[624,512]{1,0:T(8,128)(2,1)S(1)} %get-tuple-element.29.refs_0_, s32[125,128]{1,0:T(8,128)S(1)} %get-tuple-element.28.refs_1_.refs_8_.refs_0_, f32[125,128]{1,0:T(8,128)} %refs_2_.2, ...), custom_call_target="tpu_custom_call" | custom-call | tf_op jit(solution)/shard_map/gather_rest/pallas_call | solution.py:537
  16.3 0.0 collective-permute-done.refs_4_
  16.3 1.3 %first_faces.1 = (f32[125,16,128]{2,1,0:T(8,128)S(1)}, f32[25,16,128]{2,1,0:T(8,128)S(1)}, f32[25,128]{1,0:T(8,128)S(1)}, f32[25,16,128]{2,1,0:T(8,128)S(1)}, f3...) custom-call(f32[75,16,128]{2,1,0:T(8,128)S(1)} %get-tuple-element.30.refs_0_.refs_4_, ...), custom_call_target="tpu_custom_call" | custom-call | tf_op jit(solution)/shard_map/first_faces/pallas_call | solution.py:537
  17.6 1.9 %collective-permute-start.1 = (bf16[13,16,128]{2,1,0:T(8,128)(2,1)S(1)}, bf16[13,16,128]{2,1,0:T(8,128)(2,1)S(1)}, u32[]{:S(2)}, u32[]{:S(2)}) collective-permute-start(bf16[13,16,128]{2,1,0:T(8,128)(2,1)S(1)} %get-tuple-element.42), channel_id=1, source_target_pairs={{4,0},{8,4},{12,8},{16,12},{20,16},{24,20},{28,24},{32,28},{36,32}... | collective-permute-start | bytes 159752 | tf_op jit(solution)/shard_map/ppermute | solution.py:554
  19.5 3.6 %collective-permute-start.2 = (bf16[13,16,128]{2,1,0:T(8,128)(2,1)S(1)}, bf16[13,16,128]{2,1,0:T(8,128)(2,1)S(1)}, u32[]{:S(2)}, u32[]{:S(2)}) collective-permute-start(bf16[13,16,128]{2,1,0:T(8,128)(2,1)S(1)} %get-tuple-element.43), channel_id=1, source_target_pairs={{0,4},{4,8},{8,12},{12,16},{16,20},{20,24},{24,28},{28,32},{32,36}... | collective-permute-start | bytes 159752 | tf_op jit(solution)/shard_map/ppermute | solution.py:554
  24.5 1.1 first_rest.1.refs_1_
  25.6 0.0 collective-permute-done.1.refs_9_
  25.6 0.0 collective-permute-done.2.refs_10_
  25.6 1.3 %second_faces.1 = (f32[125,16,128]{2,1,0:T(8,128)S(1)}, f32[75,16,128]{2,1,0:T(8,128)S(1)}, f32[25,16,128]{2,1,0:T(8,128)S(1)}, f32[25,16,128]{2,1,0:T(8,128)S(1)}, bf16[13,16,128]{2,1,0:T(8,128)(2,1)S(1)}) custom-call(f32[25,16,128]{2,1,0:T(8,128)S(1)} %get-tuple-element.37.refs_0_, f32[75,16,128]{2,1,0:T(8,128)S(1)} %first_rest.1.refs_1_, ...), custom_call_target="tpu_custom_call" | custom-call | tf_op jit(solution)/shard_map/second_faces/pallas_call | solution.py:537
  26.9 2.1 %collective-permute-start.3 = (bf16[13,16,128]{2,1,0:T(8,128)(2,1)S(1)}, bf16[13,16,128]{2,1,0:T(8,128)(2,1)S(1)}, u32[]{:S(2)}, u32[]{:S(2)}) collective-permute-start(bf16[13,16,128]{2,1,0:T(8,128)(2,1)S(1)} %get-tuple-element.50), channel_id=1, source_target_pairs={{4,0},{8,4},{12,8},{16,12},{20,16},{24,20},{28,24},{32,28},{36,32}... | collective-permute-start | bytes 159752 | tf_op jit(solution)/shard_map/ppermute | solution.py:554
  29.1 4.8 %second_rest.1 = (f32[624,256]{1,0:T(8,128)S(1)}, f32[25,16,128]{2,1,0:T(8,128)S(1)}, bf16[16,9216]{1,0:T(8,128)(2,1)S(1)}) custom-call(f32[125,16,128]{2,1,0:T(8,128)S(1)} %get-tuple-element.44.refs_0_, f32[8,128]{1,0:T(8,128)S(1)} %get-tuple-element.35.refs_5_.refs_1_.refs_11_, f32[125,128]{1,0:T(8,128)S(1)} %get-tuple-element.36.refs_6_.refs_2_.refs_12_, ...), custom_call_target="tpu_custom_call" | custom-call | tf_op jit(solution)/shard_map/second_rest/pallas_call | solution.py:537
  33.9 0.0 collective-permute-done.3.refs_4_
  33.9 2.1 %scatter_top.1 = bf16[4,16,2304]{2,1,0:T(8,128)(2,1)} custom-call(s32[125,128]{1,0:T(8,128)S(1)} %get-tuple-element.28.refs_1_.refs_8_.refs_0_, f32[624,256]{1,0:T(8,128)S(1)} %get-tuple-element.48.refs_1_, f32[25,16,128]{2,1,0:T(8,128)S(1)} %get-tuple-element.49.refs_2_, f32[25,128]{1,0:T(8,128)S(1)} %get-tuple-element.33.refs_3_.refs_8_.refs_5_, ...), custom_call_target="tpu_custom_call" | custom-call | tf_op jit(solution)/shard_map/scatter_top/pallas_call | solution.py:537
  36.0 4.2 %all-to-all-start = ((bf16[4,16,2304]{2,1,0:T(8,128)(2,1)}), bf16[4,16,2304]{2,1,0:T(8,128)(2,1)S(1)}, u32[]{:S(2)}, u32[]{:S(2)}) async-start(bf16[4,16,2304]{2,1,0:T(8,128)(2,1)} %scatter_top.1), calls=%async_computation | async-start | bytes 589824 | tf_op jit(solution)/shard_map/all_to_all | solution.py:642
  40.2 6.2 %all-to-all-done = bf16[4,16,2304]{2,1,0:T(8,128)(2,1)S(1)} async-done(((bf16[4,16,2304]{2,1,0:T(8,128)(2,1)}), bf16[4,16,2304]{2,1,0:T(8,128)(2,1)S(1)}, u32[]{:S(2)}, u32[]{:S(2)}) %all-to-all-start) | async-done | bytes 294944 | tf_op jit(solution)/shard_map/all_to_all | solution.py:642
  46.4 8.4 %project.1 = (f32[512,128]{1,0:T(8,128)S(1)}, f32[512,128]{1,0:T(8,128)S(1)}) custom-call(bf16[2048,2304]{1,0:T(8,128)(2,1)} %refs_2_.3, bf16[64,2304]{1,0:T(8,128)(2,1)S(1)} %bitcast.15, s32[1]{0:T(128)} %bitcast.5.refs_2_.refs_4_), custom_call_target="tpu_custom_call" | custom-call | tf_op jit(solution)/shard_map/project/pallas_call | solution.py:537
  54.8 0.1 collective-permute-start.4
  54.9 1.5 %collective-permute-done.4 = f32[512,128]{1,0:T(8,128)S(1)} collective-permute-done((f32[512,128]{1,0:T(8,128)S(1)}, f32[512,128]{1,0:T(8,128)S(1)}, u32[]{:S(2)}, u32[]{:S(2)}) %collective-permute-start.4) | collective-permute-done | bytes 262176 | tf_op jit(solution)/shard_map/ppermute | solution.py:662
  56.5 29.6 %all_to_all.15 = f32[128,4,128]{2,1,0:T(4,128)S(1)} all-to-all(f32[128,4,128]{2,1,0:T(4,128)S(1)} %bitcast.17), channel_id=1, replica_groups={{0,1,2,3,8,9,10,11,16,17,18,19,24,25,26,27,32,33,34,35,40,41,42,43,48,4..., dimensions={0} | all-to-all | bytes 524288 | tf_op jit(solution)/shard_map/all_to_all | solution.py:663
  86.1 0.1 reduce_sum.9
  86.3 17.8 %all_to_all.16.refs_0_ = bf16[128,4,128]{2,1,0:T(4,128)(2,1)S(1)} all-to-all(bf16[128,4,128]{2,1,0:T(4,128)(2,1)S(1)} %broadcast_in_dim.2), channel_id=1, replica_groups={{0,1,2,3,8,9,10,11,16,17,18,19,24,25,26,27,32,33,34,35,40,41,42,43,48,4..., dimensions={0} | all-to-all | bytes 262144 | tf_op jit(solution)/shard_map/all_to_all | solution.py:669
  104.0 3.0 %collective-permute-start.5 = (bf16[128,4,128]{2,1,0:T(4,128)(2,1)S(1)}, bf16[128,4,128]{2,1,0:T(4,128)(2,1)S(1)}, u32[]{:S(2)}, u32[]{:S(2)}) collective-permute-start(bf16[128,4,128]{2,1,0:T(4,128)(2,1)S(1)} %all_to_all.16.refs_0_), channel_id=1, source_target_pairs={{0,4},{4,0},{8,12},{12,8},{16,20},{20,16},{24,28},{28,24},{32,36},... | collective-permute-start | bytes 393224 | tf_op jit(solution)/shard_map/ppermute | solution.py:672
  107.0 0.1 reshape.41
  107.1 0.6 copy.11
  107.7 0.3 collective-permute-done.5.refs_1_
  108.0 5.1 %filter.1 = f32[64,2304]{1,0:T(8,128)} custom-call(bf16[128,4,128]{2,1,0:T(4,128)(2,1)S(1)} %all_to_all.16.refs_0_, bf16[128,4,128]{2,1,0:T(4,128)(2,1)S(1)} %collective-permute-done.5.refs_1_, bf16[2048,2304]{1,0:T(8,128)(2,1)} %refs_2_.3, bf16[64,2304]{1,0:T(8,128)(2,1)S(1)} %bitcast.16, s32[1]{0:T(128)} %bitcast.5.refs_2_.refs_4_), custom_call_target="tpu_custom_call" | custom-call | tf_op jit(solution)/shard_map/filter/pallas_call | solution.py:537
  (3 shorter events, 0.1 us)
Async XLA Ops:
  4.2 12.2 %collective-permute-start = (f32[13,24,128]{2,1,0:T(8,128)S(1)}, f32[13,24,128]{2,1,0:T(8,128)S(1)}, u32[]{:S(2)}, u32[]{:S(2)}) collective-permute-start(f32[13,24,128]{2,1,0:T(8,128)S(1)} %get-tuple-element.34), channel_id=1, source_target_pairs={{0,4},{4,8},{8,12},{12,16},{16,20},{20,24},{24,28},{28,32},{32,36}... | collective-permute-start | bytes 479240 | tf_op jit(solution)/shard_map/ppermute | solution.py:554
  17.6 8.0 %collective-permute-start.1 = (bf16[13,16,128]{2,1,0:T(8,128)(2,1)S(1)}, bf16[13,16,128]{2,1,0:T(8,128)(2,1)S(1)}, u32[]{:S(2)}, u32[]{:S(2)}) collective-permute-start(bf16[13,16,128]{2,1,0:T(8,128)(2,1)S(1)} %get-tuple-element.42), channel_id=1, source_target_pairs={{4,0},{8,4},{12,8},{16,12},{20,16},{24,20},{28,24},{32,28},{36,32}... | collective-permute-start | bytes 159752 | tf_op jit(solution)/shard_map/ppermute | solution.py:554
  19.5 6.1 %collective-permute-start.2 = (bf16[13,16,128]{2,1,0:T(8,128)(2,1)S(1)}, bf16[13,16,128]{2,1,0:T(8,128)(2,1)S(1)}, u32[]{:S(2)}, u32[]{:S(2)}) collective-permute-start(bf16[13,16,128]{2,1,0:T(8,128)(2,1)S(1)} %get-tuple-element.43), channel_id=1, source_target_pairs={{0,4},{4,8},{8,12},{12,16},{16,20},{20,24},{24,28},{28,32},{32,36}... | collective-permute-start | bytes 159752 | tf_op jit(solution)/shard_map/ppermute | solution.py:554
  26.9 7.0 %collective-permute-start.3 = (bf16[13,16,128]{2,1,0:T(8,128)(2,1)S(1)}, bf16[13,16,128]{2,1,0:T(8,128)(2,1)S(1)}, u32[]{:S(2)}, u32[]{:S(2)}) collective-permute-start(bf16[13,16,128]{2,1,0:T(8,128)(2,1)S(1)} %get-tuple-element.50), channel_id=1, source_target_pairs={{4,0},{8,4},{12,8},{16,12},{20,16},{24,20},{28,24},{32,28},{36,32}... | collective-permute-start | bytes 159752 | tf_op jit(solution)/shard_map/ppermute | solution.py:554
  36.0 10.4 %all-to-all-start = ((bf16[4,16,2304]{2,1,0:T(8,128)(2,1)}), bf16[4,16,2304]{2,1,0:T(8,128)(2,1)S(1)}, u32[]{:S(2)}, u32[]{:S(2)}) async-start(bf16[4,16,2304]{2,1,0:T(8,128)(2,1)} %scatter_top.1), calls=%async_computation | async-start | bytes 589824 | tf_op jit(solution)/shard_map/all_to_all | solution.py:642
  54.8 1.6 %collective-permute-start.4 = (f32[512,128]{1,0:T(8,128)S(1)}, f32[512,128]{1,0:T(8,128)S(1)}, u32[]{:S(2)}, u32[]{:S(2)}) collective-permute-start(f32[512,128]{1,0:T(8,128)S(1)} %get-tuple-element.53), channel_id=1, source_target_pairs={{0,4},{4,0},{8,12},{12,8},{16,20},{20,16},{24,28},{28,24},{32,36},... | collective-permute-start | bytes 786440 | tf_op jit(solution)/shard_map/ppermute | solution.py:662
  104.0 4.0 %collective-permute-start.5 = (bf16[128,4,128]{2,1,0:T(4,128)(2,1)S(1)}, bf16[128,4,128]{2,1,0:T(4,128)(2,1)S(1)}, u32[]{:S(2)}, u32[]{:S(2)}) collective-permute-start(bf16[128,4,128]{2,1,0:T(4,128)(2,1)S(1)} %all_to_all.16.refs_0_), channel_id=1, source_target_pairs={{0,4},{4,0},{8,12},{12,8},{16,20},{20,16},{24,28},{28,24},{32,36},... | collective-permute-start | bytes 393224 | tf_op jit(solution)/shard_map/ppermute | solution.py:672

commit v3 on v2

--- a/solution.py
+++ b/solution.py
@@ -11,6 +11,7 @@
 F32, BF16, I32 = jnp.float32, jnp.bfloat16, jnp.int32
 AXES = ("cells", "vecs")
 LANES = 128
+BLOCKS = 8
 VMEM_LIMIT = 20 * 2**20
 
 
@@ -147,14 +148,80 @@
     return jnp.where(place == within, BF16(1), BF16(0))
 
 
-def gather_rows(vectors, groups, rows, conn, table, wave, mass):
+AXIS_MASK = (1 + 8 + 32, 2 + 16 + 64)
+
+
+def place_bits(place, axis):
+    return [(place & 1) + (place & 2) * 4 + (place & 4) * 8, (place & 1) * 2 + (place & 2) * 8 + (place & 4) * 16][axis]
+
+
+def tile_plan(layers):
+    tiles = [("all", [node(a, b, c)]) for a in range(4) for b in range(4) for c in layers]
+    for axis in range(2):
+        rows = [
+            node(4, k, c) if axis == 0 else node(k, 4, c)
+            for k in range(5 - axis)
+            for c in layers
+        ]
+        tiles += [(axis, rows[i : i + 8]) for i in range(0, len(rows), 8)]
+    return tiles
+
+
+MID_PLAN, TOP_PLAN = tile_plan((1, 2, 3)), tile_plan((4,))
+
+
+def tile_groups(plan):
+    count = len(plan)
+    fives = count % 4
+    sizes = [5] * fives + [4] * ((count - 5 * fives) // 4)
+    starts = np.cumsum([0] + sizes)
+    return [(int(start), size) for start, size in zip(starts, sizes)]
+
+
+def pack_tile(kind, rows, load, empty):
+    if kind == "all":
+        return load(rows[0])
+    lane = lane_index(8)
+    place, last = axis_place(lane, kind), lane | AXIS_MASK[kind]
+    tile = jnp.full((8, LANES), empty)
+    for i, j in enumerate(rows):
+        tile = jnp.where(place == i, pick(load(j), last), tile)
+    return tile
+
+
+def repeated_places(kind, rows):
+    return [i for i, j in enumerate(rows) if kind == 0 and j // 5 == 24]
+
+
+def pack_slots(plan, conn, slots):
+    def load(j):
+        return jnp.broadcast_to(conn[j : j + 1, :], (8, LANES))
+
+    for i, (kind, rows) in enumerate(plan):
+        tile = pack_tile(kind, rows, load, jnp.int32(65535))
+        slots[i : i + 1, :] = tile[0:1, :]
+
+
+def unpack_tiles(plan, extra, load, store):
+    lane = lane_index(8)
+    for axis in (1, 0):
+        after, has_after = above_of(lane, axis)
+        for i, (kind, rows) in enumerate(plan):
+            if kind != axis:
+                continue
+            tile = extra(i)
+            for place, j in enumerate(rows):
+                source = (lane & ~AXIS_MASK[axis]) | place_bits(place, axis)
+                inner = pick(load(j - (100 if axis == 0 else 20)), after)
+                store(j, jnp.where(has_after, inner, pick(tile, source)))
+
+
+def gather_rows(vectors, groups, plan, row_of, slots_ref, table, wave, mass, wave_extra, mass_extra):
     base = vectors * groups
-    start = 0
-    while start < len(rows):
-        count = 5 if len(rows) - start == 5 else min(4, len(rows) - start)
+    whole = sum(kind == "all" for kind, _ in plan)
+    for start, count in tile_groups(plan):
         width = count * LANES
-        chunk = rows[start : start + count]
-        slots = jnp.concatenate([conn[j : j + 1, :] for j in chunk], 1)
+        slots = jnp.concatenate([slots_ref[start + i : start + i + 1, :] for i in range(count)], 1)
         chosen = one_hot(slots, width)
         found = jnp.dot(
             table[...], jnp.concatenate([chosen, chosen], 0), preferred_element_type=F32
@@ -168,14 +235,45 @@
         mine = group_row == jnp.broadcast_to(group, (groups, width))
         line = jnp.sum(jnp.where(mine, found[base : base + groups], 0.0), 0, keepdims=True)
         for i in range(count):
-            wave[start + i] = total[:, LANES * i : LANES * (i + 1)]
-            mass[start + i : start + i + 1, :] = line[:, LANES * i : LANES * (i + 1)]
-        start += count
+            kind, rows = plan[start + i]
+            columns = slice(LANES * i, LANES * (i + 1))
+            if kind == "all":
+                row = row_of(rows[0])
+                wave[row] = total[:, columns]
+                mass[row : row + 1, :] = line[:, columns]
+            else:
+                wave_extra[start + i - whole] = total[:, columns]
+                mass_extra[start + i - whole] = jnp.broadcast_to(line[:, columns], (8, LANES))
+    for half in range(vectors // 8):
+        part = slice(8 * half, 8 * (half + 1))
+
+        def store(j, value):
+            wave[row_of(j), part, :] = value
+
+        unpack_tiles(
+            plan, lambda i: wave_extra[i - whole, part, :], lambda j: wave[row_of(j), part, :], store
+        )
+
+    def store_line(j, value):
+        mass[row_of(j) : row_of(j) + 1, :] = value[0:1, :]
+
+    def load_line(j):
+        return jnp.broadcast_to(mass[row_of(j) : row_of(j) + 1, :], (8, LANES))
+
+    unpack_tiles(plan, lambda i: mass_extra[i - whole], load_line, store_line)
+
+
+def mid_row(j):
+    return 3 * (j // 5) + j % 5 - 1
+
+
+def top_row(j):
+    return j // 5
 
 
 def gather_face_kernel(
-    vectors, conn_hbm, wave_hbm, mass_hbm, table, conn, wave_top, mass_top, face_out,
-    wave_in, mass_in, sems,
+    vectors, conn_hbm, wave_hbm, mass_hbm, table, conn, slots, wave_top, mass_top, face_out,
+    wave_in, mass_in, wave_extra, mass_extra, sems,
 ):
     copies = [
         pltpu.make_async_copy(wave_hbm, wave_in, sems.at[0]),
@@ -199,7 +297,10 @@
         table[base:, columns] = jnp.concatenate([high.astype(F32), spare], 0).astype(BF16)
         columns = slice(256 + LANES * half, 256 + LANES * (half + 1))
         table[base:, columns] = jnp.concatenate([low.astype(F32), spare], 0).astype(BF16)
-    gather_rows(vectors, groups, TOP_ROWS, conn, table, wave_top, mass_top)
+    pack_slots(TOP_PLAN, conn, slots)
+    gather_rows(
+        vectors, groups, TOP_PLAN, top_row, slots, table, wave_top, mass_top, wave_extra, mass_extra
+    )
     upper, upper_one = upper_lanes(vectors), upper_lanes(1)
     for i in range(13):
         second = min(2 * i + 1, 24)
@@ -214,7 +315,7 @@
 
 def gather_rest_kernel(
     vectors, groups, table, conn, potential_hbm, levels_hbm, live_ref,
-    wave_mid, mass_mid, kinetic, coefficient, levels_in, sems,
+    slots, wave_mid, mass_mid, kinetic, coefficient, levels_in, wave_extra, mass_extra, sems,
 ):
     copies = [
         pltpu.make_async_copy(potential_hbm, coefficient, sems.at[0]),
@@ -222,7 +323,10 @@
     ]
     for copy in copies:
         copy.start()
-    gather_rows(vectors, groups, MID_ROWS, conn, table, wave_mid, mass_mid)
+    pack_slots(MID_PLAN, conn, slots)
+    gather_rows(
+        vectors, groups, MID_PLAN, mid_row, slots, table, wave_mid, mass_mid, wave_extra, mass_extra
+    )
     copies[0].wait()
     copies[1].wait()
     size = jnp.exp2(-levels_in[...].astype(F32))
@@ -355,28 +459,26 @@
     pack_lower(low_out, face_down, vectors)
 
 
-def kept_lanes(ab):
-    lane = lane_index(1)
-    keep = None
-    if ab // 5 == 4:
-        keep = axis_place(lane, 0) == 7
-    if ab % 5 == 4:
-        last = axis_place(lane, 1) == 7
-        keep = last if keep is None else jnp.logical_and(keep, last)
-    return keep
-
-
-def scatter_rows(vectors, groups, rows, conn, value_of, total):
-    start = 0
-    while start < len(rows):
-        count = 5 if len(rows) - start == 5 else min(4, len(rows) - start)
+def scatter_rows(vectors, groups, plan, slots_ref, load, total):
+    for start, count in tile_groups(plan):
         width = count * LANES
-        pieces, slots = [], []
-        for j in rows[start : start + count]:
-            keep, slot = kept_lanes(j // 5), conn[j : j + 1, :]
-            slots.append(slot if keep is None else jnp.where(keep, slot, 65535))
-            pieces.append(value_of(j).astype(BF16))
-        value, slot = jnp.concatenate(pieces, 1), jnp.concatenate(slots, 1)
+        pieces = []
+        for kind, rows in plan[start : start + count]:
+            halves = []
+            for half in range(vectors // 8):
+                part = slice(8 * half, 8 * (half + 1))
+                halves.append(pack_tile(kind, rows, lambda j: load(j, part), jnp.float32(0)))
+            pieces.append(jnp.concatenate(halves, 0).astype(BF16))
+        value = jnp.concatenate(pieces, 1)
+        slots = []
+        for i in range(count):
+            slot = slots_ref[start + i : start + i + 1, :]
+            for place in repeated_places(*plan[start + i]):
+                lane = lane_index(1)
+                again = jnp.logical_and(axis_place(lane, 0) == place, axis_place(lane, 1) < 7)
+                slot = jnp.where(again, 65535, slot)
+            slots.append(slot)
+        slot = jnp.concatenate(slots, 1)
         group = slot >> 8
         wide = jnp.broadcast_to(group.astype(F32).astype(BF16), (vectors, width))
         spread = [jnp.where(wide == BF16(h), value, BF16(0)) for h in range(groups)]
@@ -394,15 +496,22 @@
             total[...] = moved
         else:
             total[...] += moved
-        start += count
 
 
 def second_rest_kernel(
-    vectors, values, kinetic, coefficient, low, mass_mid, mass_top, base_mid, base_top, conn,
-    wave_hbm, center_ref, halfwidth_ref, total, done_top, alone, mid, top, wave_in, sems,
+    vectors, values, kinetic, coefficient, low, mass_mid, mass_top, base_mid, base_top, slots,
+    wave_hbm, earlier_hbm, center_ref, halfwidth_ref,
+    total, done_top, alone, *rest,
 ):
+    earlier, (mid, top, wave_in, sems) = rest[:-4], rest[-4:]
     copy = pltpu.make_async_copy(wave_hbm, wave_in, sems.at[0])
     copy.start()
+    loads = []
+    for i, part in enumerate(earlier):
+        size = part.shape[0]
+        source = earlier_hbm.at[size * i : size * (i + 1), :]
+        loads.append(pltpu.make_async_copy(source, part, sems.at[1 + i]))
+        loads[-1].start()
     groups = wave_in.shape[1] // 256
     center = center_ref[0]
     inverse = 1.0 / jnp.full((1, LANES), halfwidth_ref[0], F32)
@@ -416,11 +525,12 @@
         line = (2.0 * inverse) * mass_top[ab : ab + 1, :]
         done_top[ab] = base_top[ab] + line * joined
 
-    def value_of(j):
-        row = 3 * (j // 5) + j % 5 - 1
-        return base_mid[row] + (2.0 * inverse) * mass_mid[row : row + 1, :] * mid[row]
-
-    scatter_rows(vectors, groups, MID_ROWS, conn, value_of, total)
+    def load(j, part):
+        row = mid_row(j)
+        line = (2.0 * inverse) * mass_mid[row : row + 1, :]
+        return base_mid[row, part, :] + line * mid[row, part, :]
+
+    scatter_rows(vectors, groups, MID_PLAN, slots, load, total)
     copy.wait()
     wide_inverse = jnp.concatenate([inverse, inverse], 1)
     for h in range(groups):
@@ -429,78 +539,98 @@
         alone[:, 256 * h : 256 * (h + 1)] = (
             (-2.0 * center) * wide_inverse * one - wave
         ).astype(BF16)
+    for load in loads:
+        load.wait()
 
 
 def scatter_top_kernel(
-    vectors, conn, before, done_top, mass_top, above, alone, halfwidth_ref, out_ref, total
+    vectors, slots, before, done_top, mass_top, above, alone, halfwidth_ref, *rest
 ):
+    outs, (placed, total) = rest[:-2], rest[-2:]
     groups = alone.shape[1] // 256
     base = vectors * groups
-    upper = upper_lanes(vectors)
+    upper = upper_lanes(8)
     inverse = 1.0 / jnp.full((1, LANES), halfwidth_ref[0], F32)
 
-    def value_of(j):
+    def load(j, part):
         ab = j // 5
-        incoming = from_above(above[ab // 2].astype(F32), ab)
+        incoming = from_above(above[ab // 2].astype(F32)[part], ab)
         share = (2.0 * inverse) * mass_top[ab : ab + 1, :] * incoming
-        return done_top[ab] + jnp.where(upper, share, 0.0)
-
-    scatter_rows(vectors, groups, TOP_ROWS, conn, value_of, total)
-    quarter = groups // out_ref.shape[0]
+        return done_top[ab, part, :] + jnp.where(upper, share, 0.0)
+
+    scatter_rows(vectors, groups, TOP_PLAN, slots, load, total)
+    parts, part = len(outs), lax.axis_index("vecs")
+    quarter = groups // parts
     for h in range(groups):
         rows = slice(vectors * h, vectors * (h + 1))
         count = total[base + h : base + h + 1, :] + before[base + h : base + h + 1, :]
         value = total[rows, :] + before[rows, :]
         own = alone[:, 256 * h : 256 * (h + 1)].astype(F32)
         at = h % quarter
-        out_ref[h // quarter, :, 256 * at : 256 * (at + 1)] = jnp.where(
-            count > 0.5, value, own
-        ).astype(BF16)
-
-
-def stream_rows(earlier_hbm, earlier, sems):
-    count = sems.shape[0]
-    size = earlier.shape[0] // count
-    copies = []
-    for i in range(count):
-        rows = slice(size * i, size * (i + 1))
-        copy = pltpu.make_async_copy(earlier_hbm.at[rows, :], earlier.at[rows, :], sems.at[i])
-        copy.start()
-        copies.append((rows, copy))
-    return copies
-
-
-def project_kernel(
-    cores, parts, share, earlier_hbm, quarter, core_ref, keep, send, earlier, sems
-):
+        away = lax.rem(h // quarter + parts - part, parts)
+        placed[away, :, 256 * at : 256 * (at + 1)] = jnp.where(count > 0.5, value, own).astype(BF16)
+    for away, out in enumerate(outs):
+        out[...] = placed[away]
+
+
+def project_kernel(cores, parts, share, *rest):
+    pieces, earlier, (keep, send, quarter, product) = rest[:parts], rest[parts:-4], rest[-4:]
+    for away, piece in enumerate(pieces):
+        size = piece.shape[0]
+        source = lax.rem(lax.axis_index("vecs") + parts - away, parts)
+        quarter[pl.ds(pl.multiple_of(size * source, size), size), :] = piece[...]
     half = share // 2
-    for i, (rows, copy) in enumerate(stream_rows(earlier_hbm, earlier, sems)):
-        copy.wait()
-        product = lax.dot_general(
-            earlier[rows, :], quarter[...], (((1,), (1,)), ((), ())), preferred_element_type=F32
-        )
-        chunk = product.shape[0] // (cores * parts * share)
-        lines = chunk * parts * half
-        place = slice(lines * i, lines * (i + 1))
-        product = product.reshape(chunk, cores, parts, share, product.shape[-1])
-        for core in range(cores):
-            mine = product[:, core].reshape(chunk * parts, share, product.shape[-1])
-            mine = jnp.concatenate([mine[:, :half], mine[:, half:]], 2)
-            mine = mine.reshape(lines, mine.shape[-1])
-
-            @pl.when(core_ref[0] == core)
-            def _():
-                keep[place, :] = mine
-
-            @pl.when(core_ref[0] != core)
-            def _():
-                send[place, :] = mine
-
-
-def filter_kernel(
-    cores, parts, share, mine, theirs, earlier_hbm, quarter, core_ref, out_ref, low, earlier, sems
-):
-    copies = stream_rows(earlier_hbm, earlier, sems)
+    columns = quarter.shape[0]
+    this_core = lax.rem(lax.axis_index("cells"), cores)
+    product[...] = lax.dot_general(
+        jnp.concatenate([part[...] for part in earlier], 0),
+        quarter[...],
+        (((1,), (1,)), ((), ())),
+        preferred_element_type=F32,
+    )
+    block = parts * share
+
+    def pack(core, out):
+        for i in range(product.shape[0] // (cores * block)):
+            at = (cores * i + core) * block
+            mine = product[at : at + block, :].reshape(parts, share, columns)
+            out[parts * i : parts * (i + 1)] = jnp.concatenate([mine[:, :half], mine[:, half:]], 2)
+
+    for core in range(cores):
+
+        @pl.when(this_core == core)
+        def _():
+            pack(core, keep)
+            pack(1 - core, send)
+
+
+def pair_sum_kernel(parts, keep, received, *rest):
+    outs, placed = rest[:-1], rest[-1]
+    here = lax.axis_index("vecs")
+    total = keep[...] + received[...]
+    total = total.reshape(total.shape[0] // parts, parts, *total.shape[1:])
+    for part in range(parts):
+        placed[lax.rem(part + parts - here, parts)] = total[:, part]
+    for away, out in enumerate(outs):
+        out[...] = placed[away]
+
+
+def part_sum_kernel(*refs):
+    total = refs[0][...]
+    for ref in refs[1:-1]:
+        total = total + ref[...]
+    refs[-1][...] = total
+
+
+def own_rows_kernel(shares, own_rows, spread):
+    own = jnp.sum(shares[...], 0)
+    columns = own.shape[1] // 2
+    own_rows[...] = jnp.concatenate([own[:, :columns], own[:, columns:]], 0)
+    spread[...] = jnp.broadcast_to(own[None], spread.shape).astype(BF16)
+
+
+def filter_kernel(cores, parts, share, mine, theirs, quarter, *rest):
+    earlier, (out_ref, low) = rest[:-2], rest[-2:]
     half = share // 2
     columns = mine.shape[-1] // 2
     block = parts * share
@@ -515,17 +645,21 @@
 
     for core in range(cores):
 
-        @pl.when(core_ref[0] == core)
+        @pl.when(lax.rem(lax.axis_index("cells"), cores) == core)
         def _():
             unpack(mine, core)
             unpack(theirs, 1 - core)
 
-    out_ref[...] = quarter[...].astype(F32)
-    for rows, copy in copies:
-        copy.wait()
-        out_ref[...] -= lax.dot_general(
-            low[rows, :], earlier[rows, :], (((0,), (0,)), ((), ())), preferred_element_type=F32
+    width = 256
+    for i in range(out_ref.shape[1] // width):
+        at = slice(width * i, width * (i + 1))
+        product = lax.dot_general(
+            low[...],
+            jnp.concatenate([part[:, at] for part in earlier], 0),
+            (((0,), (0,)), ((), ())),
+            preferred_element_type=F32,
         )
+        out_ref[:, at] = quarter[:, at].astype(F32) - product
 
 
 VMEM_SPEC = pl.BlockSpec(memory_space=pltpu.VMEM)
@@ -563,6 +697,7 @@
     table_rows = vectors * groups + 48
     cells, parts = lax.axis_size("cells"), lax.axis_size("vecs")
     devices, cores = cells * parts, 2
+    turn = lambda away: [(i, (i + away) % parts) for i in range(parts)]
     center, halfwidth = center.reshape(1), halfwidth.reshape(1)
 
     def shape(*sizes, kind=F32):
@@ -578,24 +713,28 @@
     scratch_rows = lambda count: pltpu.VMEM((count, vectors, LANES), F32)
     wave_scratch = pltpu.VMEM((vectors, owned), F32)
 
-    table, conn, wave_top, mass_top, face = call(
+    extra = lambda count: [scratch_rows(count), pltpu.VMEM((count, 8, LANES), F32)]
+    table, conn, slots_top, wave_top, mass_top, face = call(
         lambda *refs: gather_face_kernel(vectors, *refs),
         "gather_face",
         (
-            shape(table_rows, 512, kind=BF16), shape(125, LANES, kind=I32), rows(25), lines(25),
+            shape(table_rows, 512, kind=BF16), shape(125, LANES, kind=I32),
+            shape(len(TOP_PLAN), LANES, kind=I32), rows(25), lines(25),
             shape(13, vectors + 8, LANES),
         ),
         "hhh",
-        [wave_scratch, pltpu.VMEM((owned // LANES, LANES), F32), pltpu.SemaphoreType.DMA((3,))],
+        [wave_scratch, pltpu.VMEM((owned // LANES, LANES), F32), *extra(2), pltpu.SemaphoreType.DMA((3,))],
         connectivity, wave_block, mass_scale.reshape(owned // LANES, LANES),
     )
     ghost = passed_along(face, "cells", 1)
-    wave_mid, mass_mid, kinetic, coefficient = call(
+    slots_mid, wave_mid, mass_mid, kinetic, coefficient = call(
         lambda *refs: gather_rest_kernel(vectors, groups, *refs),
         "gather_rest",
-        (rows(75), lines(75), lines(8), lines(125)),
+        (
+            shape(len(MID_PLAN), LANES, kind=I32), rows(75), lines(75), lines(8), lines(125),
+        ),
         "vvhhs",
-        [pltpu.VMEM((1, LANES), I32), pltpu.SemaphoreType.DMA((2,))],
+        [pltpu.VMEM((1, LANES), I32), *extra(4), pltpu.SemaphoreType.DMA((2,))],
         table, conn, potential, levels.reshape(1, LANES), live_cells,
     )
     values, wave_low, mass_low, low, top, face_down, face_up = call(
@@ -622,50 +761,70 @@
         above, below, kinetic, coefficient, center, halfwidth,
     )
     above = passed_along(face_down, "cells", -1)
-    before, done_top, alone = call(
+    before, done_top, alone, *earlier = call(
         lambda *refs: second_rest_kernel(vectors, *refs),
         "second_rest",
-        (shape(table_rows, 256), rows(25), shape(vectors, owned, kind=BF16)),
-        "v" * 9 + "hss",
-        [scratch_rows(75), scratch_rows(25), wave_scratch, pltpu.SemaphoreType.DMA((1,))],
-        values, kinetic, coefficient, low, mass_mid, mass_top, base_mid, base_top, conn,
-        wave_block, center, halfwidth,
-    )
-    rounded = call(
+        (
+            shape(table_rows, 256), rows(25), shape(vectors, owned, kind=BF16),
+            *[shape(earlier_vectors.shape[0] // BLOCKS, owned // parts, kind=BF16)] * BLOCKS,
+        ),
+        "v" * 9 + "hhss",
+        [scratch_rows(75), scratch_rows(25), wave_scratch, pltpu.SemaphoreType.DMA((1 + BLOCKS,))],
+        values, kinetic, coefficient, low, mass_mid, mass_top, base_mid, base_top, slots_mid,
+        wave_block, earlier_vectors, center, halfwidth,
+    )
+    pieces = call(
         lambda *refs: scatter_top_kernel(vectors, *refs),
         "scatter_top",
-        shape(parts, vectors, owned // parts, kind=BF16),
+        (shape(vectors, owned // parts, kind=BF16),) * parts,
         "vvvvvvs",
-        [pltpu.VMEM((table_rows, 256), F32)],
-        conn, before, done_top, mass_top, above, alone, halfwidth,
-    )
-    quarter = lax.all_to_all(rounded, "vecs", split_axis=0, concat_axis=0, tiled=True)
-    quarter = quarter.reshape(parts * vectors, owned // parts)
+        [pltpu.VMEM((parts, vectors, owned // parts), BF16), pltpu.VMEM((table_rows, 256), F32)],
+        slots_top, before, done_top, mass_top, above, alone, halfwidth,
+    )
+    pieces = [
+        lax.ppermute(piece, "vecs", turn(away)) if away else piece
+        for away, piece in enumerate(pieces)
+    ]
     total_vectors = parts * vectors
     share = earlier_vectors.shape[0] // devices
     half, peers = share // 2, devices // cores
-    core = (lax.axis_index("cells") % cores).astype(I32).reshape(1)
     pair = [(i, i ^ 1) for i in range(cells)]
     same_core = [
         [(cores * block + k) * parts + part for block in range(cells // cores) for part in range(parts)]
         for k in range(cores)
     ]
-    sent = shape(peers * half, 2 * total_vectors)
-    blocks = math.gcd(8, peers // parts)
-    earlier_scratch = [
-        pltpu.VMEM(earlier_vectors.shape, BF16), pltpu.SemaphoreType.DMA((blocks,))
+    sent = shape(peers, half, 2 * total_vectors)
+    keep, send, quarter = call(
+        lambda *refs: project_kernel(cores, parts, share, *refs),
+        "project",
+        (sent, sent, shape(total_vectors, owned // parts, kind=BF16)),
+        "v" * (parts + BLOCKS),
+        [pltpu.VMEM((earlier_vectors.shape[0], total_vectors), F32)],
+        *pieces, *earlier,
+    )
+    blocks = cells // cores
+    share_shape = shape(blocks, half, 2 * total_vectors)
+    pieces = call(
+        lambda *refs: pair_sum_kernel(parts, *refs),
+        "pair_sum", (share_shape,) * parts, "vv",
+        [pltpu.VMEM((parts,) + share_shape.shape, F32)],
+        keep, lax.ppermute(send, "cells", pair),
+    )
+    pieces = [
+        lax.ppermute(piece, "vecs", turn(away)) if away else piece
+        for away, piece in enumerate(pieces)
     ]
-    keep, send = call(
-        lambda *refs: project_kernel(cores, parts, share, *refs),
-        "project", (sent, sent), "hvs", earlier_scratch, earlier_vectors, quarter, core,
-    )
-    shares = (keep + lax.ppermute(send, "cells", pair)).reshape(peers, half, 2 * total_vectors)
+    shares = call(part_sum_kernel, "part_sum", share_shape, "v" * parts, [], *pieces)
     shares = lax.all_to_all(
-        shares, AXES, split_axis=0, concat_axis=0, tiled=True, axis_index_groups=same_core
-    )
-    own = jnp.sum(shares, 0)
-    own_rows = own.reshape(half, 2, total_vectors).transpose(1, 0, 2).reshape(share, total_vectors)
-    mine = jnp.broadcast_to(own.astype(BF16)[None], (peers, half, 2 * total_vectors))
+        shares, "cells", split_axis=0, concat_axis=0, tiled=True,
+        axis_index_groups=[[cores * block + k for block in range(blocks)] for k in range(cores)],
+    )
+    own_rows, mine = call(
+        own_rows_kernel,
+        "own_rows",
+        (shape(share, total_vectors), shape(peers, half, 2 * total_vectors, kind=BF16)),
+        "v", [], shares,
+    )
     mine = lax.all_to_all(
         mine, AXES, split_axis=0, concat_axis=0, tiled=True, axis_index_groups=same_core
     )
@@ -674,9 +833,9 @@
         lambda *refs: filter_kernel(cores, parts, share, *refs),
         "filter",
         shape(total_vectors, owned // parts),
-        "vvhvs",
-        [pltpu.VMEM((devices * share, total_vectors), BF16)] + earlier_scratch,
-        mine, theirs, earlier_vectors, quarter, core,
+        "vvv" + "v" * BLOCKS,
+        [pltpu.VMEM((devices * share, total_vectors), BF16)],
+        mine, theirs, quarter, *earlier,
     )
     return (filtered, own_rows)
 

time: 114 us -> 101 us (0.89)
  Pallas kernels: 34.3 us -> 23.6 us
  blocking collectives: 47.4 us -> 41.4 us
  starting transfers between devices: 19.9 us -> 25.4 us
    pallas_call x9 -> x12, Pallas kernels: 34.3 us -> 23.6 us  [call(): pl.pallas_call(kernel, out_shape=out_shape, in_specs=[{'v': VMEM_SPEC, 's...]
    ppermute x0 -> x6, starting transfers between devices: none -> 9.25 us  [per_device(): lax.ppermute(piece, 'vecs', turn(away))]
    all_to_all x1 -> x0, waiting for transfers between devices: 6.17 us -> none  [per_device(): lax.all_to_all(rounded, 'vecs', split_axis=0, concat_axis=0, tiled=True)]
    all_to_all x1, blocking collectives: 29.6 us -> 23.7 us  [per_device(): lax.all_to_all(shares, 'cells', split_axis=0, concat_axis=0, tiled=True,...]
    ppermute x0 -> x6, waiting for transfers between devices: none -> 4.98 us  [per_device(): lax.ppermute(piece, 'vecs', turn(away))]
    all_to_all x1 -> x0, starting transfers between devices: 4.19 us -> none  [per_device(): lax.all_to_all(rounded, 'vecs', split_axis=0, concat_axis=0, tiled=True)]
  transfers between devices with their start and end apart: 7 -> 12, of which waited for: 3 -> 7; matrix products, arithmetic and copies ran while one was open for 1% -> 0% of each run, Pallas kernels for 11% -> 10%
where the time goes in v3:
time: 101 us
  blocking collectives  41.4 us (41%)
  starting transfers between devices  25.4 us (25%)
  Pallas kernels  23.6 us (23%)
  waiting for transfers between devices  7.5 us (7%)
  between operations  2.7 us (3%)
    all_to_all x1, blocking collectives, per_device(): lax.all_to_all(shares, 'cells', split_axis=0, concat_axis=0, tiled=True,...  23.7 us
    pallas_call x12, Pallas kernels, call(): pl.pallas_call(kernel, out_shape=out_shape, in_specs=[{'v': VMEM_SPEC, 's...  23.6 us
    all_to_all x1, blocking collectives, per_device(): lax.all_to_all(mine, AXES, split_axis=0, concat_axis=0, tiled=True, axis_...  17.7 us
    ppermute x4, starting transfers between devices, passed_along(): lax.ppermute(value, axis, [(source, source + steps) for source in range(l...  12.4 us
    ppermute x6, starting transfers between devices, per_device(): lax.ppermute(piece, 'vecs', turn(away))  9.25 us
    ppermute x6, waiting for transfers between devices, per_device(): lax.ppermute(piece, 'vecs', turn(away))  4.98 us
    ppermute x1, starting transfers between devices, per_device(): theirs = lax.ppermute(mine, 'cells', pair)  3.62 us
  transfers between devices with their start and end apart: 12, of which 7 were waited for; matrix products, arithmetic and copies ran while one was open for 0% of the time, Pallas kernels for 10%

profile of v3, /device:TPU:1, one launch (start us, length us, event | category | flops | bytes accessed | tf_op | source)
XLA Modules:
  0.0 100.6 jit_solution(3334627966410793472)
XLA Ops:
  0.6 3.2 %gather_face.1 = (bf16[624,512]{1,0:T(8,128)(2,1)S(1)}, s32[125,128]{1,0:T(8,128)S(1)}, s32[18,128]{1,0:T(8,128)S(1)}, f32[25,16,128]{2,1,0:T(8,128)S(1)}, f32[2...) custom-call(s32[125,128]{1,0:T(8,128)} %refs_0_.1, f32[16,9216]{1,0:T(8,128)} %refs_9_.1, f32[72,128]{1,0:T(8,128)} %bitcast.9), custom_call_target="tpu_custom_call" | custom-call | tf_op jit(solution)/shard_map/gather_face/pallas_call | solution.py:671
  3.8 4.9 %collective-permute-start = (f32[13,24,128]{2,1,0:T(8,128)S(1)}, f32[13,24,128]{2,1,0:T(8,128)S(1)}, u32[]{:S(2)}, u32[]{:S(2)}) collective-permute-start(f32[13,24,128]{2,1,0:T(8,128)S(1)} %get-tuple-element.56), channel_id=1, source_target_pairs={{0,4},{4,8},{8,12},{12,16},{16,20},{20,24},{24,28},{28,32},{32,36}... | collective-permute-start | bytes 479240 | tf_op jit(solution)/shard_map/ppermute | solution.py:688
  9.4 4.9 %gather_rest.1 = (s32[52,128]{1,0:T(8,128)S(1)}, f32[75,16,128]{2,1,0:T(8,128)S(1)}, f32[75,128]{1,0:T(8,128)S(1)}, f32[8,128]{1,0:T(8,128)S(1)}, f32[125,128]{1,0:T(8,128)S(1)}) custom-call(bf16[624,512]{1,0:T(8,128)(2,1)S(1)} %get-tuple-element.50.refs_0_, s32[125,128]{1,0:T(8,128)S(1)} %get-tuple-element.51.refs_1_, f32[125,128]{1,0:T(8,128)} %refs_2_.1, ...), custom_call_target="tpu_custom_call" | custom-call | tf_op jit(solution)/shard_map/gather_rest/pallas_call | solution.py:671
  14.3 0.0 collective-permute-done.refs_4_
  14.4 1.3 %first_faces.1 = (f32[125,16,128]{2,1,0:T(8,128)S(1)}, f32[25,16,128]{2,1,0:T(8,128)S(1)}, f32[25,128]{1,0:T(8,128)S(1)}, f32[25,16,128]{2,1,0:T(8,128)S(1)}, f3...) custom-call(f32[75,16,128]{2,1,0:T(8,128)S(1)} %get-tuple-element.52.refs_0_.refs_4_, ...), custom_call_target="tpu_custom_call" | custom-call | tf_op jit(solution)/shard_map/first_faces/pallas_call | solution.py:671
  15.6 1.9 %collective-permute-start.1 = (bf16[13,16,128]{2,1,0:T(8,128)(2,1)S(1)}, bf16[13,16,128]{2,1,0:T(8,128)(2,1)S(1)}, u32[]{:S(2)}, u32[]{:S(2)}) collective-permute-start(bf16[13,16,128]{2,1,0:T(8,128)(2,1)S(1)} %get-tuple-element.64), channel_id=1, source_target_pairs={{4,0},{8,4},{12,8},{16,12},{20,16},{24,20},{28,24},{32,28},{36,32}... | collective-permute-start | bytes 159752 | tf_op jit(solution)/shard_map/ppermute | solution.py:688
  17.6 3.6 %collective-permute-start.2 = (bf16[13,16,128]{2,1,0:T(8,128)(2,1)S(1)}, bf16[13,16,128]{2,1,0:T(8,128)(2,1)S(1)}, u32[]{:S(2)}, u32[]{:S(2)}) collective-permute-start(bf16[13,16,128]{2,1,0:T(8,128)(2,1)S(1)} %get-tuple-element.65), channel_id=1, source_target_pairs={{0,4},{4,8},{8,12},{12,16},{16,20},{20,24},{24,28},{28,32},{32,36}... | collective-permute-start | bytes 159752 | tf_op jit(solution)/shard_map/ppermute | solution.py:688
  22.5 1.1 %first_rest.1.refs_1_ = f32[75,16,128]{2,1,0:T(8,128)S(1)} custom-call(f32[125,16,128]{2,1,0:T(8,128)S(1)} %get-tuple-element.60.refs_0_, f32[8,128]{1,0:T(8,128)S(1)} %get-tuple-element.57.refs_5_.refs_1_.refs_11_, f32[125,128]{1,0:T(8,128)S(1)} %get-tuple-element.58.refs_6_.refs_2_.refs_12_), custom_call_target="tpu_custom_call" | custom-call | tf_op jit(solution)/shard_map/first_rest/pallas_call | solution.py:671
  23.6 0.0 collective-permute-done.1.refs_9_
  23.6 0.0 collective-permute-done.2.refs_10_
  23.6 1.3 %second_faces.1 = (f32[125,16,128]{2,1,0:T(8,128)S(1)}, f32[75,16,128]{2,1,0:T(8,128)S(1)}, f32[25,16,128]{2,1,0:T(8,128)S(1)}, f32[25,16,128]{2,1,0:T(8,128)S(1)}, bf16[13,16,128]{2,1,0:T(8,128)(2,1)S(1)}) custom-call(f32[25,16,128]{2,1,0:T(8,128)S(1)} %get-tuple-element.59.refs_0_, f32[75,16,128]{2,1,0:T(8,128)S(1)} %first_rest.1.refs_1_, ...), custom_call_target="tpu_custom_call" | custom-call | tf_op jit(solution)/shard_map/second_faces/pallas_call | solution.py:671
  25.0 1.9 %collective-permute-start.3 = (bf16[13,16,128]{2,1,0:T(8,128)(2,1)S(1)}, bf16[13,16,128]{2,1,0:T(8,128)(2,1)S(1)}, u32[]{:S(2)}, u32[]{:S(2)}) collective-permute-start(bf16[13,16,128]{2,1,0:T(8,128)(2,1)S(1)} %get-tuple-element.73), channel_id=1, source_target_pairs={{4,0},{8,4},{12,8},{16,12},{20,16},{24,20},{28,24},{32,28},{36,32}... | collective-permute-start | bytes 159752 | tf_op jit(solution)/shard_map/ppermute | solution.py:688
  26.9 4.0 %second_rest.1 = (f32[624,256]{1,0:T(8,128)S(1)}, f32[25,16,128]{2,1,0:T(8,128)S(1)}, bf16[16,9216]{1,0:T(8,128)(2,1)S(1)}, bf16[256,2304]{1,0:T(8,128)(2,1)S(1)...) custom-call(f32[125,16,128]{2,1,0:T(8,128)S(1)} %get-tuple-element.6, ...), custom_call_target="tpu_custom_call" | custom-call | tf_op jit(solution)/shard_map/second_rest/pallas_call | solution.py:671
  30.9 0.0 collective-permute-done.3.refs_4_
  30.9 1.2 %scatter_top.1 = (bf16[16,2304]{1,0:T(8,128)(2,1)S(1)}, bf16[16,2304]{1,0:T(8,128)(2,1)S(1)}, bf16[16,2304]{1,0:T(8,128)(2,1)S(1)}, bf16[16,2304]{1,0:T(8,128)(2,1)S(1)}) custom-call(s32[18,128]{1,0:T(8,128)S(1)} %get-tuple-element.49.refs_0_, f32[624,256]{1,0:T(8,128)S(1)} %get-tuple-element.71.refs_1_, f32[25,16,128]{2,1,0:T(8,128)S(1)} %get-tuple-element.72.refs_2_, ...), custom_call_target="tpu_custom_call" | custom-call | tf_op jit(solution)/shard_map/scatter_top/pallas_call | solution.py:671
  32.1 1.4 %collective-permute-start.4 = (bf16[16,2304]{1,0:T(8,128)(2,1)S(1)}, bf16[16,2304]{1,0:T(8,128)(2,1)S(1)}, u32[]{:S(2)}, u32[]{:S(2)}) collective-permute-start(bf16[16,2304]{1,0:T(8,128)(2,1)S(1)} %get-tuple-element.76), channel_id=1, source_target_pairs={{0,1},{1,2},{2,3},{3,0},{4,5},{5,6},{6,7},{7,4},{8,9},{9,10},{10,1... | collective-permute-start | bytes 221192 | tf_op jit(solution)/shard_map/ppermute | solution.py:785
  33.4 2.6 %collective-permute-start.5 = (bf16[16,2304]{1,0:T(8,128)(2,1)S(1)}, bf16[16,2304]{1,0:T(8,128)(2,1)S(1)}, u32[]{:S(2)}, u32[]{:S(2)}) collective-permute-start(bf16[16,2304]{1,0:T(8,128)(2,1)S(1)} %get-tuple-element.77), channel_id=1, source_target_pairs={{0,2},{1,3},{2,0},{3,1},{4,6},{5,7},{6,4},{7,5},{8,10},{9,11},{10,... | collective-permute-start | bytes 221192 | tf_op jit(solution)/shard_map/ppermute | solution.py:785
  36.1 1.1 %collective-permute-start.6 = (bf16[16,2304]{1,0:T(8,128)(2,1)S(1)}, bf16[16,2304]{1,0:T(8,128)(2,1)S(1)}, u32[]{:S(2)}, u32[]{:S(2)}) collective-permute-start(bf16[16,2304]{1,0:T(8,128)(2,1)S(1)} %get-tuple-element.78), channel_id=1, source_target_pairs={{0,3},{1,0},{2,1},{3,2},{4,7},{5,4},{6,5},{7,6},{8,11},{9,8},{10,9... | collective-permute-start | bytes 221192 | tf_op jit(solution)/shard_map/ppermute | solution.py:785
  37.1 0.5 collective-permute-done.4.refs_1_
  37.6 1.2 %collective-permute-done.5.refs_2_ = bf16[16,2304]{1,0:T(8,128)(2,1)S(1)} collective-permute-done((bf16[16,2304]{1,0:T(8,128)(2,1)S(1)}, bf16[16,2304]{1,0:T(8,128)(2,1)S(1)}, u32[]{:S(2)}, u32[]{:S(2)}) %collective-permute-start.5) | collective-permute-done | bytes 73760 | tf_op jit(solution)/shard_map/ppermute | solution.py:785
  38.8 0.5 collective-permute-done.6.refs_3_
  39.3 3.0 %project.1 = (f32[128,4,128]{2,1,0:T(4,128)S(1)}, f32[128,4,128]{2,1,0:T(4,128)S(1)}, bf16[64,2304]{1,0:T(8,128)(2,1)S(1)}) custom-call(bf16[16,2304]{1,0:T(8,128)(2,1)S(1)} %get-tuple-element.75.refs_0_, bf16[16,2304]{1,0:T(8,128)(2,1)S(1)} %collective-permute-done.4.refs_1_, bf16[16,2304]{1,0:T(8,128)(2,1)S(1)} %collective-permute-done.5.refs_2_, ...), custom_call_target="tpu_custom_call" | custom-call | tf_op jit(solution)/shard_map/project/pallas_call | solution.py:671
  42.2 0.1 collective-permute-start.7
  42.3 1.5 %collective-permute-done.7.refs_1_ = f32[128,4,128]{2,1,0:T(4,128)S(1)} collective-permute-done((f32[128,4,128]{2,1,0:T(4,128)S(1)}, f32[128,4,128]{2,1,0:T(4,128)S(1)}, u32[]{:S(2)}, u32[]{:S(2)}) %collective-permute-start.7) | collective-permute-done | bytes 262176 | tf_op jit(solution)/shard_map/ppermute | solution.py:811
  43.9 0.1 pair_sum.1
  44.0 1.0 %collective-permute-start.8 = (f32[32,4,128]{2,1,0:T(4,128)S(1)}, f32[32,4,128]{2,1,0:T(4,128)S(1)}, u32[]{:S(2)}, u32[]{:S(2)}) collective-permute-start(f32[32,4,128]{2,1,0:T(4,128)S(1)} %get-tuple-element.90), channel_id=1, source_target_pairs={{0,1},{1,2},{2,3},{3,0},{4,5},{5,6},{6,7},{7,4},{8,9},{9,10},{10,1... | collective-permute-start | bytes 196616 | tf_op jit(solution)/shard_map/ppermute | solution.py:814
  45.0 2.5 %collective-permute-start.9 = (f32[32,4,128]{2,1,0:T(4,128)S(1)}, f32[32,4,128]{2,1,0:T(4,128)S(1)}, u32[]{:S(2)}, u32[]{:S(2)}) collective-permute-start(f32[32,4,128]{2,1,0:T(4,128)S(1)} %get-tuple-element.91), channel_id=1, source_target_pairs={{0,2},{1,3},{2,0},{3,1},{4,6},{5,7},{6,4},{7,5},{8,10},{9,11},{10,... | collective-permute-start | bytes 196616 | tf_op jit(solution)/shard_map/ppermute | solution.py:814
  47.5 0.6 collective-permute-start.10
  48.2 0.6 collective-permute-done.8.refs_1_
  48.8 2.2 %collective-permute-done.9.refs_2_ = f32[32,4,128]{2,1,0:T(4,128)S(1)} collective-permute-done((f32[32,4,128]{2,1,0:T(4,128)S(1)}, f32[32,4,128]{2,1,0:T(4,128)S(1)}, u32[]{:S(2)}, u32[]{:S(2)}) %collective-permute-start.9) | collective-permute-done | bytes 65568 | tf_op jit(solution)/shard_map/ppermute | solution.py:814
  51.0 0.0 collective-permute-done.10.refs_3_
  51.1 23.7 %all_to_all.10.shares = f32[32,4,128]{2,1,0:T(4,128)S(1)} all-to-all(f32[32,4,128]{2,1,0:T(4,128)S(1)} %part_sum.1), channel_id=1, replica_groups={{0,8,16,24,32,40,48,56,64,72,80,88,96,104,112,120,128,136,144,152,160,1..., dimensions={0} | all-to-all | bytes 131072 | tf_op jit(solution)/shard_map/all_to_all | solution.py:818
  74.8 0.7 own_rows.1
  75.5 17.7 %all_to_all.11.refs_0_ = bf16[128,4,128]{2,1,0:T(4,128)(2,1)S(1)} all-to-all(bf16[128,4,128]{2,1,0:T(4,128)(2,1)S(1)} %get-tuple-element.93), channel_id=1, replica_groups={{0,1,2,3,8,9,10,11,16,17,18,19,24,25,26,27,32,33,34,35,40,41,42,43,48,4..., dimensions={0} | all-to-all | bytes 262144 | tf_op jit(solution)/shard_map/all_to_all | solution.py:828
  93.2 3.6 %collective-permute-start.11 = (bf16[128,4,128]{2,1,0:T(4,128)(2,1)S(1)}, bf16[128,4,128]{2,1,0:T(4,128)(2,1)S(1)}, u32[]{:S(2)}, u32[]{:S(2)}) collective-permute-start(bf16[128,4,128]{2,1,0:T(4,128)(2,1)S(1)} %all_to_all.11.refs_0_), channel_id=1, source_target_pairs={{0,4},{4,0},{8,12},{12,8},{16,20},{20,16},{24,28},{28,24},{32,36},... | collective-permute-start | bytes 393224 | tf_op jit(solution)/shard_map/ppermute | solution.py:831
  96.8 1.0 collective-permute-done.11.refs_1_
  97.8 2.8 %filter.1 = f32[64,2304]{1,0:T(8,128)} custom-call(bf16[128,4,128]{2,1,0:T(4,128)(2,1)S(1)} %all_to_all.11.refs_0_, bf16[128,4,128]{2,1,0:T(4,128)(2,1)S(1)} %collective-permute-done.11.refs_1_, bf16[64,2304]{1,0:T(8,128)(2,1)S(1)} %get-tuple-element.94.refs_2_, bf16[256,2304]{1,0:T(8,128)(2,1)S(1)} %get-tuple-element.79.refs_4_.refs_3_, ...), custom_call_target="tpu_custom_call" | custom-call | tf_op jit(solution)/shard_map/filter/pallas_call | solution.py:671
  (1 shorter events, 0.0 us)
Async XLA Ops:
  3.8 10.5 %collective-permute-start = (f32[13,24,128]{2,1,0:T(8,128)S(1)}, f32[13,24,128]{2,1,0:T(8,128)S(1)}, u32[]{:S(2)}, u32[]{:S(2)}) collective-permute-start(f32[13,24,128]{2,1,0:T(8,128)S(1)} %get-tuple-element.56), channel_id=1, source_target_pairs={{0,4},{4,8},{8,12},{12,16},{16,20},{20,24},{24,28},{28,32},{32,36}... | collective-permute-start | bytes 479240 | tf_op jit(solution)/shard_map/ppermute | solution.py:688
  15.6 8.0 %collective-permute-start.1 = (bf16[13,16,128]{2,1,0:T(8,128)(2,1)S(1)}, bf16[13,16,128]{2,1,0:T(8,128)(2,1)S(1)}, u32[]{:S(2)}, u32[]{:S(2)}) collective-permute-start(bf16[13,16,128]{2,1,0:T(8,128)(2,1)S(1)} %get-tuple-element.64), channel_id=1, source_target_pairs={{4,0},{8,4},{12,8},{16,12},{20,16},{24,20},{28,24},{32,28},{36,32}... | collective-permute-start | bytes 159752 | tf_op jit(solution)/shard_map/ppermute | solution.py:688
  17.6 6.1 %collective-permute-start.2 = (bf16[13,16,128]{2,1,0:T(8,128)(2,1)S(1)}, bf16[13,16,128]{2,1,0:T(8,128)(2,1)S(1)}, u32[]{:S(2)}, u32[]{:S(2)}) collective-permute-start(bf16[13,16,128]{2,1,0:T(8,128)(2,1)S(1)} %get-tuple-element.65), channel_id=1, source_target_pairs={{0,4},{4,8},{8,12},{12,16},{16,20},{20,24},{24,28},{28,32},{32,36}... | collective-permute-start | bytes 159752 | tf_op jit(solution)/shard_map/ppermute | solution.py:688
  25.0 5.9 %collective-permute-start.3 = (bf16[13,16,128]{2,1,0:T(8,128)(2,1)S(1)}, bf16[13,16,128]{2,1,0:T(8,128)(2,1)S(1)}, u32[]{:S(2)}, u32[]{:S(2)}) collective-permute-start(bf16[13,16,128]{2,1,0:T(8,128)(2,1)S(1)} %get-tuple-element.73), channel_id=1, source_target_pairs={{4,0},{8,4},{12,8},{16,12},{20,16},{24,20},{28,24},{32,28},{36,32}... | collective-permute-start | bytes 159752 | tf_op jit(solution)/shard_map/ppermute | solution.py:688
  32.1 5.6 %collective-permute-start.4 = (bf16[16,2304]{1,0:T(8,128)(2,1)S(1)}, bf16[16,2304]{1,0:T(8,128)(2,1)S(1)}, u32[]{:S(2)}, u32[]{:S(2)}) collective-permute-start(bf16[16,2304]{1,0:T(8,128)(2,1)S(1)} %get-tuple-element.76), channel_id=1, source_target_pairs={{0,1},{1,2},{2,3},{3,0},{4,5},{5,6},{6,7},{7,4},{8,9},{9,10},{10,1... | collective-permute-start | bytes 221192 | tf_op jit(solution)/shard_map/ppermute | solution.py:785
  33.4 5.3 %collective-permute-start.5 = (bf16[16,2304]{1,0:T(8,128)(2,1)S(1)}, bf16[16,2304]{1,0:T(8,128)(2,1)S(1)}, u32[]{:S(2)}, u32[]{:S(2)}) collective-permute-start(bf16[16,2304]{1,0:T(8,128)(2,1)S(1)} %get-tuple-element.77), channel_id=1, source_target_pairs={{0,2},{1,3},{2,0},{3,1},{4,6},{5,7},{6,4},{7,5},{8,10},{9,11},{10,... | collective-permute-start | bytes 221192 | tf_op jit(solution)/shard_map/ppermute | solution.py:785
  36.1 3.2 %collective-permute-start.6 = (bf16[16,2304]{1,0:T(8,128)(2,1)S(1)}, bf16[16,2304]{1,0:T(8,128)(2,1)S(1)}, u32[]{:S(2)}, u32[]{:S(2)}) collective-permute-start(bf16[16,2304]{1,0:T(8,128)(2,1)S(1)} %get-tuple-element.78), channel_id=1, source_target_pairs={{0,3},{1,0},{2,1},{3,2},{4,7},{5,4},{6,5},{7,6},{8,11},{9,8},{10,9... | collective-permute-start | bytes 221192 | tf_op jit(solution)/shard_map/ppermute | solution.py:785
  42.2 1.6 %collective-permute-start.7 = (f32[128,4,128]{2,1,0:T(4,128)S(1)}, f32[128,4,128]{2,1,0:T(4,128)S(1)}, u32[]{:S(2)}, u32[]{:S(2)}) collective-permute-start(f32[128,4,128]{2,1,0:T(4,128)S(1)} %get-tuple-element.88), channel_id=1, source_target_pairs={{0,4},{4,0},{8,12},{12,8},{16,20},{20,16},{24,28},{28,24},{32,36},... | collective-permute-start | bytes 786440 | tf_op jit(solution)/shard_map/ppermute | solution.py:811
  44.0 4.8 %collective-permute-start.8 = (f32[32,4,128]{2,1,0:T(4,128)S(1)}, f32[32,4,128]{2,1,0:T(4,128)S(1)}, u32[]{:S(2)}, u32[]{:S(2)}) collective-permute-start(f32[32,4,128]{2,1,0:T(4,128)S(1)} %get-tuple-element.90), channel_id=1, source_target_pairs={{0,1},{1,2},{2,3},{3,0},{4,5},{5,6},{6,7},{7,4},{8,9},{9,10},{10,1... | collective-permute-start | bytes 196616 | tf_op jit(solution)/shard_map/ppermute | solution.py:814
  45.0 6.0 %collective-permute-start.9 = (f32[32,4,128]{2,1,0:T(4,128)S(1)}, f32[32,4,128]{2,1,0:T(4,128)S(1)}, u32[]{:S(2)}, u32[]{:S(2)}) collective-permute-start(f32[32,4,128]{2,1,0:T(4,128)S(1)} %get-tuple-element.91), channel_id=1, source_target_pairs={{0,2},{1,3},{2,0},{3,1},{4,6},{5,7},{6,4},{7,5},{8,10},{9,11},{10,... | collective-permute-start | bytes 196616 | tf_op jit(solution)/shard_map/ppermute | solution.py:814
  47.5 3.5 %collective-permute-start.10 = (f32[32,4,128]{2,1,0:T(4,128)S(1)}, f32[32,4,128]{2,1,0:T(4,128)S(1)}, u32[]{:S(2)}, u32[]{:S(2)}) collective-permute-start(f32[32,4,128]{2,1,0:T(4,128)S(1)} %get-tuple-element.92), channel_id=1, source_target_pairs={{0,3},{1,0},{2,1},{3,2},{4,7},{5,4},{6,5},{7,6},{8,11},{9,8},{10,9... | collective-permute-start | bytes 196616 | tf_op jit(solution)/shard_map/ppermute | solution.py:814
  93.2 4.6 %collective-permute-start.11 = (bf16[128,4,128]{2,1,0:T(4,128)(2,1)S(1)}, bf16[128,4,128]{2,1,0:T(4,128)(2,1)S(1)}, u32[]{:S(2)}, u32[]{:S(2)}) collective-permute-start(bf16[128,4,128]{2,1,0:T(4,128)(2,1)S(1)} %all_to_all.11.refs_0_), channel_id=1, source_target_pairs={{0,4},{4,0},{8,12},{12,8},{16,20},{20,16},{24,28},{28,24},{32,36},... | collective-permute-start | bytes 393224 | tf_op jit(solution)/shard_map/ppermute | solution.py:831

commit v4 on v3

--- a/solution.py
+++ b/solution.py
@@ -276,13 +276,15 @@
     wave_in, mass_in, wave_extra, mass_extra, sems,
 ):
     copies = [
+        pltpu.make_async_copy(conn_hbm, conn, sems.at[2]),
         pltpu.make_async_copy(wave_hbm, wave_in, sems.at[0]),
         pltpu.make_async_copy(mass_hbm, mass_in, sems.at[1]),
-        pltpu.make_async_copy(conn_hbm, conn, sems.at[2]),
     ]
     for copy in copies:
         copy.start()
-    for copy in copies:
+    copies[0].wait()
+    pack_slots(TOP_PLAN, conn, slots)
+    for copy in copies[1:]:
         copy.wait()
     groups = wave_in.shape[1] // 256
     base = vectors * groups
@@ -297,7 +299,6 @@
         table[base:, columns] = jnp.concatenate([high.astype(F32), spare], 0).astype(BF16)
         columns = slice(256 + LANES * half, 256 + LANES * (half + 1))
         table[base:, columns] = jnp.concatenate([low.astype(F32), spare], 0).astype(BF16)
-    pack_slots(TOP_PLAN, conn, slots)
     gather_rows(
         vectors, groups, TOP_PLAN, top_row, slots, table, wave_top, mass_top, wave_extra, mass_extra
     )
@@ -314,7 +315,7 @@
 
 
 def gather_rest_kernel(
-    vectors, groups, table, conn, potential_hbm, levels_hbm, live_ref,
+    vectors, groups, table, conn, potential_hbm, levels_hbm, constants,
     slots, wave_mid, mass_mid, kinetic, coefficient, levels_in, wave_extra, mass_extra, sems,
 ):
     copies = [
@@ -327,10 +328,10 @@
     gather_rows(
         vectors, groups, MID_PLAN, mid_row, slots, table, wave_mid, mass_mid, wave_extra, mass_extra
     )
-    copies[0].wait()
-    copies[1].wait()
+    for copy in copies:
+        copy.wait()
     size = jnp.exp2(-levels_in[...].astype(F32))
-    in_use = jnp.where(lane_index(1) < live_ref[0], 1.0, 0.0).astype(F32)
+    in_use = jnp.where(lane_index(1).astype(F32) < constants[2:3, :], 1.0, 0.0)
     kinetic[...] = jnp.broadcast_to(size / 4.0 * in_use, (8, LANES))
     volume = size * size * size / 8.0 * in_use
     for j in ALL_ROWS:
@@ -427,12 +428,11 @@
 
 def second_faces_kernel(
     vectors, low, mid, top, wave_low, wave_mid, wave_top, mass_low, mass_mid, mass_top,
-    above, below, kinetic, coefficient, center_ref, halfwidth_ref,
+    above, below, kinetic, coefficient, constants,
     values, base_mid, base_top, low_out, face_down,
 ):
     upper = upper_lanes(vectors)
-    center = center_ref[0]
-    inverse = 1.0 / jnp.full((1, LANES), halfwidth_ref[0], F32)
+    center, inverse = constants[0:1, :], constants[1:2, :]
     again = (-2.0 * center) * inverse
     sums = Nodes(low, mid, top)
     wave, mass = Nodes(wave_low, wave_mid, wave_top), Nodes(mass_low, mass_mid, mass_top)
@@ -500,7 +500,7 @@
 
 def second_rest_kernel(
     vectors, values, kinetic, coefficient, low, mass_mid, mass_top, base_mid, base_top, slots,
-    wave_hbm, earlier_hbm, center_ref, halfwidth_ref,
+    wave_hbm, earlier_hbm, constants,
     total, done_top, alone, *rest,
 ):
     earlier, (mid, top, wave_in, sems) = rest[:-4], rest[-4:]
@@ -513,8 +513,7 @@
         loads.append(pltpu.make_async_copy(source, part, sems.at[1 + i]))
         loads[-1].start()
     groups = wave_in.shape[1] // 256
-    center = center_ref[0]
-    inverse = 1.0 / jnp.full((1, LANES), halfwidth_ref[0], F32)
+    center, inverse = constants[0:1, :], constants[1:2, :]
     terms = Nodes(None, mid, top)
     apply_cells(values, terms, kinetic, coefficient, MID_ROWS + TOP_ROWS, vectors)
     join_layer(terms, (1, 2, 3, 4), vectors)
@@ -533,24 +532,25 @@
     scatter_rows(vectors, groups, MID_PLAN, slots, load, total)
     copy.wait()
     wide_inverse = jnp.concatenate([inverse, inverse], 1)
+    wide_center = jnp.concatenate([center, center], 1)
     for h in range(groups):
         wave = wave_in[:, 256 * h : 256 * (h + 1)]
-        one = -center * wave * wide_inverse
+        one = -wide_center * wave * wide_inverse
         alone[:, 256 * h : 256 * (h + 1)] = (
-            (-2.0 * center) * wide_inverse * one - wave
+            (-2.0 * wide_center) * wide_inverse * one - wave
         ).astype(BF16)
     for load in loads:
         load.wait()
 
 
 def scatter_top_kernel(
-    vectors, slots, before, done_top, mass_top, above, alone, halfwidth_ref, *rest
+    vectors, slots, before, done_top, mass_top, above, alone, constants, *rest
 ):
     outs, (placed, total) = rest[:-2], rest[-2:]
     groups = alone.shape[1] // 256
     base = vectors * groups
     upper = upper_lanes(8)
-    inverse = 1.0 / jnp.full((1, LANES), halfwidth_ref[0], F32)
+    inverse = constants[1:2, :]
 
     def load(j, part):
         ab = j // 5
@@ -573,57 +573,52 @@
         out[...] = placed[away]
 
 
-def project_kernel(cores, parts, share, *rest):
-    pieces, earlier, (keep, send, quarter, product) = rest[:parts], rest[parts:-4], rest[-4:]
-    for away, piece in enumerate(pieces):
+def earlier_rows(earlier, start, size):
+    pieces, height = [], earlier[0].shape[0]
+    while size > 0:
+        block, at = divmod(start, height)
+        count = min(size, height - at)
+        pieces.append(earlier[block][at : at + count, :])
+        start, size = start + count, size - count
+    return pieces
+
+
+def project_kernel(cores, parts, share, other, quarter, *rest):
+    earlier, (out,) = rest[:-1], rest[-1:]
+    half, block = share // 2, parts * share
+    total = sum(part.shape[0] for part in earlier)
+    here = lax.rem(lax.axis_index("cells"), cores)
+    for core in range(cores):
+
+        @pl.when(here == (1 - core if other else core))
+        def _():
+            pieces = []
+            for start in range(core * block, total, cores * block):
+                pieces += earlier_rows(earlier, start, block)
+            product = lax.dot_general(
+                jnp.concatenate(pieces, 0),
+                quarter[...],
+                (((1,), (1,)), ((), ())),
+                preferred_element_type=F32,
+            )
+            product = product.reshape(out.shape[0], share, product.shape[-1])
+            out[...] = jnp.concatenate([product[:, :half], product[:, half:]], 2)
+
+
+def gather_pieces_kernel(parts, *refs):
+    quarter = refs[-1]
+    for away, piece in enumerate(refs[:-1]):
         size = piece.shape[0]
         source = lax.rem(lax.axis_index("vecs") + parts - away, parts)
         quarter[pl.ds(pl.multiple_of(size * source, size), size), :] = piece[...]
-    half = share // 2
-    columns = quarter.shape[0]
-    this_core = lax.rem(lax.axis_index("cells"), cores)
-    product[...] = lax.dot_general(
-        jnp.concatenate([part[...] for part in earlier], 0),
-        quarter[...],
-        (((1,), (1,)), ((), ())),
-        preferred_element_type=F32,
-    )
-    block = parts * share
-
-    def pack(core, out):
-        for i in range(product.shape[0] // (cores * block)):
-            at = (cores * i + core) * block
-            mine = product[at : at + block, :].reshape(parts, share, columns)
-            out[parts * i : parts * (i + 1)] = jnp.concatenate([mine[:, :half], mine[:, half:]], 2)
-
-    for core in range(cores):
-
-        @pl.when(this_core == core)
-        def _():
-            pack(core, keep)
-            pack(1 - core, send)
-
-
-def pair_sum_kernel(parts, keep, received, *rest):
-    outs, placed = rest[:-1], rest[-1]
-    here = lax.axis_index("vecs")
-    total = keep[...] + received[...]
-    total = total.reshape(total.shape[0] // parts, parts, *total.shape[1:])
-    for part in range(parts):
-        placed[lax.rem(part + parts - here, parts)] = total[:, part]
-    for away, out in enumerate(outs):
-        out[...] = placed[away]
-
-
-def part_sum_kernel(*refs):
-    total = refs[0][...]
-    for ref in refs[1:-1]:
-        total = total + ref[...]
-    refs[-1][...] = total
+
+
+def pair_sum_kernel(keep, received, out):
+    out[...] = (keep[...] + received[...]).astype(out.dtype)
 
 
 def own_rows_kernel(shares, own_rows, spread):
-    own = jnp.sum(shares[...], 0)
+    own = jnp.sum(shares[...].astype(F32), 0)
     columns = own.shape[1] // 2
     own_rows[...] = jnp.concatenate([own[:, :columns], own[:, columns:]], 0)
     spread[...] = jnp.broadcast_to(own[None], spread.shape).astype(BF16)
@@ -663,7 +658,6 @@
 
 
 VMEM_SPEC = pl.BlockSpec(memory_space=pltpu.VMEM)
-SMEM_SPEC = pl.BlockSpec(memory_space=pltpu.SMEM)
 HBM_SPEC = pl.BlockSpec(memory_space=pltpu.HBM)
 
 
@@ -671,7 +665,7 @@
     return pl.pallas_call(
         kernel,
         out_shape=out_shape,
-        in_specs=[{"v": VMEM_SPEC, "s": SMEM_SPEC, "h": HBM_SPEC}[letter] for letter in specs],
+        in_specs=[{"v": VMEM_SPEC, "h": HBM_SPEC}[letter] for letter in specs],
         out_specs=jax.tree.map(lambda _: VMEM_SPEC, out_shape),
         scratch_shapes=scratch,
         compiler_params=pltpu.CompilerParams(vmem_limit_bytes=VMEM_LIMIT),
@@ -698,7 +692,9 @@
     cells, parts = lax.axis_size("cells"), lax.axis_size("vecs")
     devices, cores = cells * parts, 2
     turn = lambda away: [(i, (i + away) % parts) for i in range(parts)]
-    center, halfwidth = center.reshape(1), halfwidth.reshape(1)
+    line = lax.broadcasted_iota(I32, (8, LANES), 0)
+    constants = jnp.where(line == 1, 1.0 / halfwidth, live_cells[0].astype(F32))
+    constants = jnp.where(line == 0, center, constants)
 
     def shape(*sizes, kind=F32):
         return jax.ShapeDtypeStruct(sizes, kind)
@@ -733,9 +729,11 @@
         (
             shape(len(MID_PLAN), LANES, kind=I32), rows(75), lines(75), lines(8), lines(125),
         ),
-        "vvhhs",
-        [pltpu.VMEM((1, LANES), I32), *extra(4), pltpu.SemaphoreType.DMA((2,))],
-        table, conn, potential, levels.reshape(1, LANES), live_cells,
+        "vvhhv",
+        [
+            pltpu.VMEM((1, LANES), I32), *extra(4), pltpu.SemaphoreType.DMA((2,)),
+        ],
+        table, conn, potential, levels.reshape(1, LANES), constants,
     )
     values, wave_low, mass_low, low, top, face_down, face_up = call(
         lambda *refs: first_faces_kernel(vectors, *refs),
@@ -755,10 +753,10 @@
         lambda *refs: second_faces_kernel(vectors, *refs),
         "second_faces",
         (rows(125), rows(75), rows(25), rows(25), packed),
-        "v" * 13 + "ss",
+        "v" * 14,
         [],
         low, mid, top, wave_low, wave_mid, wave_top, mass_low, mass_mid, mass_top,
-        above, below, kinetic, coefficient, center, halfwidth,
+        above, below, kinetic, coefficient, constants,
     )
     above = passed_along(face_down, "cells", -1)
     before, done_top, alone, *earlier = call(
@@ -768,18 +766,18 @@
             shape(table_rows, 256), rows(25), shape(vectors, owned, kind=BF16),
             *[shape(earlier_vectors.shape[0] // BLOCKS, owned // parts, kind=BF16)] * BLOCKS,
         ),
-        "v" * 9 + "hhss",
+        "v" * 9 + "hhv",
         [scratch_rows(75), scratch_rows(25), wave_scratch, pltpu.SemaphoreType.DMA((1 + BLOCKS,))],
         values, kinetic, coefficient, low, mass_mid, mass_top, base_mid, base_top, slots_mid,
-        wave_block, earlier_vectors, center, halfwidth,
+        wave_block, earlier_vectors, constants,
     )
     pieces = call(
         lambda *refs: scatter_top_kernel(vectors, *refs),
         "scatter_top",
         (shape(vectors, owned // parts, kind=BF16),) * parts,
-        "vvvvvvs",
+        "vvvvvvv",
         [pltpu.VMEM((parts, vectors, owned // parts), BF16), pltpu.VMEM((table_rows, 256), F32)],
-        slots_top, before, done_top, mass_top, above, alone, halfwidth,
+        slots_top, before, done_top, mass_top, above, alone, constants,
     )
     pieces = [
         lax.ppermute(piece, "vecs", turn(away)) if away else piece
@@ -794,30 +792,26 @@
         for k in range(cores)
     ]
     sent = shape(peers, half, 2 * total_vectors)
-    keep, send, quarter = call(
-        lambda *refs: project_kernel(cores, parts, share, *refs),
-        "project",
-        (sent, sent, shape(total_vectors, owned // parts, kind=BF16)),
-        "v" * (parts + BLOCKS),
-        [pltpu.VMEM((earlier_vectors.shape[0], total_vectors), F32)],
-        *pieces, *earlier,
-    )
-    blocks = cells // cores
-    share_shape = shape(blocks, half, 2 * total_vectors)
-    pieces = call(
-        lambda *refs: pair_sum_kernel(parts, *refs),
-        "pair_sum", (share_shape,) * parts, "vv",
-        [pltpu.VMEM((parts,) + share_shape.shape, F32)],
+    quarter = call(
+        lambda *refs: gather_pieces_kernel(parts, *refs),
+        "gather_pieces",
+        shape(total_vectors, owned // parts, kind=BF16),
+        "v" * parts, [], *pieces,
+    )
+    send, keep = [
+        call(
+            lambda *refs, other=other: project_kernel(cores, parts, share, other, *refs),
+            "project_other" if other else "project_own",
+            sent, "v" * (1 + BLOCKS), [], quarter, *earlier,
+        )
+        for other in (True, False)
+    ]
+    shares = call(
+        pair_sum_kernel, "pair_sum", shape(*sent.shape, kind=BF16), "vv", [],
         keep, lax.ppermute(send, "cells", pair),
     )
-    pieces = [
-        lax.ppermute(piece, "vecs", turn(away)) if away else piece
-        for away, piece in enumerate(pieces)
-    ]
-    shares = call(part_sum_kernel, "part_sum", share_shape, "v" * parts, [], *pieces)
     shares = lax.all_to_all(
-        shares, "cells", split_axis=0, concat_axis=0, tiled=True,
-        axis_index_groups=[[cores * block + k for block in range(blocks)] for k in range(cores)],
+        shares, AXES, split_axis=0, concat_axis=0, tiled=True, axis_index_groups=same_core
     )
     own_rows, mine = call(
         own_rows_kernel,

time: 101 us -> 98.2 us (0.972)
  blocking collectives: 41.4 us -> 47.5 us
  starting transfers between devices: 25.4 us -> 20.4 us
  waiting for transfers between devices: 7.5 us -> 3.41 us
    all_to_all x1, blocking collectives: 23.7 us -> 30.7 us  [per_device(): lax.all_to_all(shares, AXES, split_axis=0, concat_axis=0, tiled=True, axi...]
    ppermute x6 -> x3, starting transfers between devices: 9.25 us -> 5.07 us  [per_device(): lax.ppermute(piece, 'vecs', turn(away))]
    ppermute x6 -> x3, waiting for transfers between devices: 4.98 us -> 2.13 us  [per_device(): lax.ppermute(piece, 'vecs', turn(away))]
    ppermute x1, waiting for transfers between devices: 1.52 us -> 0.07 us  [per_device(): lax.ppermute(send, 'cells', pair)]
    pallas_call x12 -> x13, Pallas kernels: 23.6 us -> 23.7 us  [call(): pl.pallas_call(kernel, out_shape=out_shape, in_specs=[{'v': VMEM_SPEC, 'h...]
  transfers between devices with their start and end apart: 12 -> 9, of which waited for: 7 -> 7; matrix products, arithmetic and copies ran while one was open for 0% -> 0% of each run, Pallas kernels for 10% -> 12%
where the time goes in v4:
time: 98.2 us; the launch traced here: 97.9 us
  blocking collectives  47.5 us (48%)
  Pallas kernels  23.7 us (24%)
  starting transfers between devices  20.4 us (21%)
  waiting for transfers between devices  3.41 us (3%)
  between operations  2.75 us (3%)
    all_to_all x1, blocking collectives, per_device(): lax.all_to_all(shares, AXES, split_axis=0, concat_axis=0, tiled=True, axi...  30.7 us
    pallas_call x13, Pallas kernels, call(): pl.pallas_call(kernel, out_shape=out_shape, in_specs=[{'v': VMEM_SPEC, 'h...  23.7 us
    all_to_all x1, blocking collectives, per_device(): lax.all_to_all(mine, AXES, split_axis=0, concat_axis=0, tiled=True, axis_...  16.8 us
    ppermute x4, starting transfers between devices, passed_along(): lax.ppermute(value, axis, [(source, source + steps) for source in range(l...  12.4 us
    ppermute x3, starting transfers between devices, per_device(): lax.ppermute(piece, 'vecs', turn(away))  5.07 us
    ppermute x1, starting transfers between devices, per_device(): theirs = lax.ppermute(mine, 'cells', pair)  2.84 us
    ppermute x3, waiting for transfers between devices, per_device(): lax.ppermute(piece, 'vecs', turn(away))  2.13 us
  transfers between devices with their start and end apart: 9, of which 7 were waited for; matrix products, arithmetic and copies ran while one was open for 0% of the time, Pallas kernels for 12%

profile of v4, /device:TPU:1, one launch (start us, length us, event | category | flops | bytes accessed | tf_op | source)
XLA Modules:
  0.0 97.9 jit_solution(17538554811908368274)
XLA Ops:
  0.6 3.2 %gather_face.1 = (bf16[624,512]{1,0:T(8,128)(2,1)S(1)}, s32[125,128]{1,0:T(8,128)S(1)}, s32[18,128]{1,0:T(8,128)S(1)}, f32[25,16,128]{2,1,0:T(8,128)S(1)}, f32[2...) custom-call(s32[125,128]{1,0:T(8,128)} %refs_0_.1, f32[16,9216]{1,0:T(8,128)} %refs_9_.1, f32[72,128]{1,0:T(8,128)} %bitcast.3), custom_call_target="tpu_custom_call" | custom-call | tf_op jit(solution)/shard_map/gather_face/pallas_call | solution.py:665
  3.9 4.9 %collective-permute-start = (f32[13,24,128]{2,1,0:T(8,128)S(1)}, f32[13,24,128]{2,1,0:T(8,128)S(1)}, u32[]{:S(2)}, u32[]{:S(2)}) collective-permute-start(f32[13,24,128]{2,1,0:T(8,128)S(1)} %get-tuple-element.49), channel_id=1, source_target_pairs={{0,4},{4,8},{8,12},{12,16},{16,20},{20,24},{24,28},{28,32},{32,36}... | collective-permute-start | bytes 479240 | tf_op jit(solution)/shard_map/ppermute | solution.py:682
  10.8 0.1 broadcast_select_fusion.refs_4_.refs_13_.refs_11_.refs_6_
  10.9 4.9 %gather_rest.1 = (s32[52,128]{1,0:T(8,128)S(1)}, f32[75,16,128]{2,1,0:T(8,128)S(1)}, f32[75,128]{1,0:T(8,128)S(1)}, f32[8,128]{1,0:T(8,128)S(1)}, f32[125,128]{1,0:T(8,128)S(1)}) custom-call(bf16[624,512]{1,0:T(8,128)(2,1)S(1)} %get-tuple-element.43.refs_0_, s32[125,128]{1,0:T(8,128)S(1)} %get-tuple-element.44.refs_1_, f32[125,128]{1,0:T(8,128)} %refs_2_.1, ...), custom_call_target="tpu_custom_call" | custom-call | tf_op jit(solution)/shard_map/gather_rest/pallas_call | solution.py:665
  15.8 0.0 collective-permute-done.refs_4_
  15.8 1.3 %first_faces.1 = (f32[125,16,128]{2,1,0:T(8,128)S(1)}, f32[25,16,128]{2,1,0:T(8,128)S(1)}, f32[25,128]{1,0:T(8,128)S(1)}, f32[25,16,128]{2,1,0:T(8,128)S(1)}, f3...) custom-call(f32[75,16,128]{2,1,0:T(8,128)S(1)} %get-tuple-element.45.refs_0_.refs_4_, ...), custom_call_target="tpu_custom_call" | custom-call | tf_op jit(solution)/shard_map/first_faces/pallas_call | solution.py:665
  17.1 1.9 %collective-permute-start.1 = (bf16[13,16,128]{2,1,0:T(8,128)(2,1)S(1)}, bf16[13,16,128]{2,1,0:T(8,128)(2,1)S(1)}, u32[]{:S(2)}, u32[]{:S(2)}) collective-permute-start(bf16[13,16,128]{2,1,0:T(8,128)(2,1)S(1)} %get-tuple-element.57), channel_id=1, source_target_pairs={{4,0},{8,4},{12,8},{16,12},{20,16},{24,20},{28,24},{32,28},{36,32}... | collective-permute-start | bytes 159752 | tf_op jit(solution)/shard_map/ppermute | solution.py:682
  19.0 3.6 %collective-permute-start.2 = (bf16[13,16,128]{2,1,0:T(8,128)(2,1)S(1)}, bf16[13,16,128]{2,1,0:T(8,128)(2,1)S(1)}, u32[]{:S(2)}, u32[]{:S(2)}) collective-permute-start(bf16[13,16,128]{2,1,0:T(8,128)(2,1)S(1)} %get-tuple-element.58), channel_id=1, source_target_pairs={{0,4},{4,8},{8,12},{12,16},{16,20},{20,24},{24,28},{28,32},{32,36}... | collective-permute-start | bytes 159752 | tf_op jit(solution)/shard_map/ppermute | solution.py:682
  22.7 1.1 %first_rest.1.refs_1_ = f32[75,16,128]{2,1,0:T(8,128)S(1)} custom-call(f32[125,16,128]{2,1,0:T(8,128)S(1)} %get-tuple-element.53.refs_0_, f32[8,128]{1,0:T(8,128)S(1)} %get-tuple-element.50.refs_5_.refs_1_.refs_11_, f32[125,128]{1,0:T(8,128)S(1)} %get-tuple-element.51.refs_6_.refs_2_.refs_12_), custom_call_target="tpu_custom_call" | custom-call | tf_op jit(solution)/shard_map/first_rest/pallas_call | solution.py:665
  23.8 0.0 collective-permute-done.1.refs_9_
  23.8 0.1 collective-permute-done.2.refs_10_
  23.9 1.3 %second_faces.1 = (f32[125,16,128]{2,1,0:T(8,128)S(1)}, f32[75,16,128]{2,1,0:T(8,128)S(1)}, f32[25,16,128]{2,1,0:T(8,128)S(1)}, f32[25,16,128]{2,1,0:T(8,128)S(1)}, bf16[13,16,128]{2,1,0:T(8,128)(2,1)S(1)}) custom-call(f32[25,16,128]{2,1,0:T(8,128)S(1)} %get-tuple-element.52.refs_0_, f32[75,16,128]{2,1,0:T(8,128)S(1)} %first_rest.1.refs_1_, ...), custom_call_target="tpu_custom_call" | custom-call | tf_op jit(solution)/shard_map/second_faces/pallas_call | solution.py:665
  25.2 1.9 %collective-permute-start.3 = (bf16[13,16,128]{2,1,0:T(8,128)(2,1)S(1)}, bf16[13,16,128]{2,1,0:T(8,128)(2,1)S(1)}, u32[]{:S(2)}, u32[]{:S(2)}) collective-permute-start(bf16[13,16,128]{2,1,0:T(8,128)(2,1)S(1)} %get-tuple-element.66), channel_id=1, source_target_pairs={{4,0},{8,4},{12,8},{16,12},{20,16},{24,20},{28,24},{32,28},{36,32}... | collective-permute-start | bytes 159752 | tf_op jit(solution)/shard_map/ppermute | solution.py:682
  27.1 4.0 %second_rest.1 = (f32[624,256]{1,0:T(8,128)S(1)}, f32[25,16,128]{2,1,0:T(8,128)S(1)}, bf16[16,9216]{1,0:T(8,128)(2,1)S(1)}, bf16[256,2304]{1,0:T(8,128)(2,1)S(1)...) custom-call(f32[125,16,128]{2,1,0:T(8,128)S(1)} %get-tuple-element.5, ...), custom_call_target="tpu_custom_call" | custom-call | tf_op jit(solution)/shard_map/second_rest/pallas_call | solution.py:665
  31.1 0.2 collective-permute-done.3.refs_4_
  31.2 1.2 %scatter_top.1 = (bf16[16,2304]{1,0:T(8,128)(2,1)S(1)}, bf16[16,2304]{1,0:T(8,128)(2,1)S(1)}, bf16[16,2304]{1,0:T(8,128)(2,1)S(1)}, bf16[16,2304]{1,0:T(8,128)(2,1)S(1)}) custom-call(s32[18,128]{1,0:T(8,128)S(1)} %get-tuple-element.42.refs_0_, f32[624,256]{1,0:T(8,128)S(1)} %get-tuple-element.64.refs_1_, f32[25,16,128]{2,1,0:T(8,128)S(1)} %get-tuple-element.65.refs_2_, ...), custom_call_target="tpu_custom_call" | custom-call | tf_op jit(solution)/shard_map/scatter_top/pallas_call | solution.py:665
  32.4 1.4 %collective-permute-start.4 = (bf16[16,2304]{1,0:T(8,128)(2,1)S(1)}, bf16[16,2304]{1,0:T(8,128)(2,1)S(1)}, u32[]{:S(2)}, u32[]{:S(2)}) collective-permute-start(bf16[16,2304]{1,0:T(8,128)(2,1)S(1)} %get-tuple-element.69), channel_id=1, source_target_pairs={{0,1},{1,2},{2,3},{3,0},{4,5},{5,6},{6,7},{7,4},{8,9},{9,10},{10,1... | collective-permute-start | bytes 221192 | tf_op jit(solution)/shard_map/ppermute | solution.py:783
  33.8 2.6 %collective-permute-start.5 = (bf16[16,2304]{1,0:T(8,128)(2,1)S(1)}, bf16[16,2304]{1,0:T(8,128)(2,1)S(1)}, u32[]{:S(2)}, u32[]{:S(2)}) collective-permute-start(bf16[16,2304]{1,0:T(8,128)(2,1)S(1)} %get-tuple-element.70), channel_id=1, source_target_pairs={{0,2},{1,3},{2,0},{3,1},{4,6},{5,7},{6,4},{7,5},{8,10},{9,11},{10,... | collective-permute-start | bytes 221192 | tf_op jit(solution)/shard_map/ppermute | solution.py:783
  36.4 1.1 %collective-permute-start.6 = (bf16[16,2304]{1,0:T(8,128)(2,1)S(1)}, bf16[16,2304]{1,0:T(8,128)(2,1)S(1)}, u32[]{:S(2)}, u32[]{:S(2)}) collective-permute-start(bf16[16,2304]{1,0:T(8,128)(2,1)S(1)} %get-tuple-element.71), channel_id=1, source_target_pairs={{0,3},{1,0},{2,1},{3,2},{4,7},{5,4},{6,5},{7,6},{8,11},{9,8},{10,9... | collective-permute-start | bytes 221192 | tf_op jit(solution)/shard_map/ppermute | solution.py:783
  37.5 0.3 collective-permute-done.4.refs_1_
  37.8 1.2 %collective-permute-done.5.refs_2_ = bf16[16,2304]{1,0:T(8,128)(2,1)S(1)} collective-permute-done((bf16[16,2304]{1,0:T(8,128)(2,1)S(1)}, bf16[16,2304]{1,0:T(8,128)(2,1)S(1)}, u32[]{:S(2)}, u32[]{:S(2)}) %collective-permute-start.5) | collective-permute-done | bytes 73760 | tf_op jit(solution)/shard_map/ppermute | solution.py:783
  39.0 0.7 collective-permute-done.6.refs_3_
  39.7 1.4 %project_other.1 = f32[128,4,128]{2,1,0:T(4,128)S(1)} custom-call(bf16[64,2304]{1,0:T(8,128)(2,1)S(1)} %gather_pieces.1.refs_0_.refs_2_, bf16[256,2304]{1,0:T(8,128)(2,1)S(1)} %get-tuple-element.72.refs_1_.refs_3_, bf16[256,2304]{1,0:T(8,128)(2,1)S(1)} %get-tuple-element.73.refs_2_.refs_4_, bf16[256,2304]{1,0:T(8,128)(2,1)S(1)} %get-tuple-element.74.refs_3_.refs_5_, ...), custom_call_target="tpu_custom_call" | custom-call | tf_op jit(solution)/shard_map/project_other/pallas_call | solution.py:665
  41.1 0.1 collective-permute-start.7
  41.2 1.4 %project_own.1.keep = f32[128,4,128]{2,1,0:T(4,128)S(1)} custom-call(bf16[64,2304]{1,0:T(8,128)(2,1)S(1)} %gather_pieces.1.refs_0_.refs_2_, bf16[256,2304]{1,0:T(8,128)(2,1)S(1)} %get-tuple-element.72.refs_1_.refs_3_, bf16[256,2304]{1,0:T(8,128)(2,1)S(1)} %get-tuple-element.73.refs_2_.refs_4_, bf16[256,2304]{1,0:T(8,128)(2,1)S(1)} %get-tuple-element.74.refs_3_.refs_5_, ...), custom_call_target="tpu_custom_call" | custom-call | tf_op jit(solution)/shard_map/project_own/pallas_call | solution.py:665
  42.7 0.1 collective-permute-done.7.received
  42.7 0.1 pair_sum.1
  42.8 30.7 %all_to_all.10.shares = bf16[128,4,128]{2,1,0:T(4,128)(2,1)S(1)} all-to-all(bf16[128,4,128]{2,1,0:T(4,128)(2,1)S(1)} %pair_sum.1), channel_id=1, replica_groups={{0,1,2,3,8,9,10,11,16,17,18,19,24,25,26,27,32,33,34,35,40,41,42,43,48,4..., dimensions={0} | all-to-all | bytes 262144 | tf_op jit(solution)/shard_map/all_to_all | solution.py:813
  73.5 0.8 own_rows.1
  74.3 16.8 %all_to_all.11.refs_0_ = bf16[128,4,128]{2,1,0:T(4,128)(2,1)S(1)} all-to-all(bf16[128,4,128]{2,1,0:T(4,128)(2,1)S(1)} %get-tuple-element.80), channel_id=1, replica_groups={{0,1,2,3,8,9,10,11,16,17,18,19,24,25,26,27,32,33,34,35,40,41,42,43,48,4..., dimensions={0} | all-to-all | bytes 262144 | tf_op jit(solution)/shard_map/all_to_all | solution.py:822
  91.1 2.8 %collective-permute-start.8 = (bf16[128,4,128]{2,1,0:T(4,128)(2,1)S(1)}, bf16[128,4,128]{2,1,0:T(4,128)(2,1)S(1)}, u32[]{:S(2)}, u32[]{:S(2)}) collective-permute-start(bf16[128,4,128]{2,1,0:T(4,128)(2,1)S(1)} %all_to_all.11.refs_0_), channel_id=1, source_target_pairs={{0,4},{4,0},{8,12},{12,8},{16,20},{20,16},{24,28},{28,24},{32,36},... | collective-permute-start | bytes 393224 | tf_op jit(solution)/shard_map/ppermute | solution.py:825
  94.0 1.0 %collective-permute-done.8.refs_1_ = bf16[128,4,128]{2,1,0:T(4,128)(2,1)S(1)} collective-permute-done((bf16[128,4,128]{2,1,0:T(4,128)(2,1)S(1)}, bf16[128,4,128]{2,1,0:T(4,128)(2,1)S(1)}, u32[]{:S(2)}, u32[]{:S(2)}) %collective-permute-start.8) | collective-permute-done | bytes 131104 | tf_op jit(solution)/shard_map/ppermute | solution.py:825
  95.0 2.9 %filter.1 = f32[64,2304]{1,0:T(8,128)} custom-call(bf16[128,4,128]{2,1,0:T(4,128)(2,1)S(1)} %all_to_all.11.refs_0_, bf16[128,4,128]{2,1,0:T(4,128)(2,1)S(1)} %collective-permute-done.8.refs_1_, bf16[64,2304]{1,0:T(8,128)(2,1)S(1)} %gather_pieces.1.refs_0_.refs_2_, bf16[256,2304]{1,0:T(8,128)(2,1)S(1)} %get-tuple-element.72.refs_1_.refs_3_, ...), custom_call_target="tpu_custom_call" | custom-call | tf_op jit(solution)/shard_map/filter/pallas_call | solution.py:665
  (3 shorter events, 0.0 us)
Async XLA Ops:
  3.9 11.9 %collective-permute-start = (f32[13,24,128]{2,1,0:T(8,128)S(1)}, f32[13,24,128]{2,1,0:T(8,128)S(1)}, u32[]{:S(2)}, u32[]{:S(2)}) collective-permute-start(f32[13,24,128]{2,1,0:T(8,128)S(1)} %get-tuple-element.49), channel_id=1, source_target_pairs={{0,4},{4,8},{8,12},{12,16},{16,20},{20,24},{24,28},{28,32},{32,36}... | collective-permute-start | bytes 479240 | tf_op jit(solution)/shard_map/ppermute | solution.py:682
  17.1 6.7 %collective-permute-start.1 = (bf16[13,16,128]{2,1,0:T(8,128)(2,1)S(1)}, bf16[13,16,128]{2,1,0:T(8,128)(2,1)S(1)}, u32[]{:S(2)}, u32[]{:S(2)}) collective-permute-start(bf16[13,16,128]{2,1,0:T(8,128)(2,1)S(1)} %get-tuple-element.57), channel_id=1, source_target_pairs={{4,0},{8,4},{12,8},{16,12},{20,16},{24,20},{28,24},{32,28},{36,32}... | collective-permute-start | bytes 159752 | tf_op jit(solution)/shard_map/ppermute | solution.py:682
  19.0 4.8 %collective-permute-start.2 = (bf16[13,16,128]{2,1,0:T(8,128)(2,1)S(1)}, bf16[13,16,128]{2,1,0:T(8,128)(2,1)S(1)}, u32[]{:S(2)}, u32[]{:S(2)}) collective-permute-start(bf16[13,16,128]{2,1,0:T(8,128)(2,1)S(1)} %get-tuple-element.58), channel_id=1, source_target_pairs={{0,4},{4,8},{8,12},{12,16},{16,20},{20,24},{24,28},{28,32},{32,36}... | collective-permute-start | bytes 159752 | tf_op jit(solution)/shard_map/ppermute | solution.py:682
  25.2 6.1 %collective-permute-start.3 = (bf16[13,16,128]{2,1,0:T(8,128)(2,1)S(1)}, bf16[13,16,128]{2,1,0:T(8,128)(2,1)S(1)}, u32[]{:S(2)}, u32[]{:S(2)}) collective-permute-start(bf16[13,16,128]{2,1,0:T(8,128)(2,1)S(1)} %get-tuple-element.66), channel_id=1, source_target_pairs={{4,0},{8,4},{12,8},{16,12},{20,16},{24,20},{28,24},{32,28},{36,32}... | collective-permute-start | bytes 159752 | tf_op jit(solution)/shard_map/ppermute | solution.py:682
  32.4 5.4 %collective-permute-start.4 = (bf16[16,2304]{1,0:T(8,128)(2,1)S(1)}, bf16[16,2304]{1,0:T(8,128)(2,1)S(1)}, u32[]{:S(2)}, u32[]{:S(2)}) collective-permute-start(bf16[16,2304]{1,0:T(8,128)(2,1)S(1)} %get-tuple-element.69), channel_id=1, source_target_pairs={{0,1},{1,2},{2,3},{3,0},{4,5},{5,6},{6,7},{7,4},{8,9},{9,10},{10,1... | collective-permute-start | bytes 221192 | tf_op jit(solution)/shard_map/ppermute | solution.py:783
  33.8 5.1 %collective-permute-start.5 = (bf16[16,2304]{1,0:T(8,128)(2,1)S(1)}, bf16[16,2304]{1,0:T(8,128)(2,1)S(1)}, u32[]{:S(2)}, u32[]{:S(2)}) collective-permute-start(bf16[16,2304]{1,0:T(8,128)(2,1)S(1)} %get-tuple-element.70), channel_id=1, source_target_pairs={{0,2},{1,3},{2,0},{3,1},{4,6},{5,7},{6,4},{7,5},{8,10},{9,11},{10,... | collective-permute-start | bytes 221192 | tf_op jit(solution)/shard_map/ppermute | solution.py:783
  36.4 3.2 %collective-permute-start.6 = (bf16[16,2304]{1,0:T(8,128)(2,1)S(1)}, bf16[16,2304]{1,0:T(8,128)(2,1)S(1)}, u32[]{:S(2)}, u32[]{:S(2)}) collective-permute-start(bf16[16,2304]{1,0:T(8,128)(2,1)S(1)} %get-tuple-element.71), channel_id=1, source_target_pairs={{0,3},{1,0},{2,1},{3,2},{4,7},{5,4},{6,5},{7,6},{8,11},{9,8},{10,9... | collective-permute-start | bytes 221192 | tf_op jit(solution)/shard_map/ppermute | solution.py:783
  41.1 1.6 %collective-permute-start.7 = (f32[128,4,128]{2,1,0:T(4,128)S(1)}, f32[128,4,128]{2,1,0:T(4,128)S(1)}, u32[]{:S(2)}, u32[]{:S(2)}) collective-permute-start(f32[128,4,128]{2,1,0:T(4,128)S(1)} %project_other.1), channel_id=1, source_target_pairs={{0,4},{4,0},{8,12},{12,8},{16,20},{20,16},{24,28},{28,24},{32,36},... | collective-permute-start | bytes 786440 | tf_op jit(solution)/shard_map/ppermute | solution.py:811
  91.1 3.8 %collective-permute-start.8 = (bf16[128,4,128]{2,1,0:T(4,128)(2,1)S(1)}, bf16[128,4,128]{2,1,0:T(4,128)(2,1)S(1)}, u32[]{:S(2)}, u32[]{:S(2)}) collective-permute-start(bf16[128,4,128]{2,1,0:T(4,128)(2,1)S(1)} %all_to_all.11.refs_0_), channel_id=1, source_target_pairs={{0,4},{4,0},{8,12},{12,8},{16,20},{20,16},{24,28},{28,24},{32,36},... | collective-permute-start | bytes 393224 | tf_op jit(solution)/shard_map/ppermute | solution.py:825

commit v5 on v4

--- a/solution.py
+++ b/solution.py
@@ -315,7 +315,7 @@
 
 
 def gather_rest_kernel(
-    vectors, groups, table, conn, potential_hbm, levels_hbm, constants,
+    vectors, groups, table, conn, potential_hbm, levels_hbm, live_ref,
     slots, wave_mid, mass_mid, kinetic, coefficient, levels_in, wave_extra, mass_extra, sems,
 ):
     copies = [
@@ -328,10 +328,10 @@
     gather_rows(
         vectors, groups, MID_PLAN, mid_row, slots, table, wave_mid, mass_mid, wave_extra, mass_extra
     )
-    for copy in copies:
-        copy.wait()
+    copies[0].wait()
+    copies[1].wait()
     size = jnp.exp2(-levels_in[...].astype(F32))
-    in_use = jnp.where(lane_index(1).astype(F32) < constants[2:3, :], 1.0, 0.0)
+    in_use = jnp.where(lane_index(1) < live_ref[0], 1.0, 0.0).astype(F32)
     kinetic[...] = jnp.broadcast_to(size / 4.0 * in_use, (8, LANES))
     volume = size * size * size / 8.0 * in_use
     for j in ALL_ROWS:
@@ -428,11 +428,12 @@
 
 def second_faces_kernel(
     vectors, low, mid, top, wave_low, wave_mid, wave_top, mass_low, mass_mid, mass_top,
-    above, below, kinetic, coefficient, constants,
+    above, below, kinetic, coefficient, center_ref, halfwidth_ref,
     values, base_mid, base_top, low_out, face_down,
 ):
     upper = upper_lanes(vectors)
-    center, inverse = constants[0:1, :], constants[1:2, :]
+    center = center_ref[0]
+    inverse = 1.0 / jnp.full((1, LANES), halfwidth_ref[0], F32)
     again = (-2.0 * center) * inverse
     sums = Nodes(low, mid, top)
     wave, mass = Nodes(wave_low, wave_mid, wave_top), Nodes(mass_low, mass_mid, mass_top)
@@ -500,7 +501,7 @@
 
 def second_rest_kernel(
     vectors, values, kinetic, coefficient, low, mass_mid, mass_top, base_mid, base_top, slots,
-    wave_hbm, earlier_hbm, constants,
+    wave_hbm, earlier_hbm, center_ref, halfwidth_ref,
     total, done_top, alone, *rest,
 ):
     earlier, (mid, top, wave_in, sems) = rest[:-4], rest[-4:]
@@ -513,7 +514,8 @@
         loads.append(pltpu.make_async_copy(source, part, sems.at[1 + i]))
         loads[-1].start()
     groups = wave_in.shape[1] // 256
-    center, inverse = constants[0:1, :], constants[1:2, :]
+    center = center_ref[0]
+    inverse = 1.0 / jnp.full((1, LANES), halfwidth_ref[0], F32)
     terms = Nodes(None, mid, top)
     apply_cells(values, terms, kinetic, coefficient, MID_ROWS + TOP_ROWS, vectors)
     join_layer(terms, (1, 2, 3, 4), vectors)
@@ -532,25 +534,24 @@
     scatter_rows(vectors, groups, MID_PLAN, slots, load, total)
     copy.wait()
     wide_inverse = jnp.concatenate([inverse, inverse], 1)
-    wide_center = jnp.concatenate([center, center], 1)
     for h in range(groups):
         wave = wave_in[:, 256 * h : 256 * (h + 1)]
-        one = -wide_center * wave * wide_inverse
+        one = -center * wave * wide_inverse
         alone[:, 256 * h : 256 * (h + 1)] = (
-            (-2.0 * wide_center) * wide_inverse * one - wave
+            (-2.0 * center) * wide_inverse * one - wave
         ).astype(BF16)
     for load in loads:
         load.wait()
 
 
 def scatter_top_kernel(
-    vectors, slots, before, done_top, mass_top, above, alone, constants, *rest
+    vectors, slots, before, done_top, mass_top, above, alone, halfwidth_ref, *rest
 ):
     outs, (placed, total) = rest[:-2], rest[-2:]
     groups = alone.shape[1] // 256
     base = vectors * groups
     upper = upper_lanes(8)
-    inverse = constants[1:2, :]
+    inverse = 1.0 / jnp.full((1, LANES), halfwidth_ref[0], F32)
 
     def load(j, part):
         ab = j // 5
@@ -573,12 +574,12 @@
         out[...] = placed[away]
 
 
-def earlier_rows(earlier, start, size):
+def earlier_rows(earlier, start, size, columns=slice(None)):
     pieces, height = [], earlier[0].shape[0]
     while size > 0:
         block, at = divmod(start, height)
         count = min(size, height - at)
-        pieces.append(earlier[block][at : at + count, :])
+        pieces.append(earlier[block][at : at + count, columns])
         start, size = start + count, size - count
     return pieces
 
@@ -624,40 +625,36 @@
     spread[...] = jnp.broadcast_to(own[None], spread.shape).astype(BF16)
 
 
-def filter_kernel(cores, parts, share, mine, theirs, quarter, *rest):
-    earlier, (out_ref, low) = rest[:-2], rest[-2:]
-    half = share // 2
-    columns = mine.shape[-1] // 2
-    block = parts * share
-
-    def unpack(ref, core):
-        value = ref[...].astype(F32)
-        value = jnp.concatenate([value[:, :, :columns], value[:, :, columns:]], 1)
-        value = value.reshape(value.shape[0] // parts, block, columns)
-        for i in range(value.shape[0]):
-            at = (cores * i + core) * block
-            low[at : at + block, :] = value[i].astype(BF16)
-
+def filter_kernel(cores, parts, share, other, spread, before, *rest):
+    earlier, (out, low) = rest[:-2], rest[-2:]
+    half, block = share // 2, parts * share
+    columns = spread.shape[-1] // 2
+    total = sum(part.shape[0] for part in earlier)
+    value = spread[...].astype(F32)
+    value = jnp.concatenate([value[:, :, :columns], value[:, :, columns:]], 1)
+    low[...] = value.reshape(low.shape).astype(BF16)
+    here = lax.rem(lax.axis_index("cells"), cores)
+    width = 256
     for core in range(cores):
 
-        @pl.when(lax.rem(lax.axis_index("cells"), cores) == core)
+        @pl.when(here == (1 - core if other else core))
         def _():
-            unpack(mine, core)
-            unpack(theirs, 1 - core)
-
-    width = 256
-    for i in range(out_ref.shape[1] // width):
-        at = slice(width * i, width * (i + 1))
-        product = lax.dot_general(
-            low[...],
-            jnp.concatenate([part[:, at] for part in earlier], 0),
-            (((0,), (0,)), ((), ())),
-            preferred_element_type=F32,
-        )
-        out_ref[:, at] = quarter[:, at].astype(F32) - product
+            for i in range(out.shape[1] // width):
+                at = slice(width * i, width * (i + 1))
+                pieces = []
+                for start in range(core * block, total, cores * block):
+                    pieces += earlier_rows(earlier, start, block, at)
+                product = lax.dot_general(
+                    low[...],
+                    jnp.concatenate(pieces, 0),
+                    (((0,), (0,)), ((), ())),
+                    preferred_element_type=F32,
+                )
+                out[:, at] = before[:, at].astype(F32) - product
 
 
 VMEM_SPEC = pl.BlockSpec(memory_space=pltpu.VMEM)
+SMEM_SPEC = pl.BlockSpec(memory_space=pltpu.SMEM)
 HBM_SPEC = pl.BlockSpec(memory_space=pltpu.HBM)
 
 
@@ -665,7 +662,7 @@
     return pl.pallas_call(
         kernel,
         out_shape=out_shape,
-        in_specs=[{"v": VMEM_SPEC, "h": HBM_SPEC}[letter] for letter in specs],
+        in_specs=[{"v": VMEM_SPEC, "s": SMEM_SPEC, "h": HBM_SPEC}[letter] for letter in specs],
         out_specs=jax.tree.map(lambda _: VMEM_SPEC, out_shape),
         scratch_shapes=scratch,
         compiler_params=pltpu.CompilerParams(vmem_limit_bytes=VMEM_LIMIT),
@@ -692,9 +689,7 @@
     cells, parts = lax.axis_size("cells"), lax.axis_size("vecs")
     devices, cores = cells * parts, 2
     turn = lambda away: [(i, (i + away) % parts) for i in range(parts)]
-    line = lax.broadcasted_iota(I32, (8, LANES), 0)
-    constants = jnp.where(line == 1, 1.0 / halfwidth, live_cells[0].astype(F32))
-    constants = jnp.where(line == 0, center, constants)
+    center, halfwidth = center.reshape(1), halfwidth.reshape(1)
 
     def shape(*sizes, kind=F32):
         return jax.ShapeDtypeStruct(sizes, kind)
@@ -729,11 +724,9 @@
         (
             shape(len(MID_PLAN), LANES, kind=I32), rows(75), lines(75), lines(8), lines(125),
         ),
-        "vvhhv",
-        [
-            pltpu.VMEM((1, LANES), I32), *extra(4), pltpu.SemaphoreType.DMA((2,)),
-        ],
-        table, conn, potential, levels.reshape(1, LANES), constants,
+        "vvhhs",
+        [pltpu.VMEM((1, LANES), I32), *extra(4), pltpu.SemaphoreType.DMA((2,))],
+        table, conn, potential, levels.reshape(1, LANES), live_cells,
     )
     values, wave_low, mass_low, low, top, face_down, face_up = call(
         lambda *refs: first_faces_kernel(vectors, *refs),
@@ -753,10 +746,10 @@
         lambda *refs: second_faces_kernel(vectors, *refs),
         "second_faces",
         (rows(125), rows(75), rows(25), rows(25), packed),
-        "v" * 14,
+        "v" * 13 + "ss",
         [],
         low, mid, top, wave_low, wave_mid, wave_top, mass_low, mass_mid, mass_top,
-        above, below, kinetic, coefficient, constants,
+        above, below, kinetic, coefficient, center, halfwidth,
     )
     above = passed_along(face_down, "cells", -1)
     before, done_top, alone, *earlier = call(
@@ -766,18 +759,18 @@
             shape(table_rows, 256), rows(25), shape(vectors, owned, kind=BF16),
             *[shape(earlier_vectors.shape[0] // BLOCKS, owned // parts, kind=BF16)] * BLOCKS,
         ),
-        "v" * 9 + "hhv",
+        "v" * 9 + "hhss",
         [scratch_rows(75), scratch_rows(25), wave_scratch, pltpu.SemaphoreType.DMA((1 + BLOCKS,))],
         values, kinetic, coefficient, low, mass_mid, mass_top, base_mid, base_top, slots_mid,
-        wave_block, earlier_vectors, constants,
+        wave_block, earlier_vectors, center, halfwidth,
     )
     pieces = call(
         lambda *refs: scatter_top_kernel(vectors, *refs),
         "scatter_top",
         (shape(vectors, owned // parts, kind=BF16),) * parts,
-        "vvvvvvv",
+        "vvvvvvs",
         [pltpu.VMEM((parts, vectors, owned // parts), BF16), pltpu.VMEM((table_rows, 256), F32)],
-        slots_top, before, done_top, mass_top, above, alone, constants,
+        slots_top, before, done_top, mass_top, above, alone, halfwidth,
     )
     pieces = [
         lax.ppermute(piece, "vecs", turn(away)) if away else piece
@@ -823,14 +816,16 @@
         mine, AXES, split_axis=0, concat_axis=0, tiled=True, axis_index_groups=same_core
     )
     theirs = lax.ppermute(mine, "cells", pair)
-    filtered = call(
-        lambda *refs: filter_kernel(cores, parts, share, *refs),
-        "filter",
-        shape(total_vectors, owned // parts),
-        "vvv" + "v" * BLOCKS,
-        [pltpu.VMEM((devices * share, total_vectors), BF16)],
-        mine, theirs, quarter, *earlier,
-    )
+    filtered = quarter
+    for other, spread in ((False, mine), (True, theirs)):
+        filtered = call(
+            lambda *refs, other=other: filter_kernel(cores, parts, share, other, *refs),
+            "filter_other" if other else "filter_own",
+            shape(total_vectors, owned // parts),
+            "vv" + "v" * BLOCKS,
+            [pltpu.VMEM((peers * share, total_vectors), BF16)],
+            spread, filtered, *earlier,
+        )
     return (filtered, own_rows)
 
 

time: 98.2 us -> 96.6 us (0.984)
  waiting for transfers between devices: 3.41 us -> 2.22 us
    ppermute x1, waiting for transfers between devices: 0.99 us -> 0.01 us  [per_device(): theirs = lax.ppermute(mine, 'cells', pair)]
    pallas_call x13 -> x14, Pallas kernels: 23.7 us -> 23.9 us  [call(): pl.pallas_call(kernel, out_shape=out_shape, in_specs=[{'v': VMEM_SPEC, 's...]
  transfers between devices with their start and end apart: 9 -> 9, of which waited for: 7 -> 4; matrix products, arithmetic and copies ran while one was open for 0% -> 0% of each run, Pallas kernels for 12% -> 13%
where the time goes in v5:
time: 96.6 us; the launch traced here: 96.3 us
  blocking collectives  47 us (49%)
  Pallas kernels  23.9 us (25%)
  starting transfers between devices  20.4 us (21%)
  between operations  2.72 us (3%)
  waiting for transfers between devices  2.22 us (2%)
    all_to_all x1, blocking collectives, per_device(): lax.all_to_all(shares, AXES, split_axis=0, concat_axis=0, tiled=True, axi...  30.3 us
    pallas_call x14, Pallas kernels, call(): pl.pallas_call(kernel, out_shape=out_shape, in_specs=[{'v': VMEM_SPEC, 's...  23.9 us
    all_to_all x1, blocking collectives, per_device(): lax.all_to_all(mine, AXES, split_axis=0, concat_axis=0, tiled=True, axis_...  16.8 us
    ppermute x4, starting transfers between devices, passed_along(): lax.ppermute(value, axis, [(source, source + steps) for source in range(l...  12.4 us
    ppermute x3, starting transfers between devices, per_device(): lax.ppermute(piece, 'vecs', turn(away))  5.07 us
    ppermute x1, starting transfers between devices, per_device(): theirs = lax.ppermute(mine, 'cells', pair)  2.84 us
    ppermute x3, waiting for transfers between devices, per_device(): lax.ppermute(piece, 'vecs', turn(away))  2.13 us
  transfers between devices with their start and end apart: 9, of which 4 were waited for; matrix products, arithmetic and copies ran while one was open for 0% of the time, Pallas kernels for 13%

profile of v5, /device:TPU:1, one launch (start us, length us, event | category | flops | bytes accessed | tf_op | source)
XLA Modules:
  0.0 96.3 jit_solution(10030048821070966468)
XLA Ops:
  0.6 3.2 %gather_face.1 = (bf16[624,512]{1,0:T(8,128)(2,1)S(1)}, s32[125,128]{1,0:T(8,128)S(1)}, s32[18,128]{1,0:T(8,128)S(1)}, f32[25,16,128]{2,1,0:T(8,128)S(1)}, f32[2...) custom-call(s32[125,128]{1,0:T(8,128)} %refs_0_.1, f32[16,9216]{1,0:T(8,128)} %refs_9_.1, f32[72,128]{1,0:T(8,128)} %bitcast.9), custom_call_target="tpu_custom_call" | custom-call | tf_op jit(solution)/shard_map/gather_face/pallas_call | solution.py:662
  3.9 4.9 %collective-permute-start = (f32[13,24,128]{2,1,0:T(8,128)S(1)}, f32[13,24,128]{2,1,0:T(8,128)S(1)}, u32[]{:S(2)}, u32[]{:S(2)}) collective-permute-start(f32[13,24,128]{2,1,0:T(8,128)S(1)} %get-tuple-element.49), channel_id=1, source_target_pairs={{0,4},{4,8},{8,12},{12,16},{16,20},{20,24},{24,28},{28,32},{32,36}... | collective-permute-start | bytes 479240 | tf_op jit(solution)/shard_map/ppermute | solution.py:679
  9.4 4.9 %gather_rest.1 = (s32[52,128]{1,0:T(8,128)S(1)}, f32[75,16,128]{2,1,0:T(8,128)S(1)}, f32[75,128]{1,0:T(8,128)S(1)}, f32[8,128]{1,0:T(8,128)S(1)}, f32[125,128]{1,0:T(8,128)S(1)}) custom-call(bf16[624,512]{1,0:T(8,128)(2,1)S(1)} %get-tuple-element.43.refs_0_, s32[125,128]{1,0:T(8,128)S(1)} %get-tuple-element.44.refs_1_, f32[125,128]{1,0:T(8,128)} %refs_2_.1, ...), custom_call_target="tpu_custom_call" | custom-call | tf_op jit(solution)/shard_map/gather_rest/pallas_call | solution.py:662
  14.4 0.0 collective-permute-done.refs_4_
  14.4 1.3 %first_faces.1 = (f32[125,16,128]{2,1,0:T(8,128)S(1)}, f32[25,16,128]{2,1,0:T(8,128)S(1)}, f32[25,128]{1,0:T(8,128)S(1)}, f32[25,16,128]{2,1,0:T(8,128)S(1)}, f3...) custom-call(f32[75,16,128]{2,1,0:T(8,128)S(1)} %get-tuple-element.45.refs_0_.refs_4_, ...), custom_call_target="tpu_custom_call" | custom-call | tf_op jit(solution)/shard_map/first_faces/pallas_call | solution.py:662
  15.7 1.9 %collective-permute-start.1 = (bf16[13,16,128]{2,1,0:T(8,128)(2,1)S(1)}, bf16[13,16,128]{2,1,0:T(8,128)(2,1)S(1)}, u32[]{:S(2)}, u32[]{:S(2)}) collective-permute-start(bf16[13,16,128]{2,1,0:T(8,128)(2,1)S(1)} %get-tuple-element.57), channel_id=1, source_target_pairs={{4,0},{8,4},{12,8},{16,12},{20,16},{24,20},{28,24},{32,28},{36,32}... | collective-permute-start | bytes 159752 | tf_op jit(solution)/shard_map/ppermute | solution.py:679
  17.6 3.6 %collective-permute-start.2 = (bf16[13,16,128]{2,1,0:T(8,128)(2,1)S(1)}, bf16[13,16,128]{2,1,0:T(8,128)(2,1)S(1)}, u32[]{:S(2)}, u32[]{:S(2)}) collective-permute-start(bf16[13,16,128]{2,1,0:T(8,128)(2,1)S(1)} %get-tuple-element.58), channel_id=1, source_target_pairs={{0,4},{4,8},{8,12},{12,16},{16,20},{20,24},{24,28},{28,32},{32,36}... | collective-permute-start | bytes 159752 | tf_op jit(solution)/shard_map/ppermute | solution.py:679
  22.5 1.1 %first_rest.1.refs_1_ = f32[75,16,128]{2,1,0:T(8,128)S(1)} custom-call(f32[125,16,128]{2,1,0:T(8,128)S(1)} %get-tuple-element.53.refs_0_, f32[8,128]{1,0:T(8,128)S(1)} %get-tuple-element.50.refs_5_.refs_1_.refs_11_, f32[125,128]{1,0:T(8,128)S(1)} %get-tuple-element.51.refs_6_.refs_2_.refs_12_), custom_call_target="tpu_custom_call" | custom-call | tf_op jit(solution)/shard_map/first_rest/pallas_call | solution.py:662
  23.7 0.0 collective-permute-done.1.refs_9_
  23.7 0.0 collective-permute-done.2.refs_10_
  23.7 1.3 %second_faces.1 = (f32[125,16,128]{2,1,0:T(8,128)S(1)}, f32[75,16,128]{2,1,0:T(8,128)S(1)}, f32[25,16,128]{2,1,0:T(8,128)S(1)}, f32[25,16,128]{2,1,0:T(8,128)S(1)}, bf16[13,16,128]{2,1,0:T(8,128)(2,1)S(1)}) custom-call(f32[25,16,128]{2,1,0:T(8,128)S(1)} %get-tuple-element.52.refs_0_, f32[75,16,128]{2,1,0:T(8,128)S(1)} %first_rest.1.refs_1_, ...), custom_call_target="tpu_custom_call" | custom-call | tf_op jit(solution)/shard_map/second_faces/pallas_call | solution.py:662
  25.0 1.9 %collective-permute-start.3 = (bf16[13,16,128]{2,1,0:T(8,128)(2,1)S(1)}, bf16[13,16,128]{2,1,0:T(8,128)(2,1)S(1)}, u32[]{:S(2)}, u32[]{:S(2)}) collective-permute-start(bf16[13,16,128]{2,1,0:T(8,128)(2,1)S(1)} %get-tuple-element.66), channel_id=1, source_target_pairs={{4,0},{8,4},{12,8},{16,12},{20,16},{24,20},{28,24},{32,28},{36,32}... | collective-permute-start | bytes 159752 | tf_op jit(solution)/shard_map/ppermute | solution.py:679
  26.9 4.0 %second_rest.1 = (f32[624,256]{1,0:T(8,128)S(1)}, f32[25,16,128]{2,1,0:T(8,128)S(1)}, bf16[16,9216]{1,0:T(8,128)(2,1)S(1)}, bf16[256,2304]{1,0:T(8,128)(2,1)S(1)...) custom-call(f32[125,16,128]{2,1,0:T(8,128)S(1)} %get-tuple-element.5, ...), custom_call_target="tpu_custom_call" | custom-call | tf_op jit(solution)/shard_map/second_rest/pallas_call | solution.py:662
  30.9 0.0 collective-permute-done.3.refs_4_
  30.9 1.2 %scatter_top.1 = (bf16[16,2304]{1,0:T(8,128)(2,1)S(1)}, bf16[16,2304]{1,0:T(8,128)(2,1)S(1)}, bf16[16,2304]{1,0:T(8,128)(2,1)S(1)}, bf16[16,2304]{1,0:T(8,128)(2,1)S(1)}) custom-call(s32[18,128]{1,0:T(8,128)S(1)} %get-tuple-element.42.refs_0_, f32[624,256]{1,0:T(8,128)S(1)} %get-tuple-element.64.refs_1_, f32[25,16,128]{2,1,0:T(8,128)S(1)} %get-tuple-element.65.refs_2_, ...), custom_call_target="tpu_custom_call" | custom-call | tf_op jit(solution)/shard_map/scatter_top/pallas_call | solution.py:662
  32.1 1.4 %collective-permute-start.4 = (bf16[16,2304]{1,0:T(8,128)(2,1)S(1)}, bf16[16,2304]{1,0:T(8,128)(2,1)S(1)}, u32[]{:S(2)}, u32[]{:S(2)}) collective-permute-start(bf16[16,2304]{1,0:T(8,128)(2,1)S(1)} %get-tuple-element.69), channel_id=1, source_target_pairs={{0,1},{1,2},{2,3},{3,0},{4,5},{5,6},{6,7},{7,4},{8,9},{9,10},{10,1... | collective-permute-start | bytes 221192 | tf_op jit(solution)/shard_map/ppermute | solution.py:776
  33.5 2.6 %collective-permute-start.5 = (bf16[16,2304]{1,0:T(8,128)(2,1)S(1)}, bf16[16,2304]{1,0:T(8,128)(2,1)S(1)}, u32[]{:S(2)}, u32[]{:S(2)}) collective-permute-start(bf16[16,2304]{1,0:T(8,128)(2,1)S(1)} %get-tuple-element.70), channel_id=1, source_target_pairs={{0,2},{1,3},{2,0},{3,1},{4,6},{5,7},{6,4},{7,5},{8,10},{9,11},{10,... | collective-permute-start | bytes 221192 | tf_op jit(solution)/shard_map/ppermute | solution.py:776
  36.1 1.1 %collective-permute-start.6 = (bf16[16,2304]{1,0:T(8,128)(2,1)S(1)}, bf16[16,2304]{1,0:T(8,128)(2,1)S(1)}, u32[]{:S(2)}, u32[]{:S(2)}) collective-permute-start(bf16[16,2304]{1,0:T(8,128)(2,1)S(1)} %get-tuple-element.71), channel_id=1, source_target_pairs={{0,3},{1,0},{2,1},{3,2},{4,7},{5,4},{6,5},{7,6},{8,11},{9,8},{10,9... | collective-permute-start | bytes 221192 | tf_op jit(solution)/shard_map/ppermute | solution.py:776
  37.2 0.5 collective-permute-done.4.refs_1_
  37.6 1.2 %collective-permute-done.5.refs_2_ = bf16[16,2304]{1,0:T(8,128)(2,1)S(1)} collective-permute-done((bf16[16,2304]{1,0:T(8,128)(2,1)S(1)}, bf16[16,2304]{1,0:T(8,128)(2,1)S(1)}, u32[]{:S(2)}, u32[]{:S(2)}) %collective-permute-start.5) | collective-permute-done | bytes 73760 | tf_op jit(solution)/shard_map/ppermute | solution.py:776
  38.8 0.5 collective-permute-done.6.refs_3_
  39.3 1.4 %project_other.1 = f32[128,4,128]{2,1,0:T(4,128)S(1)} custom-call(bf16[64,2304]{1,0:T(8,128)(2,1)S(1)} %gather_pieces.1.refs_0_.refs_1_, bf16[256,2304]{1,0:T(8,128)(2,1)S(1)} %get-tuple-element.72.refs_1_.refs_2_, bf16[256,2304]{1,0:T(8,128)(2,1)S(1)} %get-tuple-element.73.refs_2_.refs_3_, bf16[256,2304]{1,0:T(8,128)(2,1)S(1)} %get-tuple-element.74.refs_3_.refs_4_, ...), custom_call_target="tpu_custom_call" | custom-call | tf_op jit(solution)/shard_map/project_other/pallas_call | solution.py:662
  40.8 0.1 collective-permute-start.7
  40.9 1.4 %project_own.1.keep = f32[128,4,128]{2,1,0:T(4,128)S(1)} custom-call(bf16[64,2304]{1,0:T(8,128)(2,1)S(1)} %gather_pieces.1.refs_0_.refs_1_, bf16[256,2304]{1,0:T(8,128)(2,1)S(1)} %get-tuple-element.72.refs_1_.refs_2_, bf16[256,2304]{1,0:T(8,128)(2,1)S(1)} %get-tuple-element.73.refs_2_.refs_3_, bf16[256,2304]{1,0:T(8,128)(2,1)S(1)} %get-tuple-element.74.refs_3_.refs_4_, ...), custom_call_target="tpu_custom_call" | custom-call | tf_op jit(solution)/shard_map/project_own/pallas_call | solution.py:662
  42.3 0.1 collective-permute-done.7.received
  42.4 0.1 pair_sum.1
  42.5 30.3 %all_to_all.10.shares = bf16[128,4,128]{2,1,0:T(4,128)(2,1)S(1)} all-to-all(bf16[128,4,128]{2,1,0:T(4,128)(2,1)S(1)} %pair_sum.1), channel_id=1, replica_groups={{0,1,2,3,8,9,10,11,16,17,18,19,24,25,26,27,32,33,34,35,40,41,42,43,48,4..., dimensions={0} | all-to-all | bytes 262144 | tf_op jit(solution)/shard_map/all_to_all | solution.py:806
  72.7 0.8 own_rows.1
  73.5 16.8 %all_to_all.11.refs_0_ = bf16[128,4,128]{2,1,0:T(4,128)(2,1)S(1)} all-to-all(bf16[128,4,128]{2,1,0:T(4,128)(2,1)S(1)} %get-tuple-element.80), channel_id=1, replica_groups={{0,1,2,3,8,9,10,11,16,17,18,19,24,25,26,27,32,33,34,35,40,41,42,43,48,4..., dimensions={0} | all-to-all | bytes 262144 | tf_op jit(solution)/shard_map/all_to_all | solution.py:815
  90.3 2.8 %collective-permute-start.8 = (bf16[128,4,128]{2,1,0:T(4,128)(2,1)S(1)}, bf16[128,4,128]{2,1,0:T(4,128)(2,1)S(1)}, u32[]{:S(2)}, u32[]{:S(2)}) collective-permute-start(bf16[128,4,128]{2,1,0:T(4,128)(2,1)S(1)} %all_to_all.11.refs_0_), channel_id=1, source_target_pairs={{0,4},{4,0},{8,12},{12,8},{16,20},{20,16},{24,28},{28,24},{32,36},... | collective-permute-start | bytes 393224 | tf_op jit(solution)/shard_map/ppermute | solution.py:818
  93.2 1.1 %filter_own.1.refs_1_ = f32[64,2304]{1,0:T(8,128)S(1)} custom-call(bf16[128,4,128]{2,1,0:T(4,128)(2,1)S(1)} %all_to_all.11.refs_0_, bf16[64,2304]{1,0:T(8,128)(2,1)S(1)} %gather_pieces.1.refs_0_.refs_1_, bf16[256,2304]{1,0:T(8,128)(2,1)S(1)} %get-tuple-element.72.refs_1_.refs_2_, bf16[256,2304]{1,0:T(8,128)(2,1)S(1)} %get-tuple-element.73.refs_2_.refs_3_, ...), custom_call_target="tpu_custom_call" | custom-call | tf_op jit(solution)/shard_map/filter_own/pallas_call | solution.py:662
  94.3 0.0 collective-permute-done.8.refs_0_
  94.3 1.9 %filter_other.1 = f32[64,2304]{1,0:T(8,128)} custom-call(bf16[128,4,128]{2,1,0:T(4,128)(2,1)S(1)} %collective-permute-done.8.refs_0_, f32[64,2304]{1,0:T(8,128)S(1)} %filter_own.1.refs_1_, bf16[256,2304]{1,0:T(8,128)(2,1)S(1)} %get-tuple-element.72.refs_1_.refs_2_, bf16[256,2304]{1,0:T(8,128)(2,1)S(1)} %get-tuple-element.73.refs_2_.refs_3_, ...), custom_call_target="tpu_custom_call" | custom-call | tf_op jit(solution)/shard_map/filter_other/pallas_call | solution.py:662
  (1 shorter events, 0.0 us)
Async XLA Ops:
  3.9 10.5 %collective-permute-start = (f32[13,24,128]{2,1,0:T(8,128)S(1)}, f32[13,24,128]{2,1,0:T(8,128)S(1)}, u32[]{:S(2)}, u32[]{:S(2)}) collective-permute-start(f32[13,24,128]{2,1,0:T(8,128)S(1)} %get-tuple-element.49), channel_id=1, source_target_pairs={{0,4},{4,8},{8,12},{12,16},{16,20},{20,24},{24,28},{28,32},{32,36}... | collective-permute-start | bytes 479240 | tf_op jit(solution)/shard_map/ppermute | solution.py:679
  15.7 8.0 %collective-permute-start.1 = (bf16[13,16,128]{2,1,0:T(8,128)(2,1)S(1)}, bf16[13,16,128]{2,1,0:T(8,128)(2,1)S(1)}, u32[]{:S(2)}, u32[]{:S(2)}) collective-permute-start(bf16[13,16,128]{2,1,0:T(8,128)(2,1)S(1)} %get-tuple-element.57), channel_id=1, source_target_pairs={{4,0},{8,4},{12,8},{16,12},{20,16},{24,20},{28,24},{32,28},{36,32}... | collective-permute-start | bytes 159752 | tf_op jit(solution)/shard_map/ppermute | solution.py:679
  17.6 6.1 %collective-permute-start.2 = (bf16[13,16,128]{2,1,0:T(8,128)(2,1)S(1)}, bf16[13,16,128]{2,1,0:T(8,128)(2,1)S(1)}, u32[]{:S(2)}, u32[]{:S(2)}) collective-permute-start(bf16[13,16,128]{2,1,0:T(8,128)(2,1)S(1)} %get-tuple-element.58), channel_id=1, source_target_pairs={{0,4},{4,8},{8,12},{12,16},{16,20},{20,24},{24,28},{28,32},{32,36}... | collective-permute-start | bytes 159752 | tf_op jit(solution)/shard_map/ppermute | solution.py:679
  25.0 5.9 %collective-permute-start.3 = (bf16[13,16,128]{2,1,0:T(8,128)(2,1)S(1)}, bf16[13,16,128]{2,1,0:T(8,128)(2,1)S(1)}, u32[]{:S(2)}, u32[]{:S(2)}) collective-permute-start(bf16[13,16,128]{2,1,0:T(8,128)(2,1)S(1)} %get-tuple-element.66), channel_id=1, source_target_pairs={{4,0},{8,4},{12,8},{16,12},{20,16},{24,20},{28,24},{32,28},{36,32}... | collective-permute-start | bytes 159752 | tf_op jit(solution)/shard_map/ppermute | solution.py:679
  32.1 5.6 %collective-permute-start.4 = (bf16[16,2304]{1,0:T(8,128)(2,1)S(1)}, bf16[16,2304]{1,0:T(8,128)(2,1)S(1)}, u32[]{:S(2)}, u32[]{:S(2)}) collective-permute-start(bf16[16,2304]{1,0:T(8,128)(2,1)S(1)} %get-tuple-element.69), channel_id=1, source_target_pairs={{0,1},{1,2},{2,3},{3,0},{4,5},{5,6},{6,7},{7,4},{8,9},{9,10},{10,1... | collective-permute-start | bytes 221192 | tf_op jit(solution)/shard_map/ppermute | solution.py:776
  33.5 5.3 %collective-permute-start.5 = (bf16[16,2304]{1,0:T(8,128)(2,1)S(1)}, bf16[16,2304]{1,0:T(8,128)(2,1)S(1)}, u32[]{:S(2)}, u32[]{:S(2)}) collective-permute-start(bf16[16,2304]{1,0:T(8,128)(2,1)S(1)} %get-tuple-element.70), channel_id=1, source_target_pairs={{0,2},{1,3},{2,0},{3,1},{4,6},{5,7},{6,4},{7,5},{8,10},{9,11},{10,... | collective-permute-start | bytes 221192 | tf_op jit(solution)/shard_map/ppermute | solution.py:776
  36.1 3.2 %collective-permute-start.6 = (bf16[16,2304]{1,0:T(8,128)(2,1)S(1)}, bf16[16,2304]{1,0:T(8,128)(2,1)S(1)}, u32[]{:S(2)}, u32[]{:S(2)}) collective-permute-start(bf16[16,2304]{1,0:T(8,128)(2,1)S(1)} %get-tuple-element.71), channel_id=1, source_target_pairs={{0,3},{1,0},{2,1},{3,2},{4,7},{5,4},{6,5},{7,6},{8,11},{9,8},{10,9... | collective-permute-start | bytes 221192 | tf_op jit(solution)/shard_map/ppermute | solution.py:776
  40.8 1.6 %collective-permute-start.7 = (f32[128,4,128]{2,1,0:T(4,128)S(1)}, f32[128,4,128]{2,1,0:T(4,128)S(1)}, u32[]{:S(2)}, u32[]{:S(2)}) collective-permute-start(f32[128,4,128]{2,1,0:T(4,128)S(1)} %project_other.1), channel_id=1, source_target_pairs={{0,4},{4,0},{8,12},{12,8},{16,20},{20,16},{24,28},{28,24},{32,36},... | collective-permute-start | bytes 786440 | tf_op jit(solution)/shard_map/ppermute | solution.py:804
  90.3 4.0 %collective-permute-start.8 = (bf16[128,4,128]{2,1,0:T(4,128)(2,1)S(1)}, bf16[128,4,128]{2,1,0:T(4,128)(2,1)S(1)}, u32[]{:S(2)}, u32[]{:S(2)}) collective-permute-start(bf16[128,4,128]{2,1,0:T(4,128)(2,1)S(1)} %all_to_all.11.refs_0_), channel_id=1, source_target_pairs={{0,4},{4,0},{8,12},{12,8},{16,20},{20,16},{24,28},{28,24},{32,36},... | collective-permute-start | bytes 393224 | tf_op jit(solution)/shard_map/ppermute | solution.py:818

commit v6 on v5

--- a/solution.py
+++ b/solution.py
@@ -622,7 +622,7 @@
     own = jnp.sum(shares[...].astype(F32), 0)
     columns = own.shape[1] // 2
     own_rows[...] = jnp.concatenate([own[:, :columns], own[:, columns:]], 0)
-    spread[...] = jnp.broadcast_to(own[None], spread.shape).astype(BF16)
+    spread[...] = jnp.broadcast_to(own.astype(BF16)[None], spread.shape)
 
 
 def filter_kernel(cores, parts, share, other, spread, before, *rest):
@@ -772,10 +772,9 @@
         [pltpu.VMEM((parts, vectors, owned // parts), BF16), pltpu.VMEM((table_rows, 256), F32)],
         slots_top, before, done_top, mass_top, above, alone, halfwidth,
     )
-    pieces = [
-        lax.ppermute(piece, "vecs", turn(away)) if away else piece
-        for away, piece in enumerate(pieces)
-    ]
+    pieces = list(pieces)
+    for away in sorted(range(1, parts), key=lambda k: -min(k, parts - k)):
+        pieces[away] = lax.ppermute(pieces[away], "vecs", turn(away))
     total_vectors = parts * vectors
     share = earlier_vectors.shape[0] // devices
     half, peers = share // 2, devices // cores

time: 96.6 us -> 96.6 us (level)
  no operation moved by 1% of the time
where the time goes in v6:
time: 96.6 us; the launch traced here: 96.3 us
  blocking collectives  47 us (49%)
  Pallas kernels  23.9 us (25%)
  starting transfers between devices  20.4 us (21%)
  between operations  2.72 us (3%)
  waiting for transfers between devices  2.22 us (2%)
    all_to_all x1, blocking collectives, per_device(): lax.all_to_all(shares, AXES, split_axis=0, concat_axis=0, tiled=True, axi...  30.3 us
    pallas_call x14, Pallas kernels, call(): pl.pallas_call(kernel, out_shape=out_shape, in_specs=[{'v': VMEM_SPEC, 's...  23.9 us
    all_to_all x1, blocking collectives, per_device(): lax.all_to_all(mine, AXES, split_axis=0, concat_axis=0, tiled=True, axis_...  16.8 us
    ppermute x4, starting transfers between devices, passed_along(): lax.ppermute(value, axis, [(source, source + steps) for source in range(l...  12.4 us
    ppermute x3, starting transfers between devices, per_device(): pieces[away] = lax.ppermute(pieces[away], 'vecs', turn(away))  5.07 us
    ppermute x1, starting transfers between devices, per_device(): theirs = lax.ppermute(mine, 'cells', pair)  2.84 us
    ppermute x3, waiting for transfers between devices, per_device(): pieces[away] = lax.ppermute(pieces[away], 'vecs', turn(away))  2.13 us
  transfers between devices with their start and end apart: 9, of which 4 were waited for; matrix products, arithmetic and copies ran while one was open for 0% of the time, Pallas kernels for 13%

profile of v6, /device:TPU:1, one launch (start us, length us, event | category | flops | bytes accessed | tf_op | source)
XLA Modules:
  0.0 96.3 jit_solution(10030048821070966468)
XLA Ops:
  0.6 3.2 %gather_face.1 = (bf16[624,512]{1,0:T(8,128)(2,1)S(1)}, s32[125,128]{1,0:T(8,128)S(1)}, s32[18,128]{1,0:T(8,128)S(1)}, f32[25,16,128]{2,1,0:T(8,128)S(1)}, f32[2...) custom-call(s32[125,128]{1,0:T(8,128)} %refs_0_.1, f32[16,9216]{1,0:T(8,128)} %refs_9_.1, f32[72,128]{1,0:T(8,128)} %bitcast.9), custom_call_target="tpu_custom_call" | custom-call | tf_op jit(solution)/shard_map/gather_face/pallas_call | solution.py:662
  3.9 4.9 %collective-permute-start = (f32[13,24,128]{2,1,0:T(8,128)S(1)}, f32[13,24,128]{2,1,0:T(8,128)S(1)}, u32[]{:S(2)}, u32[]{:S(2)}) collective-permute-start(f32[13,24,128]{2,1,0:T(8,128)S(1)} %get-tuple-element.49), channel_id=1, source_target_pairs={{0,4},{4,8},{8,12},{12,16},{16,20},{20,24},{24,28},{28,32},{32,36}... | collective-permute-start | bytes 479240 | tf_op jit(solution)/shard_map/ppermute | solution.py:679
  9.4 4.9 %gather_rest.1 = (s32[52,128]{1,0:T(8,128)S(1)}, f32[75,16,128]{2,1,0:T(8,128)S(1)}, f32[75,128]{1,0:T(8,128)S(1)}, f32[8,128]{1,0:T(8,128)S(1)}, f32[125,128]{1,0:T(8,128)S(1)}) custom-call(bf16[624,512]{1,0:T(8,128)(2,1)S(1)} %get-tuple-element.43.refs_0_, s32[125,128]{1,0:T(8,128)S(1)} %get-tuple-element.44.refs_1_, f32[125,128]{1,0:T(8,128)} %refs_2_.1, ...), custom_call_target="tpu_custom_call" | custom-call | tf_op jit(solution)/shard_map/gather_rest/pallas_call | solution.py:662
  14.4 0.0 collective-permute-done.refs_4_
  14.4 1.3 %first_faces.1 = (f32[125,16,128]{2,1,0:T(8,128)S(1)}, f32[25,16,128]{2,1,0:T(8,128)S(1)}, f32[25,128]{1,0:T(8,128)S(1)}, f32[25,16,128]{2,1,0:T(8,128)S(1)}, f3...) custom-call(f32[75,16,128]{2,1,0:T(8,128)S(1)} %get-tuple-element.45.refs_0_.refs_4_, ...), custom_call_target="tpu_custom_call" | custom-call | tf_op jit(solution)/shard_map/first_faces/pallas_call | solution.py:662
  15.7 1.9 %collective-permute-start.1 = (bf16[13,16,128]{2,1,0:T(8,128)(2,1)S(1)}, bf16[13,16,128]{2,1,0:T(8,128)(2,1)S(1)}, u32[]{:S(2)}, u32[]{:S(2)}) collective-permute-start(bf16[13,16,128]{2,1,0:T(8,128)(2,1)S(1)} %get-tuple-element.57), channel_id=1, source_target_pairs={{4,0},{8,4},{12,8},{16,12},{20,16},{24,20},{28,24},{32,28},{36,32}... | collective-permute-start | bytes 159752 | tf_op jit(solution)/shard_map/ppermute | solution.py:679
  17.6 3.6 %collective-permute-start.2 = (bf16[13,16,128]{2,1,0:T(8,128)(2,1)S(1)}, bf16[13,16,128]{2,1,0:T(8,128)(2,1)S(1)}, u32[]{:S(2)}, u32[]{:S(2)}) collective-permute-start(bf16[13,16,128]{2,1,0:T(8,128)(2,1)S(1)} %get-tuple-element.58), channel_id=1, source_target_pairs={{0,4},{4,8},{8,12},{12,16},{16,20},{20,24},{24,28},{28,32},{32,36}... | collective-permute-start | bytes 159752 | tf_op jit(solution)/shard_map/ppermute | solution.py:679
  22.5 1.1 %first_rest.1.refs_1_ = f32[75,16,128]{2,1,0:T(8,128)S(1)} custom-call(f32[125,16,128]{2,1,0:T(8,128)S(1)} %get-tuple-element.53.refs_0_, f32[8,128]{1,0:T(8,128)S(1)} %get-tuple-element.50.refs_5_.refs_1_.refs_11_, f32[125,128]{1,0:T(8,128)S(1)} %get-tuple-element.51.refs_6_.refs_2_.refs_12_), custom_call_target="tpu_custom_call" | custom-call | tf_op jit(solution)/shard_map/first_rest/pallas_call | solution.py:662
  23.7 0.0 collective-permute-done.1.refs_9_
  23.7 0.0 collective-permute-done.2.refs_10_
  23.7 1.3 %second_faces.1 = (f32[125,16,128]{2,1,0:T(8,128)S(1)}, f32[75,16,128]{2,1,0:T(8,128)S(1)}, f32[25,16,128]{2,1,0:T(8,128)S(1)}, f32[25,16,128]{2,1,0:T(8,128)S(1)}, bf16[13,16,128]{2,1,0:T(8,128)(2,1)S(1)}) custom-call(f32[25,16,128]{2,1,0:T(8,128)S(1)} %get-tuple-element.52.refs_0_, f32[75,16,128]{2,1,0:T(8,128)S(1)} %first_rest.1.refs_1_, ...), custom_call_target="tpu_custom_call" | custom-call | tf_op jit(solution)/shard_map/second_faces/pallas_call | solution.py:662
  25.0 1.9 %collective-permute-start.3 = (bf16[13,16,128]{2,1,0:T(8,128)(2,1)S(1)}, bf16[13,16,128]{2,1,0:T(8,128)(2,1)S(1)}, u32[]{:S(2)}, u32[]{:S(2)}) collective-permute-start(bf16[13,16,128]{2,1,0:T(8,128)(2,1)S(1)} %get-tuple-element.66), channel_id=1, source_target_pairs={{4,0},{8,4},{12,8},{16,12},{20,16},{24,20},{28,24},{32,28},{36,32}... | collective-permute-start | bytes 159752 | tf_op jit(solution)/shard_map/ppermute | solution.py:679
  26.9 4.0 %second_rest.1 = (f32[624,256]{1,0:T(8,128)S(1)}, f32[25,16,128]{2,1,0:T(8,128)S(1)}, bf16[16,9216]{1,0:T(8,128)(2,1)S(1)}, bf16[256,2304]{1,0:T(8,128)(2,1)S(1)...) custom-call(f32[125,16,128]{2,1,0:T(8,128)S(1)} %get-tuple-element.5, ...), custom_call_target="tpu_custom_call" | custom-call | tf_op jit(solution)/shard_map/second_rest/pallas_call | solution.py:662
  30.9 0.0 collective-permute-done.3.refs_4_
  30.9 1.2 %scatter_top.1 = (bf16[16,2304]{1,0:T(8,128)(2,1)S(1)}, bf16[16,2304]{1,0:T(8,128)(2,1)S(1)}, bf16[16,2304]{1,0:T(8,128)(2,1)S(1)}, bf16[16,2304]{1,0:T(8,128)(2,1)S(1)}) custom-call(s32[18,128]{1,0:T(8,128)S(1)} %get-tuple-element.42.refs_0_, f32[624,256]{1,0:T(8,128)S(1)} %get-tuple-element.64.refs_1_, f32[25,16,128]{2,1,0:T(8,128)S(1)} %get-tuple-element.65.refs_2_, ...), custom_call_target="tpu_custom_call" | custom-call | tf_op jit(solution)/shard_map/scatter_top/pallas_call | solution.py:662
  32.1 1.4 %collective-permute-start.4 = (bf16[16,2304]{1,0:T(8,128)(2,1)S(1)}, bf16[16,2304]{1,0:T(8,128)(2,1)S(1)}, u32[]{:S(2)}, u32[]{:S(2)}) collective-permute-start(bf16[16,2304]{1,0:T(8,128)(2,1)S(1)} %get-tuple-element.69), channel_id=1, source_target_pairs={{0,1},{1,2},{2,3},{3,0},{4,5},{5,6},{6,7},{7,4},{8,9},{9,10},{10,1... | collective-permute-start | bytes 221192 | tf_op jit(solution)/shard_map/ppermute | solution.py:777
  33.5 2.6 %collective-permute-start.5 = (bf16[16,2304]{1,0:T(8,128)(2,1)S(1)}, bf16[16,2304]{1,0:T(8,128)(2,1)S(1)}, u32[]{:S(2)}, u32[]{:S(2)}) collective-permute-start(bf16[16,2304]{1,0:T(8,128)(2,1)S(1)} %get-tuple-element.70), channel_id=1, source_target_pairs={{0,2},{1,3},{2,0},{3,1},{4,6},{5,7},{6,4},{7,5},{8,10},{9,11},{10,... | collective-permute-start | bytes 221192 | tf_op jit(solution)/shard_map/ppermute | solution.py:777
  36.1 1.1 %collective-permute-start.6 = (bf16[16,2304]{1,0:T(8,128)(2,1)S(1)}, bf16[16,2304]{1,0:T(8,128)(2,1)S(1)}, u32[]{:S(2)}, u32[]{:S(2)}) collective-permute-start(bf16[16,2304]{1,0:T(8,128)(2,1)S(1)} %get-tuple-element.71), channel_id=1, source_target_pairs={{0,3},{1,0},{2,1},{3,2},{4,7},{5,4},{6,5},{7,6},{8,11},{9,8},{10,9... | collective-permute-start | bytes 221192 | tf_op jit(solution)/shard_map/ppermute | solution.py:777
  37.2 0.5 collective-permute-done.4.refs_1_
  37.6 1.2 %collective-permute-done.5.refs_2_ = bf16[16,2304]{1,0:T(8,128)(2,1)S(1)} collective-permute-done((bf16[16,2304]{1,0:T(8,128)(2,1)S(1)}, bf16[16,2304]{1,0:T(8,128)(2,1)S(1)}, u32[]{:S(2)}, u32[]{:S(2)}) %collective-permute-start.5) | collective-permute-done | bytes 73760 | tf_op jit(solution)/shard_map/ppermute | solution.py:777
  38.8 0.5 collective-permute-done.6.refs_3_
  39.3 1.4 %project_other.1 = f32[128,4,128]{2,1,0:T(4,128)S(1)} custom-call(bf16[64,2304]{1,0:T(8,128)(2,1)S(1)} %gather_pieces.1.refs_0_.refs_1_, bf16[256,2304]{1,0:T(8,128)(2,1)S(1)} %get-tuple-element.72.refs_1_.refs_2_, bf16[256,2304]{1,0:T(8,128)(2,1)S(1)} %get-tuple-element.73.refs_2_.refs_3_, bf16[256,2304]{1,0:T(8,128)(2,1)S(1)} %get-tuple-element.74.refs_3_.refs_4_, ...), custom_call_target="tpu_custom_call" | custom-call | tf_op jit(solution)/shard_map/project_other/pallas_call | solution.py:662
  40.8 0.1 collective-permute-start.7
  40.9 1.4 %project_own.1.keep = f32[128,4,128]{2,1,0:T(4,128)S(1)} custom-call(bf16[64,2304]{1,0:T(8,128)(2,1)S(1)} %gather_pieces.1.refs_0_.refs_1_, bf16[256,2304]{1,0:T(8,128)(2,1)S(1)} %get-tuple-element.72.refs_1_.refs_2_, bf16[256,2304]{1,0:T(8,128)(2,1)S(1)} %get-tuple-element.73.refs_2_.refs_3_, bf16[256,2304]{1,0:T(8,128)(2,1)S(1)} %get-tuple-element.74.refs_3_.refs_4_, ...), custom_call_target="tpu_custom_call" | custom-call | tf_op jit(solution)/shard_map/project_own/pallas_call | solution.py:662
  42.3 0.1 collective-permute-done.7.received
  42.4 0.1 pair_sum.1
  42.5 30.3 %all_to_all.10.shares = bf16[128,4,128]{2,1,0:T(4,128)(2,1)S(1)} all-to-all(bf16[128,4,128]{2,1,0:T(4,128)(2,1)S(1)} %pair_sum.1), channel_id=1, replica_groups={{0,1,2,3,8,9,10,11,16,17,18,19,24,25,26,27,32,33,34,35,40,41,42,43,48,4..., dimensions={0} | all-to-all | bytes 262144 | tf_op jit(solution)/shard_map/all_to_all | solution.py:805
  72.7 0.8 own_rows.1
  73.5 16.8 %all_to_all.11.refs_0_ = bf16[128,4,128]{2,1,0:T(4,128)(2,1)S(1)} all-to-all(bf16[128,4,128]{2,1,0:T(4,128)(2,1)S(1)} %get-tuple-element.80), channel_id=1, replica_groups={{0,1,2,3,8,9,10,11,16,17,18,19,24,25,26,27,32,33,34,35,40,41,42,43,48,4..., dimensions={0} | all-to-all | bytes 262144 | tf_op jit(solution)/shard_map/all_to_all | solution.py:814
  90.3 2.8 %collective-permute-start.8 = (bf16[128,4,128]{2,1,0:T(4,128)(2,1)S(1)}, bf16[128,4,128]{2,1,0:T(4,128)(2,1)S(1)}, u32[]{:S(2)}, u32[]{:S(2)}) collective-permute-start(bf16[128,4,128]{2,1,0:T(4,128)(2,1)S(1)} %all_to_all.11.refs_0_), channel_id=1, source_target_pairs={{0,4},{4,0},{8,12},{12,8},{16,20},{20,16},{24,28},{28,24},{32,36},... | collective-permute-start | bytes 393224 | tf_op jit(solution)/shard_map/ppermute | solution.py:817
  93.2 1.1 %filter_own.1.refs_1_ = f32[64,2304]{1,0:T(8,128)S(1)} custom-call(bf16[128,4,128]{2,1,0:T(4,128)(2,1)S(1)} %all_to_all.11.refs_0_, bf16[64,2304]{1,0:T(8,128)(2,1)S(1)} %gather_pieces.1.refs_0_.refs_1_, bf16[256,2304]{1,0:T(8,128)(2,1)S(1)} %get-tuple-element.72.refs_1_.refs_2_, bf16[256,2304]{1,0:T(8,128)(2,1)S(1)} %get-tuple-element.73.refs_2_.refs_3_, ...), custom_call_target="tpu_custom_call" | custom-call | tf_op jit(solution)/shard_map/filter_own/pallas_call | solution.py:662
  94.3 0.0 collective-permute-done.8.refs_0_
  94.3 1.9 %filter_other.1 = f32[64,2304]{1,0:T(8,128)} custom-call(bf16[128,4,128]{2,1,0:T(4,128)(2,1)S(1)} %collective-permute-done.8.refs_0_, f32[64,2304]{1,0:T(8,128)S(1)} %filter_own.1.refs_1_, bf16[256,2304]{1,0:T(8,128)(2,1)S(1)} %get-tuple-element.72.refs_1_.refs_2_, bf16[256,2304]{1,0:T(8,128)(2,1)S(1)} %get-tuple-element.73.refs_2_.refs_3_, ...), custom_call_target="tpu_custom_call" | custom-call | tf_op jit(solution)/shard_map/filter_other/pallas_call | solution.py:662
  (1 shorter events, 0.0 us)
Async XLA Ops:
  3.9 10.5 %collective-permute-start = (f32[13,24,128]{2,1,0:T(8,128)S(1)}, f32[13,24,128]{2,1,0:T(8,128)S(1)}, u32[]{:S(2)}, u32[]{:S(2)}) collective-permute-start(f32[13,24,128]{2,1,0:T(8,128)S(1)} %get-tuple-element.49), channel_id=1, source_target_pairs={{0,4},{4,8},{8,12},{12,16},{16,20},{20,24},{24,28},{28,32},{32,36}... | collective-permute-start | bytes 479240 | tf_op jit(solution)/shard_map/ppermute | solution.py:679
  15.7 8.0 %collective-permute-start.1 = (bf16[13,16,128]{2,1,0:T(8,128)(2,1)S(1)}, bf16[13,16,128]{2,1,0:T(8,128)(2,1)S(1)}, u32[]{:S(2)}, u32[]{:S(2)}) collective-permute-start(bf16[13,16,128]{2,1,0:T(8,128)(2,1)S(1)} %get-tuple-element.57), channel_id=1, source_target_pairs={{4,0},{8,4},{12,8},{16,12},{20,16},{24,20},{28,24},{32,28},{36,32}... | collective-permute-start | bytes 159752 | tf_op jit(solution)/shard_map/ppermute | solution.py:679
  17.6 6.1 %collective-permute-start.2 = (bf16[13,16,128]{2,1,0:T(8,128)(2,1)S(1)}, bf16[13,16,128]{2,1,0:T(8,128)(2,1)S(1)}, u32[]{:S(2)}, u32[]{:S(2)}) collective-permute-start(bf16[13,16,128]{2,1,0:T(8,128)(2,1)S(1)} %get-tuple-element.58), channel_id=1, source_target_pairs={{0,4},{4,8},{8,12},{12,16},{16,20},{20,24},{24,28},{28,32},{32,36}... | collective-permute-start | bytes 159752 | tf_op jit(solution)/shard_map/ppermute | solution.py:679
  25.0 5.9 %collective-permute-start.3 = (bf16[13,16,128]{2,1,0:T(8,128)(2,1)S(1)}, bf16[13,16,128]{2,1,0:T(8,128)(2,1)S(1)}, u32[]{:S(2)}, u32[]{:S(2)}) collective-permute-start(bf16[13,16,128]{2,1,0:T(8,128)(2,1)S(1)} %get-tuple-element.66), channel_id=1, source_target_pairs={{4,0},{8,4},{12,8},{16,12},{20,16},{24,20},{28,24},{32,28},{36,32}... | collective-permute-start | bytes 159752 | tf_op jit(solution)/shard_map/ppermute | solution.py:679
  32.1 5.6 %collective-permute-start.4 = (bf16[16,2304]{1,0:T(8,128)(2,1)S(1)}, bf16[16,2304]{1,0:T(8,128)(2,1)S(1)}, u32[]{:S(2)}, u32[]{:S(2)}) collective-permute-start(bf16[16,2304]{1,0:T(8,128)(2,1)S(1)} %get-tuple-element.69), channel_id=1, source_target_pairs={{0,1},{1,2},{2,3},{3,0},{4,5},{5,6},{6,7},{7,4},{8,9},{9,10},{10,1... | collective-permute-start | bytes 221192 | tf_op jit(solution)/shard_map/ppermute | solution.py:777
  33.5 5.3 %collective-permute-start.5 = (bf16[16,2304]{1,0:T(8,128)(2,1)S(1)}, bf16[16,2304]{1,0:T(8,128)(2,1)S(1)}, u32[]{:S(2)}, u32[]{:S(2)}) collective-permute-start(bf16[16,2304]{1,0:T(8,128)(2,1)S(1)} %get-tuple-element.70), channel_id=1, source_target_pairs={{0,2},{1,3},{2,0},{3,1},{4,6},{5,7},{6,4},{7,5},{8,10},{9,11},{10,... | collective-permute-start | bytes 221192 | tf_op jit(solution)/shard_map/ppermute | solution.py:777
  36.1 3.2 %collective-permute-start.6 = (bf16[16,2304]{1,0:T(8,128)(2,1)S(1)}, bf16[16,2304]{1,0:T(8,128)(2,1)S(1)}, u32[]{:S(2)}, u32[]{:S(2)}) collective-permute-start(bf16[16,2304]{1,0:T(8,128)(2,1)S(1)} %get-tuple-element.71), channel_id=1, source_target_pairs={{0,3},{1,0},{2,1},{3,2},{4,7},{5,4},{6,5},{7,6},{8,11},{9,8},{10,9... | collective-permute-start | bytes 221192 | tf_op jit(solution)/shard_map/ppermute | solution.py:777
  40.8 1.6 %collective-permute-start.7 = (f32[128,4,128]{2,1,0:T(4,128)S(1)}, f32[128,4,128]{2,1,0:T(4,128)S(1)}, u32[]{:S(2)}, u32[]{:S(2)}) collective-permute-start(f32[128,4,128]{2,1,0:T(4,128)S(1)} %project_other.1), channel_id=1, source_target_pairs={{0,4},{4,0},{8,12},{12,8},{16,20},{20,16},{24,28},{28,24},{32,36},... | collective-permute-start | bytes 786440 | tf_op jit(solution)/shard_map/ppermute | solution.py:803
  90.3 4.0 %collective-permute-start.8 = (bf16[128,4,128]{2,1,0:T(4,128)(2,1)S(1)}, bf16[128,4,128]{2,1,0:T(4,128)(2,1)S(1)}, u32[]{:S(2)}, u32[]{:S(2)}) collective-permute-start(bf16[128,4,128]{2,1,0:T(4,128)(2,1)S(1)} %all_to_all.11.refs_0_), channel_id=1, source_target_pairs={{0,4},{4,0},{8,12},{12,8},{16,20},{20,16},{24,28},{28,24},{32,36},... | collective-permute-start | bytes 393224 | tf_op jit(solution)/shard_map/ppermute | solution.py:817
